TPU v7x, 32 devices: a whole 2x2x4 slice. The times are simulated.
32 devices in a mesh: groups: 2 (over y), tile: 4 (over z), pair: 2 (over x), sub: 2 (over core).
Axes of the slice: x: 2, y: 2, z: 4, core: 2. Of those that a mesh axis runs over, the one named last changes fastest.
Arguments:
- ref_chips: bfloat16 [4, 256, 4096], P(('groups', 'pair'), ('tile', 'sub')), parts along dimension 0, may hold values from -300 to 700
- search_windows: bfloat16 [4, 512, 16384], P(('groups', 'pair'), ('tile', 'sub')), parts along dimension 0, may hold values from -300 to 700
- dest_block: int32 [4, 512, 1], P(('groups', 'pair'), ('tile', 'sub')), parts along dimension 0, may hold values from 0 to 7; in each aligned block of 64 rows (0 to 63, 64 to 127, ..., all dimensions but the last counted through in order) at most 16 rows name the same one
- dest_slot: int32 [4, 512], P(('groups', 'pair'), ('tile', 'sub')), parts along dimension 0, may hold values from 0 to 31
Outputs:
- smoothed_scores: float32 [4, 256, 4096], P(('groups', 'pair'), ('tile', 'sub')), parts along dimension 0
There are 2 independent parts, one for each index of `groups`. A program takes and returns all parts, laid end to end along the dimension named above; each array names one. Nothing has to cross between parts.
Inputs may be any that keep to these rules, and one draw needn't show every extreme that they name: `dest_block`: in the rows of one device (aligned blocks of 64 windows), no block index is named by more than 16 windows.
All inputs are finite; a program needn't handle non-finite values.
Results may differ from a plain program's by a relative error of at most 0.0003.
Values may be sent and summed in bfloat16 or wider, within the bound.
No kernel may reach another device: no remote copies, remote signals or barrier semaphores. Data moves between devices by JAX's collectives and lax.ppermute only.
A program may use at most 64 MiB of HBM per device.

v0:
```python
import math

import jax
import jax.numpy as jnp
from jax import lax
from jax.sharding import PartitionSpec as P

CHIP = 64
WIN = 128
GC = 8


precise = lax.Precision.HIGHEST
epsilon = 1e-06


def padded(block, sides, width):
    for axis, dim in sides:
        count = lax.axis_size(axis)
        forward = [(i, i + 1) for i in range(count - 1)]
        backward = [(target, source) for source, target in forward]
        low = lax.ppermute(
            lax.slice_in_dim(block, block.shape[dim] - width, None, axis=dim), axis, forward
        )
        high = lax.ppermute(lax.slice_in_dim(block, 0, width, axis=dim), axis, backward)
        block = jnp.concatenate([low, block, high], axis=dim)
    return block


def tables(length, width):
    freqs = jnp.arange(length, dtype=jnp.int32)[:, None]
    places = jnp.arange(width, dtype=jnp.int32)[None, :]
    phase = freqs * places % length
    angle = phase.astype(jnp.float32) * (2.0 * math.pi / length)
    return (jnp.cos(angle), jnp.sin(angle))


def spectrum(image, cosine, sine_table):
    first_real = jnp.einsum("kn,bnm->bkm", cosine, image, precision=precise)
    first_imag = -jnp.einsum("kn,bnm->bkm", sine_table, image, precision=precise)
    spec_real = jnp.einsum("bkm,lm->bkl", first_real, cosine, precision=precise) + jnp.einsum(
        "bkm,lm->bkl", first_imag, sine_table, precision=precise
    )
    spec_imag = jnp.einsum("bkm,lm->bkl", first_imag, cosine, precision=precise) - jnp.einsum(
        "bkm,lm->bkl", first_real, sine_table, precision=precise
    )
    return (spec_real, spec_imag)


def centre(chips_raw, chip_side):
    chip_float = chips_raw.astype(jnp.float32).reshape(-1, chip_side, chip_side)
    centred = chip_float - jnp.mean(chip_float, axis=(1, 2), keepdims=True)
    chip_std = jnp.sqrt(jnp.mean(centred * centred, axis=(1, 2)) + epsilon)
    return (centred, chip_std)


def match(chip_real, chip_imag, chip_std, windows_raw, chip_side, window_side):
    offsets = window_side - chip_side
    cos_full, sin_full = tables(window_side, window_side)
    cos_part = cos_full[:offsets]
    sin_part = sin_full[:offsets]
    window_float = windows_raw.astype(jnp.float32).reshape(-1, window_side, window_side)
    win_real, win_imag = spectrum(window_float, cos_full, sin_full)
    product_real = chip_real * win_real + chip_imag * win_imag
    product_imag = chip_real * win_imag - chip_imag * win_real
    half_real = jnp.einsum("ak,bkl->bal", cos_part, product_real, precision=precise) - jnp.einsum(
        "ak,bkl->bal", sin_part, product_imag, precision=precise
    )
    half_imag = jnp.einsum("ak,bkl->bal", cos_part, product_imag, precision=precise) + jnp.einsum(
        "ak,bkl->bal", sin_part, product_real, precision=precise
    )
    numerator = (
        jnp.einsum("bal,el->bae", half_real, cos_part, precision=precise)
        - jnp.einsum("bal,el->bae", half_imag, sin_part, precision=precise)
    ) / (window_side * window_side)
    starts = jnp.arange(offsets, dtype=jnp.int32)[:, None]
    pixels = jnp.arange(window_side, dtype=jnp.int32)[None, :]
    window_band = ((pixels >= starts) & (pixels < starts + chip_side)).astype(jnp.float32)
    first_rows = jnp.einsum("ax,bxy->bay", window_band, window_float, precision=precise)
    first_sum = jnp.einsum("bay,ey->bae", first_rows, window_band, precision=precise)
    second_rows = jnp.einsum(
        "ax,bxy->bay", window_band, window_float * window_float, precision=precise
    )
    second_sum = jnp.einsum("bay,ey->bae", second_rows, window_band, precision=precise)
    patch_mean = first_sum / (chip_side * chip_side)
    patch_var = second_sum / (chip_side * chip_side) - patch_mean * patch_mean
    score = numerator / (chip_side * chip_std[:, None, None] * jnp.sqrt(patch_var + epsilon))
    return score.reshape(-1, offsets * offsets)


def in_blocks(function, operands):
    amount = operands[0].shape[0]
    block_rows = 16
    shaped = tuple(
        (item.reshape((amount // block_rows, block_rows) + item.shape[1:]) for item in operands)
    )
    result = lax.map(lambda grouped: function(*grouped), shaped)
    return result.reshape(amount, -1)


def on_device(ref_chips, search_windows, dest_block, dest_slot):
    chips = ref_chips[0]
    windows = search_windows[0]
    targets = dest_block[0, :, 0]
    target_slot = dest_slot[0]
    chip_side = CHIP
    window_side = WIN
    offsets = window_side - chip_side
    window_amount = windows.shape[0]
    chip_amount = chips.shape[0]
    devices = lax.axis_size(("tile", "sub"))
    capacity = max(2, 2 * window_amount // devices)
    slot_amount = devices * capacity
    order = jnp.arange(window_amount, dtype=jnp.int32)
    matches = targets[:, None] == targets[None, :]
    earlier = order[:, None] > order[None, :]
    ranking = jnp.sum((matches & earlier).astype(jnp.int32), axis=1)
    positions = targets * capacity + ranking
    slot_buffer = jnp.full((slot_amount,), -1, jnp.int32).at[positions].set(target_slot)
    cos_chip, sin_chip = tables(window_side, chip_side)
    requests = slot_buffer.reshape(devices, capacity)
    found = jnp.take(
        chips,
        jnp.maximum(
            lax.all_to_all(requests, ("tile", "sub"), split_axis=0, concat_axis=0, tiled=True), 0
        ),
        axis=0,
    )
    fetched = lax.all_to_all(found, ("tile", "sub"), split_axis=0, concat_axis=0, tiled=True)
    own_chips = jnp.take(fetched.reshape(slot_amount, chip_side * chip_side), positions, axis=0)

    def match_own(chip_part, window_part):
        centred_part, std_part = centre(chip_part, chip_side)
        real_part, imag_part = spectrum(centred_part, cos_chip, sin_chip)
        return match(real_part, imag_part, std_part, window_part, chip_side, window_side)

    own_scores = in_blocks(match_own, (own_chips, windows))
    score_buffer = (
        jnp.zeros((slot_amount, offsets * offsets), jnp.float32).at[positions].set(own_scores)
    )
    scores, slots_here = (
        lax.all_to_all(score_buffer, ("tile", "sub"), split_axis=0, concat_axis=0, tiled=True),
        lax.all_to_all(slot_buffer, ("tile", "sub"), split_axis=0, concat_axis=0, tiled=True),
    )
    hits_table = (slots_here[None, :] == jnp.arange(chip_amount, dtype=jnp.int32)[:, None]).astype(
        jnp.float32
    )
    total = jnp.dot(hits_table, scores, precision=precise)
    looks = jnp.sum(hits_table, axis=1)
    average = total / jnp.maximum(looks, 1.0)[:, None]
    grid = average.reshape(-1, GC, offsets * offsets)
    extended = padded(grid, ((("tile", "sub"), 0),), 1)
    vertical = extended[:-2] + extended[2:]
    sideways = jnp.pad(grid, ((0, 0), (1, 1), (0, 0)))
    horizontal = sideways[:, :-2] + sideways[:, 2:]
    smoothed = (4.0 * grid + vertical + horizontal) / 8.0
    return smoothed.reshape(1, chip_amount, offsets * offsets)


def solution(mesh):
    return jax.shard_map(
        on_device,
        mesh=mesh,
        in_specs=(
            P(("groups", "pair"), ("tile", "sub"), None),
            P(("groups", "pair"), ("tile", "sub"), None),
            P(("groups", "pair"), ("tile", "sub"), None),
            P(("groups", "pair"), ("tile", "sub")),
        ),
        out_specs=P(("groups", "pair"), ("tile", "sub"), None),
        check_vma=False,
    )
```

profile of v0, /device:TPU:1, one launch (start us, length us, event | category | flops | bytes accessed | tf_op | source)
XLA Modules:
  0.0 226.2 jit_solution(14719844709658617581)
XLA Ops:
  2.6 11.0 %all_to_all.35 = s32[8,1,16]{2,1,0:T(1,128)S(1)} all-to-all(s32[8,1,16]{2,1,0:T(1,128)S(1)} %bitcast.236), channel_id=1, replica_groups=mesh['groups'=2,'tile'=4,'pair'=2,'sub'=2] {'tile','sub'}, dimensions={0} | all-to-all | bytes 1024 | tf_op jit(solution)/shard_map/all_to_all | solution.py:125
  16.1 4.2 %all-to-all-start.2 = ((bf16[8,16,4096]{2,1,0:T(8,128)(2,1)}), bf16[8,16,4096]{2,1,0:T(8,128)(2,1)S(1)}, u32[]{:S(2)}, u32[]{:S(2)}) async-start(bf16[8,16,4096]{2,1,0:T(8,128)(2,1)} %broadcast_select_fusion), calls=%async_computation.2 | async-start | bytes 2097152 | tf_op jit(solution)/shard_map/all_to_all | solution.py:129
  21.1 24.7 %all-to-all-done.2 = bf16[8,16,4096]{2,1,0:T(8,128)(2,1)S(1)} async-done(((bf16[8,16,4096]{2,1,0:T(8,128)(2,1)}), bf16[8,16,4096]{2,1,0:T(8,128)(2,1)S(1)}, u32[]{:S(2)}, u32[]{:S(2)}) %all-to-all-start.2) | async-done | bytes 1048608 | tf_op jit(solution)/shard_map/all_to_all | solution.py:129
  45.9 4.2 %all-to-all-start = ((s32[8,16,1]{1,2,0:T(1,128)}), s32[8,16,1]{1,2,0:T(1,128)S(1)}, u32[]{:S(2)}, u32[]{:S(2)}) async-start(s32[8,16,1]{1,2,0:T(1,128)} %bitcast.5), calls=%async_computation | async-start | bytes 8192 | tf_op jit(solution)/shard_map/all_to_all | solution.py:143
  51.0 109.2 %while.14 = (s32[]{:T(128)}, f32[4,16,4096]{2,1,0:T(8,128)S(1)}, bf16[4,16,4096]{2,1,0:T(8,128)(2,1)S(1)}, bf16[4,16,16384]{2,1,0:T(8,128)(2,1)}, s32[]{:T(128)}) while((s32[]{:T(128)}, f32[4,16,4096]{2,1,0:T(8,128)S(1)}, bf16[4,16,4096]{2,1,0:T(8,128)(2,1)S(1)}, bf16[4,16,16384]{2,1,0:T(8,128)(2,1)}, s32[]{:T(128)}) %tuple.39), condition=%wide.region_5.6_spmd.clone.clone, body=%wide.region_2.5_spmd.clone.clone.sunk | while | flops 4872994816 | bytes 46598104 | solution.py:97
  58.1 2.0 fusion.248
  60.1 1.9 convolution_add_fusion.5
  62.1 1.9 fusion.252
  64.0 1.9 convolution_subtract_fusion.5
  85.4 2.0 fusion.248
  87.4 1.9 convolution_add_fusion.5
  91.3 1.9 convolution_subtract_fusion.5
  112.7 2.0 fusion.248
  114.6 1.9 convolution_add_fusion.5
  118.5 1.9 convolution_subtract_fusion.5
  139.9 2.0 fusion.248
  141.9 1.9 convolution_add_fusion.5
  143.8 1.9 fusion.252
  145.8 1.9 convolution_subtract_fusion.5
  160.3 2.6 %scatter_custom_fusion.1 = f32[128,4096]{1,0:T(8,128)} fusion(s32[64]{0:T(128)S(1)} %fusion.136, f32[64,4096]{1,0:T(8,128)S(1)} %bitcast.237, f32[]{:T(128)} %constant.141.clone.1), kind=kCustom, calls=%fused_computation.150 | custom fusion | bytes 2097156 | tf_op jit(solution)/shard_map/scatter | solution.py:139
  162.9 5.1 %all-to-all-start.3 = ((f32[8,16,4096]{2,1,0:T(8,128)}), f32[8,16,4096]{2,1,0:T(8,128)S(1)}, u32[]{:S(2)}, u32[]{:S(2)}) async-start(f32[8,16,4096]{2,1,0:T(8,128)} %bitcast.15), calls=%async_computation.3 | async-start | bytes 4194304 | tf_op jit(solution)/shard_map/all_to_all | solution.py:142
  169.4 46.7 %all-to-all-done.3 = f32[8,16,4096]{2,1,0:T(8,128)S(1)} async-done(((f32[8,16,4096]{2,1,0:T(8,128)}), f32[8,16,4096]{2,1,0:T(8,128)S(1)}, u32[]{:S(2)}, u32[]{:S(2)}) %all-to-all-start.3) | async-done | bytes 2097184 | tf_op jit(solution)/shard_map/all_to_all | solution.py:142
  218.9 2.4 %collective-permute-start.1 = (f32[1,8,4096]{2,1,0:T(8,128)S(1)}, f32[1,8,4096]{2,1,0:T(8,128)S(1)}, u32[]{:S(2)}, u32[]{:S(2)}) collective-permute-start(f32[1,8,4096]{2,1,0:T(8,128)S(1)} %get-tuple-element.139), channel_id=1, source_target_pairs={{1,0},{4,1},{5,4},{8,5},{9,8},{12,9},{13,12},{3,2},{6,3},{7,6},{10... | collective-permute-start | bytes 393224 | tf_op jit(solution)/shard_map/ppermute | solution.py:25
  221.3 3.9 %collective-permute-done.1 = f32[1,8,4096]{2,1,0:T(8,128)S(1)} collective-permute-done((f32[1,8,4096]{2,1,0:T(8,128)S(1)}, f32[1,8,4096]{2,1,0:T(8,128)S(1)}, u32[]{:S(2)}, u32[]{:S(2)}) %collective-permute-start.1) | collective-permute-done | bytes 131104 | tf_op jit(solution)/shard_map/ppermute | solution.py:25
  (164 shorter events, 92.8 us)
Async XLA Ops:
  0.0 13.7 %copy-start = (bf16[1,32,4096]{2,1,0:T(8,128)(2,1)S(1)}, bf16[1,32,4096]{2,1,0:T(8,128)(2,1)}, u32[]{:S(2)}) copy-start(bf16[1,32,4096]{2,1,0:T(8,128)(2,1)} %param.6) | copy-start | bytes 786436
  14.9 6.1 %copy-start.1 = (s32[1,64,1]{1,2,0:T(1,128)S(1)}, s32[1,64,1]{1,2,0:T(1,128)}, u32[]{:S(2)}) copy-start(s32[1,64,1]{1,2,0:T(1,128)} %param.8) | copy-start | bytes 772
  16.1 29.8 %all-to-all-start.2 = ((bf16[8,16,4096]{2,1,0:T(8,128)(2,1)}), bf16[8,16,4096]{2,1,0:T(8,128)(2,1)S(1)}, u32[]{:S(2)}, u32[]{:S(2)}) async-start(bf16[8,16,4096]{2,1,0:T(8,128)(2,1)} %broadcast_select_fusion), calls=%async_computation.2 | async-start | bytes 2097152 | tf_op jit(solution)/shard_map/all_to_all | solution.py:129
  45.9 117.0 %all-to-all-start = ((s32[8,16,1]{1,2,0:T(1,128)}), s32[8,16,1]{1,2,0:T(1,128)S(1)}, u32[]{:S(2)}, u32[]{:S(2)}) async-start(s32[8,16,1]{1,2,0:T(1,128)} %bitcast.5), calls=%async_computation | async-start | bytes 8192 | tf_op jit(solution)/shard_map/all_to_all | solution.py:143
  162.9 53.2 %all-to-all-start.3 = ((f32[8,16,4096]{2,1,0:T(8,128)}), f32[8,16,4096]{2,1,0:T(8,128)S(1)}, u32[]{:S(2)}, u32[]{:S(2)}) async-start(f32[8,16,4096]{2,1,0:T(8,128)} %bitcast.15), calls=%async_computation.3 | async-start | bytes 4194304 | tf_op jit(solution)/shard_map/all_to_all | solution.py:142
  217.0 4.3 %collective-permute-start = (f32[1,8,4096]{2,1,0:T(8,128)S(1)}, f32[1,8,4096]{2,1,0:T(8,128)S(1)}, u32[]{:S(2)}, u32[]{:S(2)}) collective-permute-start(f32[1,8,4096]{2,1,0:T(8,128)S(1)} %get-tuple-element.138), channel_id=1, source_target_pairs={{0,1},{1,4},{4,5},{5,8},{8,9},{9,12},{12,13},{2,3},{3,6},{6,7},{7,... | collective-permute-start | bytes 393224 | tf_op jit(solution)/shard_map/ppermute | solution.py:22
  218.9 6.3 %collective-permute-start.1 = (f32[1,8,4096]{2,1,0:T(8,128)S(1)}, f32[1,8,4096]{2,1,0:T(8,128)S(1)}, u32[]{:S(2)}, u32[]{:S(2)}) collective-permute-start(f32[1,8,4096]{2,1,0:T(8,128)S(1)} %get-tuple-element.139), channel_id=1, source_target_pairs={{1,0},{4,1},{5,4},{8,5},{9,8},{12,9},{13,12},{3,2},{6,3},{7,6},{10... | collective-permute-start | bytes 393224 | tf_op jit(solution)/shard_map/ppermute | solution.py:25
where the time goes:
time: 227 us; the launch traced here: 226 us
  matrix products  98 us (43%)
  waiting for transfers between devices  75.3 us (33%)
  starting transfers between devices  17.8 us (8%)
  local copies, waits for them, and re-layouts  14.4 us (6%)
  blocking collectives  11 us (5%)
  other arithmetic  8.43 us (4%)
    all_to_all x1, waiting for transfers between devices, on_device(): lax.all_to_all(score_buffer, ('tile', 'sub'), split_axis=0, concat_axis=0...  46.7 us
    all_to_all x1, waiting for transfers between devices, on_device(): lax.all_to_all(found, ('tile', 'sub'), split_axis=0, concat_axis=0, tiled...  24.7 us
    dot_general x8, matrix products, spectrum(): jnp.einsum('bkm,lm->bkl', first_real, sine_table, precision=precise)  15.5 us
    dot_general x8, matrix products, spectrum(): jnp.einsum('bkm,lm->bkl', first_real, cosine, precision=precise)  15.1 us
    dot_general x8, matrix products, spectrum(): jnp.einsum('bkm,lm->bkl', first_imag, sine_table, precision=precise)  15.1 us
    dot_general x8, matrix products, spectrum(): jnp.einsum('bkm,lm->bkl', first_imag, cosine, precision=precise)  15 us
    all_to_all x1, blocking collectives, on_device(): lax.all_to_all(requests, ('tile', 'sub'), split_axis=0, concat_axis=0, ti...  11 us
    dot_general x8, matrix products, spectrum(): first_real = jnp.einsum('kn,bnm->bkm', cosine, image, precision=precise)  6.31 us
  transfers between devices with their start and end apart: 5, of which 3 were waited for; matrix products, arithmetic and copies ran while one was open for 50% of the time, Pallas kernels for 0%

commit v1 on v0

v1 whole, which is shorter than its diff:
```python
import functools

import jax
import jax.numpy as jnp
import ml_dtypes
import numpy as np
from jax import lax
from jax.experimental import pallas as pl
from jax.experimental.pallas import tpu as pltpu
from jax.sharding import PartitionSpec as P

CHIP = 64
WIN = 128
GC = 8
OFF = WIN - CHIP
PERIOD = WIN - 1
HALF = WIN // 2
ROWS = OFF * OFF // WIN
GROUP = 8
CODE = 32767.0
epsilon = 1e-06
f32 = jnp.float32
bf16 = jnp.bfloat16


def split_table(table):
    high = table.astype(ml_dtypes.bfloat16)
    low = (table - high.astype(np.float64)).astype(ml_dtypes.bfloat16)
    return (high, low)


def basis():
    freqs = np.arange(HALF)[:, None]
    places = np.arange(WIN)[None, :]
    angle = (freqs * places % PERIOD) * (2.0 * np.pi / PERIOD)
    used = (places < PERIOD).astype(np.float64)
    return (np.cos(angle) * used, np.sin(angle) * used)


def interleaved(table):
    return np.concatenate([table[0::2], table[1::2]], axis=0)


def twice(block):
    zero = np.zeros_like(block)
    return np.block([[block, zero], [zero, block]])


def tables():
    cosine, sine = basis()
    forward = np.concatenate([cosine, sine], axis=0)
    high, low = split_table(forward)
    starts = np.arange(OFF)[:, None]
    places = np.arange(WIN)[None, :]
    band = ((places >= starts) & (places < starts + CHIP)).astype(ml_dtypes.bfloat16)
    rows_band = interleaved(band)
    window_rows = np.concatenate([high, low, rows_band], axis=0)
    square_rows = np.concatenate([rows_band, rows_band], axis=1)
    window_lanes = np.concatenate([high.T, low.T], axis=1)
    window_lanes = np.concatenate([window_lanes, window_lanes], axis=0)
    band_lanes = twice(band.T)

    def chip_rows_of(part):
        joined = np.concatenate([part[:, 0:CHIP:2], part[:, 1:CHIP:2]], axis=1)
        return np.concatenate([joined, joined], axis=1)

    chip_rows = np.concatenate([chip_rows_of(high), chip_rows_of(low)], axis=0)
    same = np.concatenate([cosine, cosine], axis=0)[:, :CHIP].T
    cross = np.concatenate([sine, -sine], axis=0)[:, :CHIP].T
    same_high, same_low = split_table(same)
    cross_high, cross_low = split_table(cross)
    chip_lanes = np.concatenate([same_high, cross_high, same_low, cross_low], axis=1)
    chip_lanes = np.concatenate([chip_lanes] * 4, axis=0)
    weight = np.full((2 * HALF, 1), 2.0 / PERIOD)
    weight[0] = 1.0 / PERIOD
    inverse = (forward * weight)[:, :OFF].T
    inv_high, inv_low = split_table(inverse)
    rows_high, rows_low = interleaved(inv_high), interleaved(inv_low)
    inverse_rows = np.block([[rows_high, rows_high], [rows_low, rows_low]])
    inverse_lanes = np.concatenate([twice(inv_high.T), twice(inv_low.T)], axis=1)
    inverse_lanes = np.concatenate([inverse_lanes, inverse_lanes], axis=0)
    return dict(
        window_rows=window_rows, square_rows=square_rows, window_lanes=window_lanes,
        band_lanes=band_lanes, chip_rows=chip_rows, chip_lanes=chip_lanes,
        inverse_rows=inverse_rows, inverse_lanes=inverse_lanes,
    )


def dot(left, right):
    return jnp.dot(left, right, preferred_element_type=f32)


def halves(value):
    high = value.astype(bf16)
    low = (value - high.astype(f32)).astype(bf16)
    return (high, low)


def thirds(value):
    high = value.astype(bf16)
    rest = value - high.astype(f32)
    middle = rest.astype(bf16)
    low = (rest - middle.astype(f32)).astype(bf16)
    return (high, middle, low)


def window_kernel(windows, window_rows, square_rows, window_lanes, band_lanes, spectra, scale):
    group = windows.shape[0]
    for first in range(0, group, 2):
        image = jnp.concatenate([windows[first], windows[first + 1]], axis=1)
        rows = dot(window_rows[...], image)
        spec_rows = rows[:WIN] + rows[WIN:2 * WIN]
        sums = rows[2 * WIN:]
        wide = image.astype(f32)
        square_high, square_low = halves(wide * wide)
        squares = dot(square_rows[...], jnp.concatenate([square_high, square_low], axis=0))
        for part in range(2):
            lanes = slice(part * WIN, (part + 1) * WIN)
            high, low = halves(spec_rows[:, lanes])
            both = dot(jnp.concatenate([high, low], axis=1), window_lanes[...])
            spectra[first + part] = both[:, :WIN] + both[:, WIN:]
            pieces = []
            for source in (sums, squares):
                own = source[:, lanes]
                packed = jnp.concatenate([own[:ROWS], own[ROWS:]], axis=1)
                pieces.extend(thirds(packed))
            boxed = dot(jnp.concatenate(pieces, axis=0), band_lanes[...])
            boxes = [boxed[i * ROWS:(i + 1) * ROWS] for i in range(6)]
            mean = (boxes[0] + boxes[1] + boxes[2]) * (1.0 / (CHIP * CHIP))
            second = (boxes[3] + boxes[4] + boxes[5]) * (1.0 / (CHIP * CHIP))
            variance = second - mean * mean
            scale[first + part] = lax.rsqrt(variance + epsilon)


def full_sum(value):
    return jnp.sum(jnp.sum(value, axis=0, keepdims=True), axis=1, keepdims=True)


def score_kernel(
    capacity, chip_amount, choice, place, target, ranks, slots, position,
    spectra, scale, chip_rows, chip_lanes, inverse_rows, inverse_lanes, *rest,
):
    *sources, out, marks = rest
    step = pl.program_id(0)
    group = spectra.shape[0]
    body = capacity * ROWS
    lane = lax.broadcasted_iota(jnp.int32, (8, WIN), 1)
    line = lax.broadcasted_iota(jnp.int32, (8, WIN), 0)

    @pl.when(step == 0)
    def _():
        out[...] = jnp.zeros_like(out)
        marks[...] = jnp.zeros_like(marks)

    even = lax.broadcasted_iota(jnp.int32, (ROWS, WIN), 1) < CHIP
    zero = jnp.zeros((ROWS, WIN), f32)
    for first in range(0, group, 2):
        images = []
        gains = []
        for part in range(2):
            window = step * group + first + part
            raw = sources[0][place[window]].astype(f32)
            for index in range(1, len(sources)):
                other = sources[index][place[window]].astype(f32)
                raw = jnp.where(choice[window] == index, other, raw)
            centred = raw - full_sum(raw) * (1.0 / (CHIP * CHIP))
            power = full_sum(centred * centred) * (1.0 / (CHIP * CHIP))
            gains.append(lax.rsqrt(power + epsilon) * (1.0 / CHIP))
            high = centred.astype(bf16).astype(f32)
            low = centred - high
            images.append(jnp.concatenate([
                jnp.where(even, high, zero).astype(bf16), jnp.where(even, zero, high).astype(bf16),
                jnp.where(even, low, zero).astype(bf16), jnp.where(even, zero, low).astype(bf16),
            ], axis=0))
        rows = dot(chip_rows[...], jnp.concatenate(images, axis=1))
        rows = rows[:WIN] + rows[WIN:]
        products = []
        for part in range(2):
            high, low = halves(rows[:, part * WIN:(part + 1) * WIN])
            both = dot(jnp.concatenate([high, low], axis=1), chip_lanes[...])
            both = both[:, :2 * WIN] + both[:, 2 * WIN:]
            same, cross = both[:, :WIN], both[:, WIN:]
            own = spectra[first + part]
            turned = pltpu.roll(own, HALF, 1)
            same_c, same_s = same[:HALF], same[HALF:]
            cross_c, cross_s = cross[:HALF], cross[HALF:]
            own_c, own_s = own[:HALF], own[HALF:]
            turned_c, turned_s = turned[:HALF], turned[HALF:]
            out_c = same_c * own_c + cross_c * turned_c + same_s * own_s + cross_s * turned_s
            out_s = same_c * own_s + cross_c * turned_s - same_s * own_c - cross_s * turned_c
            product = jnp.concatenate([out_c, out_s], axis=0)
            products.append(jnp.concatenate(halves(product), axis=0))
        back = dot(inverse_rows[...], jnp.concatenate(products, axis=1))
        back = back[:OFF] + back[OFF:]
        for part in range(2):
            window = step * group + first + part
            mine = back[:, part * WIN:(part + 1) * WIN]
            packed = jnp.concatenate([mine[:ROWS], mine[ROWS:]], axis=1)
            both = dot(jnp.concatenate(halves(packed), axis=1), inverse_lanes[...])
            numerator = both[:, :WIN] + both[:, WIN:]
            score = numerator * (scale[first + part] * gains[part])
            size = jnp.abs(score)
            largest = jnp.max(jnp.max(size, axis=0, keepdims=True), axis=1, keepdims=True)
            power = jnp.ceil(jnp.log2(jnp.maximum(largest, 1e-30)))
            root = jnp.sqrt(size * jnp.exp2(-power).astype(bf16).astype(f32))
            code = jnp.minimum(jnp.round(root * CODE), CODE)
            code = jnp.where(score < 0, -code, code).astype(jnp.int32).astype(jnp.int16)
            to = target[window]
            out[to, pl.ds(pl.multiple_of(ranks[window] * ROWS, ROWS), ROWS), :] = code
            here = lane == position[0] * capacity + ranks[window]
            named = (slots[window] + 1).astype(f32)
            mark = jnp.where(line == 0, named, jnp.where(line == 1, power, 0.0))
            marks[to] = marks[to] + jnp.where(here, mark, 0.0)

    @pl.when(step == pl.num_programs(0) - 1)
    def _():
        for to in range(out.shape[0]):
            notes = marks[to]
            notes = jnp.concatenate([notes, jnp.zeros_like(notes)], axis=0)
            out[to, body:, :] = notes.astype(jnp.int32).astype(jnp.int16)


def average_kernel(capacity, chip_amount, codes, smooth, first, last, values):
    devices = codes.shape[0]
    body = capacity * ROWS
    slots = devices * capacity
    notes = codes[0, body:, :].astype(jnp.int32).astype(f32)
    for source in range(1, devices):
        notes = notes + codes[source, body:, :].astype(jnp.int32).astype(f32)
    for source in range(devices):
        wide = codes[source, :body, :].astype(jnp.int32).astype(f32)
        values[source * body:(source + 1) * body, :] = wide * jnp.abs(wide)
    chip = lax.broadcasted_iota(jnp.int32, (chip_amount, WIN), 0)
    hit = (notes[0:1] - 1.0).astype(jnp.int32) == chip
    looks = jnp.sum(hit.astype(f32), axis=1, keepdims=True)
    weight = jnp.where(hit, jnp.exp2(notes[1:2]), 0.0).astype(bf16)[:, :slots]
    weight = jnp.concatenate([weight, weight], axis=1)
    factor = 1.0 / (jnp.maximum(looks, 1.0) * (CODE * CODE))
    factor = jnp.broadcast_to(factor, (chip_amount, WIN))
    column = chip % GC
    zero = jnp.zeros((GC, WIN), f32)
    for row in range(ROWS):
        high, low = halves(values[pl.ds(row, slots, stride=ROWS), :])
        average = dot(weight, jnp.concatenate([high, low], axis=0)) * factor
        lanes = slice(row * WIN, (row + 1) * WIN)
        first[:, lanes] = average[:GC]
        last[:, lanes] = average[chip_amount - GC:]
        below = jnp.concatenate([average[GC:], zero], axis=0)
        above = jnp.concatenate([zero, average[:-GC]], axis=0)
        left = jnp.where(column == 0, 0.0, pltpu.roll(average, 1, 0))
        right = jnp.where(column == GC - 1, 0.0, pltpu.roll(average, chip_amount - 1, 0))
        smooth[:, lanes] = (4.0 * average + above + below + left + right) * 0.125


def whole(array):
    return pl.BlockSpec(array.shape, lambda *_: (0,) * array.ndim)


def prepare_windows(windows, table):
    amount = windows.shape[0]
    group = min(GROUP, amount)
    images = windows.reshape(amount, WIN, WIN)
    constants = [jnp.asarray(table[k]) for k in ("window_rows", "square_rows", "window_lanes", "band_lanes")]
    return pl.pallas_call(
        window_kernel,
        grid=(amount // group,),
        in_specs=[pl.BlockSpec((group, WIN, WIN), lambda i: (i, 0, 0))] + [whole(c) for c in constants],
        out_specs=[
            pl.BlockSpec((group, WIN, WIN), lambda i: (i, 0, 0)),
            pl.BlockSpec((group, ROWS, WIN), lambda i: (i, 0, 0)),
        ],
        out_shape=[
            jax.ShapeDtypeStruct((amount, WIN, WIN), f32),
            jax.ShapeDtypeStruct((amount, ROWS, WIN), f32),
        ],
        name="window_spectra",
    )(images, *constants)


def score_windows(spectra, scale, sources, scalars, table, devices, capacity, chip_amount):
    amount = spectra.shape[0]
    group = min(GROUP, amount)
    constants = [jnp.asarray(table[k]) for k in ("chip_rows", "chip_lanes", "inverse_rows", "inverse_lanes")]
    shape = (devices, capacity * ROWS + 16, WIN)
    return pl.pallas_call(
        functools.partial(score_kernel, capacity, chip_amount),
        grid_spec=pltpu.PrefetchScalarGridSpec(
            num_scalar_prefetch=len(scalars),
            grid=(amount // group,),
            in_specs=[
                pl.BlockSpec((group, WIN, WIN), lambda i, *_: (i, 0, 0)),
                pl.BlockSpec((group, ROWS, WIN), lambda i, *_: (i, 0, 0)),
            ] + [whole(c) for c in constants] + [whole(s) for s in sources],
            out_specs=pl.BlockSpec(shape, lambda i, *_: (0, 0, 0)),
            scratch_shapes=[pltpu.VMEM((devices, 8, WIN), f32)],
        ),
        out_shape=jax.ShapeDtypeStruct(shape, jnp.int16),
        name="scores",
    )(*scalars, spectra, scale, *constants, *sources)


def average_scores(codes, capacity, chip_amount):
    devices = codes.shape[0]
    return pl.pallas_call(
        functools.partial(average_kernel, capacity, chip_amount),
        out_shape=[
            jax.ShapeDtypeStruct((chip_amount, OFF * OFF), f32),
            jax.ShapeDtypeStruct((GC, OFF * OFF), f32),
            jax.ShapeDtypeStruct((GC, OFF * OFF), f32),
        ],
        scratch_shapes=[pltpu.VMEM((devices * capacity * ROWS, WIN), f32)],
        name="average",
    )(codes)


def on_device(ref_chips, search_windows, dest_block, dest_slot):
    table = tables()
    chips = ref_chips[0]
    windows = search_windows[0]
    targets = dest_block[0, :, 0]
    slots = dest_slot[0]
    window_amount = windows.shape[0]
    chip_amount = chips.shape[0]
    tiles = lax.axis_size("tile")
    subs = lax.axis_size("sub")
    devices = tiles * subs
    capacity = max(2, 2 * window_amount // devices)

    images = chips.reshape(chip_amount, ROWS, WIN)
    sent = jnp.broadcast_to(images[None], (tiles,) + images.shape)
    gathered = lax.all_to_all(sent, "tile", split_axis=0, concat_axis=0, tiled=True)
    gathered = gathered.reshape(tiles * chip_amount, ROWS, WIN)
    sources = [gathered]
    for shift in range(1, subs):
        ring = [(i, (i - shift) % subs) for i in range(subs)]
        sources.append(lax.ppermute(gathered, "sub", ring))

    spectra, scale = prepare_windows(windows, table)

    order = jnp.arange(window_amount, dtype=jnp.int32)
    matches = targets[:, None] == targets[None, :]
    earlier = order[:, None] > order[None, :]
    ranks = jnp.sum((matches & earlier).astype(jnp.int32), axis=1)
    choice = (targets % subs - lax.axis_index("sub")) % subs
    place = (targets // subs) * chip_amount + slots
    position = jnp.full((1,), lax.axis_index(("tile", "sub")), jnp.int32)
    scalars = (choice, place, targets, ranks, slots, position)
    codes = score_windows(spectra, scale, sources, scalars, table, devices, capacity, chip_amount)

    received = lax.all_to_all(codes, ("tile", "sub"), split_axis=0, concat_axis=0, tiled=True)
    smooth, first, last = average_scores(received, capacity, chip_amount)
    forward = [(i, i + 1) for i in range(devices - 1)]
    backward = [(i + 1, i) for i in range(devices - 1)]
    above = lax.ppermute(last, ("tile", "sub"), forward)
    below = lax.ppermute(first, ("tile", "sub"), backward)
    top = smooth[:GC] + above * 0.125
    bottom = smooth[chip_amount - GC:] + below * 0.125
    result = jnp.concatenate([top, smooth[GC:chip_amount - GC], bottom], axis=0)
    return result[None]


def solution(mesh):
    return jax.shard_map(
        on_device,
        mesh=mesh,
        in_specs=(
            P(("groups", "pair"), ("tile", "sub"), None),
            P(("groups", "pair"), ("tile", "sub"), None),
            P(("groups", "pair"), ("tile", "sub"), None),
            P(("groups", "pair"), ("tile", "sub")),
        ),
        out_specs=P(("groups", "pair"), ("tile", "sub"), None),
        check_vma=False,
    )
```

time: 227 us -> 120 us (0.53)
  matrix products: 98 us -> 0 us
  waiting for transfers between devices: 75.3 us -> 3.59 us
  blocking collectives: 11 us -> 61.1 us
  Pallas kernels: 0 us -> 41.2 us
  starting transfers between devices: 17.8 us -> 6.22 us
  local copies, waits for them, and re-layouts: 14.4 us -> 4.18 us
  other arithmetic: 8.43 us -> 3.19 us
    dot_general x89 -> x0, matrix products: 98 us -> none  [the longest x8 15.5 us: spectrum(): jnp.einsum('bkm,lm->bkl', first_real, sine_table, precision=precise)]
    all_to_all x3 -> x0, waiting for transfers between devices: 71.4 us -> none  [the longest x1 46.7 us: on_device(): lax.all_to_all(score_buffer, ('tile', 'sub'), split_axis=0, concat_axis=0...]
    all_to_all x1 -> x2, blocking collectives: 11 us -> 61.1 us  [the longest x1 30.9 us: on_device(): lax.all_to_all(codes, ('tile', 'sub'), split_axis=0, concat_axis=0, tiled...]
    pallas_call x0 -> x3, Pallas kernels: none -> 41.2 us  [the longest x1 26.2 us: score_windows(): pl.pallas_call(functools.partial(score_kernel, capacity, chip_amount), gr...]
    all_to_all x3 -> x0, starting transfers between devices: 13.5 us -> none  [the longest x1 5.13 us: on_device(): lax.all_to_all(score_buffer, ('tile', 'sub'), split_axis=0, concat_axis=0...]
    while x8 -> x0, local copies, waits for them, and re-layouts: 4.69 us -> none
    scatter x2 -> x0, local copies, waits for them, and re-layouts: 3.51 us -> none  [the longest x1 2.61 us: on_device(): jnp.zeros((slot_amount, offsets * offsets), jnp.float32).at[positions]]
    unnamed x4 -> x10, local copies, waits for them, and re-layouts: 0.01 us -> 3.06 us
  transfers between devices with their start and end apart: 5 -> 3, of which waited for: 3 -> 1; matrix products, arithmetic and copies ran while one was open for 50% -> 4% of each run, Pallas kernels for 0% -> 9%
where the time goes in v1:
time: 120 us; the launch traced here: 119 us
  blocking collectives  61.1 us (51%)
  Pallas kernels  41.2 us (34%)
  starting transfers between devices  6.22 us (5%)
  local copies, waits for them, and re-layouts  4.18 us (3%)
  waiting for transfers between devices  3.59 us (3%)
  other arithmetic  3.19 us (3%)
    all_to_all x1, blocking collectives, on_device(): lax.all_to_all(codes, ('tile', 'sub'), split_axis=0, concat_axis=0, tiled...  30.9 us
    all_to_all x1, blocking collectives, on_device(): lax.all_to_all(sent, 'tile', split_axis=0, concat_axis=0, tiled=True)  30.1 us
    pallas_call x1, Pallas kernels, score_windows(): pl.pallas_call(functools.partial(score_kernel, capacity, chip_amount), gr...  26.2 us
    pallas_call x1, Pallas kernels, prepare_windows(): pl.pallas_call(window_kernel, grid=(amount // group,), in_specs=[pl.Block...  11.1 us
    pallas_call x1, Pallas kernels, average_scores(): pl.pallas_call(functools.partial(average_kernel, capacity, chip_amount),...  3.87 us
    ppermute x1, waiting for transfers between devices, on_device(): below = lax.ppermute(first, ('tile', 'sub'), backward)  3.58 us
    unnamed x10, local copies, waits for them, and re-layouts  3.06 us
    ppermute x1, starting transfers between devices, on_device(): above = lax.ppermute(last, ('tile', 'sub'), forward)  2.55 us
  transfers between devices with their start and end apart: 3, of which 1 were waited for; matrix products, arithmetic and copies ran while one was open for 4% of the time, Pallas kernels for 9%

profile of v1, /device:TPU:1, one launch (start us, length us, event | category | flops | bytes accessed | tf_op | source)
XLA Modules:
  0.0 119.5 jit_solution(11950444038915945552)
XLA Ops:
  0.0 0.0 copy-start.1
  0.0 1.1 copy.14
  1.1 0.2 broadcast_in_dim.17
  1.3 30.1 %all_to_all.10 = bf16[4,32,32,128]{3,2,1,0:T(8,128)(2,1)S(1)} all-to-all(bf16[4,32,32,128]{3,2,1,0:T(8,128)(2,1)S(1)} %broadcast_in_dim.17), channel_id=1, replica_groups=mesh['groups'=2,'tile'=4,'pair'=2,'sub'=2] {'tile'}, dimensions={0} | all-to-all | bytes 2097152 | tf_op jit(solution)/shard_map/all_to_all | solution.py:331
  31.5 1.8 %collective-permute-start = (bf16[128,32,128]{2,1,0:T(8,128)(2,1)S(1)}, bf16[128,32,128]{2,1,0:T(8,128)(2,1)}, u32[]{:S(2)}, u32[]{:S(2)}) collective-permute-start(bf16[128,32,128]{2,1,0:T(8,128)(2,1)S(1)} %bitcast.20), channel_id=1, source_target_pairs={{0,1},{1,0},{2,3},{3,2},{4,5},{5,4},{6,7},{7,6},{8,9},{9,8},{10,11... | collective-permute-start | bytes 3145736 | tf_op jit(solution)/shard_map/ppermute | solution.py:336
  33.2 0.0 copy-done.1
  33.2 1.9 %copy.13 = bf16[8,8,128,128]{3,2,1,0:T(8,128)(2,1)} copy(bf16[8,8,128,128]{3,1,2,0:T(8,128)(2,1)S(1)} %bitcast.22) | data formatting | bytes 4194304
  35.1 0.0 copy-done
  35.1 11.1 %window_spectra.1 = (f32[64,128,128]{2,1,0:T(8,128)}, f32[64,32,128]{2,1,0:T(8,128)}) custom-call(bf16[64,128,128]{2,1,0:T(8,128)(2,1)} %bitcast.19, bf16[320,128]{1,0:T(8,128)(2,1)} %constant.61.clone.window_rows, bf16[64,256]{1,0:T(8,128)(2,1)} %constant.62.clone.square_rows, bf16[256,256]{1,0:T(8,128)(2,1)} %constant.63.clone.window_lanes, ...), custom_call_target="tpu_custom_call" | custom-call | tf_op jit(solution)/shard_map/window_spectra/pallas_call | solution.py:264
  46.2 0.0 copy-done.3
  46.2 0.8 convert_reduce_fusion.ranks
  47.0 0.0 copy-done.2
  47.0 0.6 multiply_add_fusion.2
  47.6 0.0 collective-permute-done.rest_1_
  47.6 26.2 %scores.1 = s16[8,528,128]{2,1,0:T(8,128)(2,1)} custom-call(s32[64]{0:T(128)} %get-tuple-element.18.choice, s32[64]{0:T(128)} %get-tuple-element.17.place, s32[64]{0:T(128)} %bitcast.26, s32[64]{0:T(128)} %convert_reduce_fusion.ranks, s32[64]{0:T(128)} %bitcast.25, s32[1]{0:T(128)} %bitcast.2.position, f32[64,128,128]{2,1,0:T(8,128)} %get-tuple-element.10.spectra, ...), custom_call_target="tpu_custom_call" | custom-call | tf_op jit(solution)/shard_map/scores/pallas_call | solution.py:285
  73.8 30.9 %all_to_all.11.codes = s16[8,528,128]{2,1,0:T(8,128)(2,1)} all-to-all(s16[8,528,128]{2,1,0:T(8,128)(2,1)} %scores.1), channel_id=1, replica_groups=mesh['groups'=2,'tile'=4,'pair'=2,'sub'=2] {'tile','sub'}, dimensions={0} | all-to-all | bytes 2162688 | tf_op jit(solution)/shard_map/all_to_all | solution.py:350
  104.7 3.9 %average.1 = (f32[32,4096]{1,0:T(8,128)}, f32[8,4096]{1,0:T(8,128)}, f32[8,4096]{1,0:T(8,128)}) custom-call(s16[8,528,128]{2,1,0:T(8,128)(2,1)} %all_to_all.11.codes), custom_call_target="tpu_custom_call" | custom-call | tf_op jit(solution)/shard_map/average/pallas_call | solution.py:304
  108.6 2.5 %collective-permute-start.1 = (f32[8,4096]{1,0:T(8,128)}, f32[8,4096]{1,0:T(8,128)S(1)}, u32[]{:S(2)}, u32[]{:S(2)}) collective-permute-start(f32[8,4096]{1,0:T(8,128)} %get-tuple-element.13), channel_id=1, source_target_pairs={{0,1},{1,4},{4,5},{5,8},{8,9},{9,12},{12,13},{2,3},{3,6},{6,7},{7,... | collective-permute-start | bytes 393224 | tf_op jit(solution)/shard_map/ppermute | solution.py:354
  111.2 1.9 %collective-permute-start.2 = (f32[8,4096]{1,0:T(8,128)}, f32[8,4096]{1,0:T(8,128)S(1)}, u32[]{:S(2)}, u32[]{:S(2)}) collective-permute-start(f32[8,4096]{1,0:T(8,128)} %get-tuple-element.14), channel_id=1, source_target_pairs={{1,0},{4,1},{5,4},{8,5},{9,8},{12,9},{13,12},{3,2},{6,3},{7,6},{10... | collective-permute-start | bytes 393224 | tf_op jit(solution)/shard_map/ppermute | solution.py:355
  113.1 1.0 slice.10
  114.1 0.0 collective-permute-done.1
  114.1 3.6 %collective-permute-done.2 = f32[8,4096]{1,0:T(8,128)S(1)} collective-permute-done((f32[8,4096]{1,0:T(8,128)}, f32[8,4096]{1,0:T(8,128)S(1)}, u32[]{:S(2)}, u32[]{:S(2)}) %collective-permute-start.2) | collective-permute-done | bytes 131104 | tf_op jit(solution)/shard_map/ppermute | solution.py:355
  117.7 1.0 multiply_add_fusion.1
  118.7 0.8 maximum_bitcast_fusion
  (3 shorter events, 0.0 us)
Async XLA Ops:
  0.0 33.2 %copy-start.1 = (bf16[1,64,16384]{2,1,0:T(8,128)(2,1)S(1)}, bf16[1,64,16384]{2,1,0:T(8,128)(2,1)}, u32[]{:S(2)}) copy-start(bf16[1,64,16384]{2,1,0:T(8,128)(2,1)} %param.13) | copy-start | bytes 6291460
  31.5 3.7 %copy-start = (bf16[4,32,32,128]{3,2,1,0:T(8,128)(2,1)}, bf16[4,32,32,128]{3,2,1,0:T(8,128)(2,1)S(1)}, u32[]{:S(2)}) copy-start(bf16[4,32,32,128]{3,2,1,0:T(8,128)(2,1)S(1)} %all_to_all.10) | copy-start | bytes 3145732
  31.5 16.1 %collective-permute-start = (bf16[128,32,128]{2,1,0:T(8,128)(2,1)S(1)}, bf16[128,32,128]{2,1,0:T(8,128)(2,1)}, u32[]{:S(2)}, u32[]{:S(2)}) collective-permute-start(bf16[128,32,128]{2,1,0:T(8,128)(2,1)S(1)} %bitcast.20), channel_id=1, source_target_pairs={{0,1},{1,0},{2,3},{3,2},{4,5},{5,4},{6,7},{7,6},{8,9},{9,8},{10,11... | collective-permute-start | bytes 3145736 | tf_op jit(solution)/shard_map/ppermute | solution.py:336
  35.1 11.1 %copy-start.3 = (s32[1,64,1]{1,2,0:T(1,128)S(1)}, s32[1,64,1]{1,2,0:T(1,128)}, u32[]{:S(2)}) copy-start(s32[1,64,1]{1,2,0:T(1,128)} %param.14) | copy-start | bytes 772
  35.1 11.9 %copy-start.2 = (s32[1,64]{1,0:T(1,128)S(1)}, s32[1,64]{1,0:T(1,128)}, u32[]{:S(2)}) copy-start(s32[1,64]{1,0:T(1,128)} %param.15) | copy-start | bytes 772
  108.6 5.5 %collective-permute-start.1 = (f32[8,4096]{1,0:T(8,128)}, f32[8,4096]{1,0:T(8,128)S(1)}, u32[]{:S(2)}, u32[]{:S(2)}) collective-permute-start(f32[8,4096]{1,0:T(8,128)} %get-tuple-element.13), channel_id=1, source_target_pairs={{0,1},{1,4},{4,5},{5,8},{8,9},{9,12},{12,13},{2,3},{3,6},{6,7},{7,... | collective-permute-start | bytes 393224 | tf_op jit(solution)/shard_map/ppermute | solution.py:354
  111.2 6.5 %collective-permute-start.2 = (f32[8,4096]{1,0:T(8,128)}, f32[8,4096]{1,0:T(8,128)S(1)}, u32[]{:S(2)}, u32[]{:S(2)}) collective-permute-start(f32[8,4096]{1,0:T(8,128)} %get-tuple-element.14), channel_id=1, source_target_pairs={{1,0},{4,1},{5,4},{8,5},{9,8},{12,9},{13,12},{3,2},{6,3},{7,6},{10... | collective-permute-start | bytes 393224 | tf_op jit(solution)/shard_map/ppermute | solution.py:355

commit v2 on v1

--- a/solution.py
+++ b/solution.py
@@ -17,6 +17,7 @@
 HALF = WIN // 2
 ROWS = OFF * OFF // WIN
 GROUP = 8
+SCORE_GROUP = 16
 CODE = 32767.0
 epsilon = 1e-06
 f32 = jnp.float32
@@ -60,17 +61,14 @@
     window_lanes = np.concatenate([window_lanes, window_lanes], axis=0)
     band_lanes = twice(band.T)
 
-    def chip_rows_of(part):
-        joined = np.concatenate([part[:, 0:CHIP:2], part[:, 1:CHIP:2]], axis=1)
-        return np.concatenate([joined, joined], axis=1)
-
-    chip_rows = np.concatenate([chip_rows_of(high), chip_rows_of(low)], axis=0)
+    def pair_of(part):
+        return np.concatenate([part[:, 0:CHIP:2], part[:, 1:CHIP:2]], axis=1)
+
+    chip_rows = np.concatenate([pair_of(high), pair_of(high), pair_of(low)], axis=1)
     same = np.concatenate([cosine, cosine], axis=0)[:, :CHIP].T
     cross = np.concatenate([sine, -sine], axis=0)[:, :CHIP].T
-    same_high, same_low = split_table(same)
-    cross_high, cross_low = split_table(cross)
-    chip_lanes = np.concatenate([same_high, cross_high, same_low, cross_low], axis=1)
-    chip_lanes = np.concatenate([chip_lanes] * 4, axis=0)
+    lane_high, lane_low = split_table(twice(np.concatenate([same, cross], axis=1)))
+    chip_lanes = np.concatenate([lane_high, lane_high, lane_low], axis=0)
     weight = np.full((2 * HALF, 1), 2.0 / PERIOD)
     weight[0] = 1.0 / PERIOD
     inverse = (forward * weight)[:, :OFF].T
@@ -132,15 +130,11 @@
             scale[first + part] = lax.rsqrt(variance + epsilon)
 
 
-def full_sum(value):
-    return jnp.sum(jnp.sum(value, axis=0, keepdims=True), axis=1, keepdims=True)
-
-
 def score_kernel(
-    capacity, chip_amount, choice, place, target, ranks, slots, position,
-    spectra, scale, chip_rows, chip_lanes, inverse_rows, inverse_lanes, *rest,
+    capacity, choice, place, target, ranks, slots, position,
+    spectra, scale, chip_lanes, chip_rows, inverse_rows, inverse_lanes, *rest,
 ):
-    *sources, out, marks = rest
+    *sources, out, marks, lefts, lines, packs, pairs, products, backs = rest
     step = pl.program_id(0)
     group = spectra.shape[0]
     body = capacity * ROWS
@@ -152,65 +146,93 @@
         out[...] = jnp.zeros_like(out)
         marks[...] = jnp.zeros_like(marks)
 
-    even = lax.broadcasted_iota(jnp.int32, (ROWS, WIN), 1) < CHIP
-    zero = jnp.zeros((ROWS, WIN), f32)
-    for first in range(0, group, 2):
-        images = []
-        gains = []
-        for part in range(2):
-            window = step * group + first + part
-            raw = sources[0][place[window]].astype(f32)
-            for index in range(1, len(sources)):
-                other = sources[index][place[window]].astype(f32)
-                raw = jnp.where(choice[window] == index, other, raw)
-            centred = raw - full_sum(raw) * (1.0 / (CHIP * CHIP))
-            power = full_sum(centred * centred) * (1.0 / (CHIP * CHIP))
-            gains.append(lax.rsqrt(power + epsilon) * (1.0 / CHIP))
-            high = centred.astype(bf16).astype(f32)
-            low = centred - high
-            images.append(jnp.concatenate([
-                jnp.where(even, high, zero).astype(bf16), jnp.where(even, zero, high).astype(bf16),
-                jnp.where(even, low, zero).astype(bf16), jnp.where(even, zero, low).astype(bf16),
-            ], axis=0))
-        rows = dot(chip_rows[...], jnp.concatenate(images, axis=1))
-        rows = rows[:WIN] + rows[WIN:]
-        products = []
-        for part in range(2):
-            high, low = halves(rows[:, part * WIN:(part + 1) * WIN])
-            both = dot(jnp.concatenate([high, low], axis=1), chip_lanes[...])
-            both = both[:, :2 * WIN] + both[:, 2 * WIN:]
-            same, cross = both[:, :WIN], both[:, WIN:]
-            own = spectra[first + part]
-            turned = pltpu.roll(own, HALF, 1)
-            same_c, same_s = same[:HALF], same[HALF:]
-            cross_c, cross_s = cross[:HALF], cross[HALF:]
-            own_c, own_s = own[:HALF], own[HALF:]
-            turned_c, turned_s = turned[:HALF], turned[HALF:]
+    raws = []
+    for part in range(group):
+        window = step * group + part
+        raw = sources[0][place[window]]
+        for index in range(1, len(sources)):
+            raw = jnp.where(choice[window] == index, sources[index][place[window]], raw)
+        raws.append(raw.astype(f32))
+    total = jnp.concatenate([jnp.sum(raw, axis=0, keepdims=True) for raw in raws], axis=0)
+    mean = jnp.sum(total, axis=1, keepdims=True) * (1.0 / (CHIP * CHIP))
+    raws = [raws[part] - mean[part:part + 1] for part in range(group)]
+    total = jnp.concatenate([jnp.sum(raw * raw, axis=0, keepdims=True) for raw in raws], axis=0)
+    power = jnp.sum(total, axis=1, keepdims=True) * (1.0 / (CHIP * CHIP))
+    gain = lax.rsqrt(power + epsilon) * (1.0 / CHIP)
+    for part in range(group):
+        own = slice(part * ROWS, (part + 1) * ROWS)
+        high, low = halves(raws[part])
+        lefts[own, :WIN] = high
+        lefts[own, WIN:2 * WIN] = low
+        lefts[own, 2 * WIN:] = high
+    lines[...] = dot(lefts[...], chip_lanes[...])
+
+    def chip_spectrum(part):
+        high, low = halves(lines[part * ROWS:(part + 1) * ROWS, :])
+        pieces = [high[:, :2 * WIN], high[:, 2 * WIN:], low[:, :2 * WIN], low[:, 2 * WIN:]]
+        pairs[part] = dot(chip_rows[...], jnp.concatenate(pieces + pieces[:2], axis=0))
+
+    def multiply(part):
+        lanes = slice(part % 2 * WIN, (part % 2 + 1) * WIN)
+        for row in range(0, HALF, 32):
+            upper, lower = slice(row, row + 32), slice(HALF + row, HALF + row + 32)
+            own_c, own_s = spectra[part, upper], spectra[part, lower]
+            turned_c, turned_s = pltpu.roll(own_c, HALF, 1), pltpu.roll(own_s, HALF, 1)
+            same_c, same_s = pairs[part, upper, :WIN], pairs[part, lower, :WIN]
+            cross_c, cross_s = pairs[part, upper, WIN:], pairs[part, lower, WIN:]
             out_c = same_c * own_c + cross_c * turned_c + same_s * own_s + cross_s * turned_s
             out_s = same_c * own_s + cross_c * turned_s - same_s * own_c - cross_s * turned_c
-            product = jnp.concatenate([out_c, out_s], axis=0)
-            products.append(jnp.concatenate(halves(product), axis=0))
-        back = dot(inverse_rows[...], jnp.concatenate(products, axis=1))
-        back = back[:OFF] + back[OFF:]
-        for part in range(2):
-            window = step * group + first + part
-            mine = back[:, part * WIN:(part + 1) * WIN]
-            packed = jnp.concatenate([mine[:ROWS], mine[ROWS:]], axis=1)
-            both = dot(jnp.concatenate(halves(packed), axis=1), inverse_lanes[...])
-            numerator = both[:, :WIN] + both[:, WIN:]
-            score = numerator * (scale[first + part] * gains[part])
-            size = jnp.abs(score)
-            largest = jnp.max(jnp.max(size, axis=0, keepdims=True), axis=1, keepdims=True)
-            power = jnp.ceil(jnp.log2(jnp.maximum(largest, 1e-30)))
-            root = jnp.sqrt(size * jnp.exp2(-power).astype(bf16).astype(f32))
-            code = jnp.minimum(jnp.round(root * CODE), CODE)
-            code = jnp.where(score < 0, -code, code).astype(jnp.int32).astype(jnp.int16)
-            to = target[window]
-            out[to, pl.ds(pl.multiple_of(ranks[window] * ROWS, ROWS), ROWS), :] = code
-            here = lane == position[0] * capacity + ranks[window]
-            named = (slots[window] + 1).astype(f32)
-            mark = jnp.where(line == 0, named, jnp.where(line == 1, power, 0.0))
-            marks[to] = marks[to] + jnp.where(here, mark, 0.0)
+            for value, place_to in ((out_c, row), (out_s, HALF + row)):
+                high, low = halves(value)
+                products[part // 2, place_to:place_to + 32, lanes] = high
+                products[part // 2, WIN + place_to:WIN + place_to + 32, lanes] = low
+
+    def invert(pair):
+        back = dot(inverse_rows[...], products[pair])
+        backs[pair] = back[:OFF] + back[OFF:]
+
+    def pack(pair):
+        for part in (2 * pair, 2 * pair + 1):
+            lanes = slice(part % 2 * WIN, (part % 2 + 1) * WIN)
+            own = slice(part * ROWS, (part + 1) * ROWS)
+            high, low = halves(backs[pair, :, lanes])
+            packs[own, :WIN] = high[:ROWS]
+            packs[own, WIN:2 * WIN] = high[ROWS:]
+            packs[own, 2 * WIN:3 * WIN] = low[:ROWS]
+            packs[own, 3 * WIN:] = low[ROWS:]
+
+    for part in range(group + 4):
+        if part < group:
+            chip_spectrum(part)
+        if 2 <= part < group + 2:
+            multiply(part - 2)
+            if part % 2 == 1:
+                invert((part - 2) // 2)
+        if part >= 4 and part % 2 == 1:
+            pack((part - 4) // 2)
+    both = dot(packs[...], inverse_lanes[...])
+    scores = []
+    for part in range(group):
+        own = slice(part * ROWS, (part + 1) * ROWS)
+        numerator = both[own, :WIN] + both[own, WIN:]
+        scores.append(numerator * (scale[part] * gain[part:part + 1]))
+    largest = jnp.concatenate([jnp.max(jnp.abs(score), axis=0, keepdims=True) for score in scores], axis=0)
+    largest = jnp.max(largest, axis=1, keepdims=True)
+    power = jnp.ceil(jnp.log2(jnp.maximum(largest, 1e-30)))
+    shrink = jnp.exp2(-power).astype(bf16).astype(f32)
+    for part in range(group):
+        window = step * group + part
+        score = scores[part]
+        size = jnp.maximum(jnp.abs(score) * shrink[part:part + 1], 1e-30)
+        root = size * lax.rsqrt(size) * CODE
+        root = jnp.minimum(root, CODE)
+        code = jnp.round(jnp.where(score < 0, -root, root)).astype(jnp.int32).astype(jnp.int16)
+        to = target[window]
+        out[to, pl.ds(pl.multiple_of(ranks[window] * ROWS, ROWS), ROWS), :] = code
+        here = lane == position[0] * capacity + ranks[window]
+        named = (slots[window] + 1).astype(f32)
+        mark = jnp.where(line == 0, named, jnp.where(line == 1, power[part:part + 1], 0.0))
+        marks[to] = marks[to] + jnp.where(here, mark, 0.0)
 
     @pl.when(step == pl.num_programs(0) - 1)
     def _():
@@ -256,34 +278,52 @@
     return pl.BlockSpec(array.shape, lambda *_: (0,) * array.ndim)
 
 
-def prepare_windows(windows, table):
-    amount = windows.shape[0]
+def window_parts(amount, parts):
+    groups = amount // min(GROUP, amount)
+    parts = max(1, min(parts, groups))
+    sizes = [groups // parts + (1 if i < groups % parts else 0) for i in range(parts)]
+    return [(sum(sizes[:i]), sizes[i]) for i in range(parts)]
+
+
+def continue_kernel(*refs):
+    window_kernel(*refs[:5], *refs[7:])
+
+
+def prepare_windows(images, table, start, count, previous):
+    amount = images.shape[0]
     group = min(GROUP, amount)
-    images = windows.reshape(amount, WIN, WIN)
     constants = [jnp.asarray(table[k]) for k in ("window_rows", "square_rows", "window_lanes", "band_lanes")]
+    kept = [] if previous is None else list(previous)
+    done = count * group
     return pl.pallas_call(
-        window_kernel,
-        grid=(amount // group,),
-        in_specs=[pl.BlockSpec((group, WIN, WIN), lambda i: (i, 0, 0))] + [whole(c) for c in constants],
+        window_kernel if previous is None else continue_kernel,
+        grid=(count,),
+        in_specs=[pl.BlockSpec((group, WIN, WIN), lambda i: (i + start, 0, 0))]
+        + [whole(c) for c in constants]
+        + [pl.BlockSpec(memory_space=pl.ANY) for _ in kept],
         out_specs=[
-            pl.BlockSpec((group, WIN, WIN), lambda i: (i, 0, 0)),
-            pl.BlockSpec((group, ROWS, WIN), lambda i: (i, 0, 0)),
+            pl.BlockSpec((group, WIN, WIN), lambda i: (i + start, 0, 0)),
+            pl.BlockSpec((group, ROWS, WIN), lambda i: (i + start, 0, 0)),
         ],
         out_shape=[
             jax.ShapeDtypeStruct((amount, WIN, WIN), f32),
             jax.ShapeDtypeStruct((amount, ROWS, WIN), f32),
         ],
+        input_output_aliases={5: 0, 6: 1} if kept else {},
+        cost_estimate=pl.CostEstimate(
+            flops=done * 2 * 900 * 65536, transcendentals=done * ROWS * WIN, bytes_accessed=done * 120000
+        ),
         name="window_spectra",
-    )(images, *constants)
-
-
-def score_windows(spectra, scale, sources, scalars, table, devices, capacity, chip_amount):
+    )(images, *constants, *kept)
+
+
+def score_windows(spectra, scale, sources, scalars, table, devices, capacity):
     amount = spectra.shape[0]
-    group = min(GROUP, amount)
-    constants = [jnp.asarray(table[k]) for k in ("chip_rows", "chip_lanes", "inverse_rows", "inverse_lanes")]
+    group = min(SCORE_GROUP, amount)
+    constants = [jnp.asarray(table[k]) for k in ("chip_lanes", "chip_rows", "inverse_rows", "inverse_lanes")]
     shape = (devices, capacity * ROWS + 16, WIN)
     return pl.pallas_call(
-        functools.partial(score_kernel, capacity, chip_amount),
+        functools.partial(score_kernel, capacity),
         grid_spec=pltpu.PrefetchScalarGridSpec(
             num_scalar_prefetch=len(scalars),
             grid=(amount // group,),
@@ -292,7 +332,15 @@
                 pl.BlockSpec((group, ROWS, WIN), lambda i, *_: (i, 0, 0)),
             ] + [whole(c) for c in constants] + [whole(s) for s in sources],
             out_specs=pl.BlockSpec(shape, lambda i, *_: (0, 0, 0)),
-            scratch_shapes=[pltpu.VMEM((devices, 8, WIN), f32)],
+            scratch_shapes=[
+                pltpu.VMEM((devices, 8, WIN), f32),
+                pltpu.VMEM((group * ROWS, 3 * WIN), bf16),
+                pltpu.VMEM((group * ROWS, 4 * WIN), f32),
+                pltpu.VMEM((group * ROWS, 4 * WIN), bf16),
+                pltpu.VMEM((group, WIN, 2 * WIN), f32),
+                pltpu.VMEM((group // 2, 2 * WIN, 2 * WIN), bf16),
+                pltpu.VMEM((group // 2, OFF, 2 * WIN), f32),
+            ],
         ),
         out_shape=jax.ShapeDtypeStruct(shape, jnp.int16),
         name="scores",
@@ -326,26 +374,60 @@
     devices = tiles * subs
     capacity = max(2, 2 * window_amount // devices)
 
-    images = chips.reshape(chip_amount, ROWS, WIN)
-    sent = jnp.broadcast_to(images[None], (tiles,) + images.shape)
-    gathered = lax.all_to_all(sent, "tile", split_axis=0, concat_axis=0, tiled=True)
-    gathered = gathered.reshape(tiles * chip_amount, ROWS, WIN)
-    sources = [gathered]
-    for shift in range(1, subs):
-        ring = [(i, (i - shift) % subs) for i in range(subs)]
-        sources.append(lax.ppermute(gathered, "sub", ring))
-
-    spectra, scale = prepare_windows(windows, table)
+    block = chips.reshape(chip_amount, ROWS, WIN)
+    images = windows.reshape(window_amount, WIN, WIN)
+    tile, sub = lax.axis_index("tile"), lax.axis_index("sub")
+    parts = window_parts(window_amount, tiles - 1)
+    prepared = None
+    others = [[] for _ in range(1, subs)]
+    own = []
+
+    def share(pieces):
+        own.extend(pieces)
+        joined = pieces[0] if len(pieces) == 1 else jnp.concatenate(pieces, axis=0)
+        for shift in range(1, subs):
+            ring = [(i, (i - shift) % subs) for i in range(subs)]
+            others[shift - 1].append(lax.ppermute(joined, "sub", ring))
+
+    right = left = block
+    fresh = [block]
+    for hop in range(1, tiles):
+        ahead = [(i, i + 1) for i in range(hop - 1, tiles - 1)]
+        behind = [(i + 1, i) for i in range(tiles - hop)]
+        if 2 * (hop - 1) >= tiles:
+            right = left = lax.ppermute(right, "tile", ahead + behind)
+            arrived = [right]
+        else:
+            right = lax.ppermute(right, "tile", ahead)
+            left = lax.ppermute(left, "tile", behind)
+            arrived = [right, left]
+            if 2 * hop >= tiles:
+                right = left = jnp.where(tile >= hop, right, left)
+                arrived = [right]
+        share(fresh)
+        if hop <= len(parts):
+            prepared = prepare_windows(images, table, *parts[hop - 1], prepared)
+        fresh = arrived
+    share(fresh)
+    if prepared is None:
+        prepared = prepare_windows(images, table, *parts[0], None)
+    spectra, scale = prepared
+    sources = [jnp.concatenate(own, axis=0)]
+    sources.extend(jnp.concatenate(pieces, axis=0) for pieces in others)
 
     order = jnp.arange(window_amount, dtype=jnp.int32)
     matches = targets[:, None] == targets[None, :]
     earlier = order[:, None] > order[None, :]
     ranks = jnp.sum((matches & earlier).astype(jnp.int32), axis=1)
-    choice = (targets % subs - lax.axis_index("sub")) % subs
-    place = (targets // subs) * chip_amount + slots
+    choice = (targets % subs - sub) % subs
+    apart = targets // subs - tile
+    far = jnp.abs(apart)
+    single = (tiles + 1) // 2
+    arrival = jnp.where(far < single, 2 * far - (apart < 0), far + single - 1)
+    place = jnp.maximum(arrival, 0) * chip_amount + slots
     position = jnp.full((1,), lax.axis_index(("tile", "sub")), jnp.int32)
     scalars = (choice, place, targets, ranks, slots, position)
-    codes = score_windows(spectra, scale, sources, scalars, table, devices, capacity, chip_amount)
+    codes = score_windows(spectra, scale, sources, scalars, table, devices, capacity)
 
     received = lax.all_to_all(codes, ("tile", "sub"), split_axis=0, concat_axis=0, tiled=True)
     smooth, first, last = average_scores(received, capacity, chip_amount)

time: 120 us -> 114 us (0.950)
  blocking collectives: 61.1 us -> 31 us
  waiting for transfers between devices: 3.59 us -> 21.6 us
  starting transfers between devices: 6.22 us -> 16.7 us
  Pallas kernels: 41.2 us -> 31.9 us
  local copies, waits for them, and re-layouts: 4.18 us -> 6.59 us
  other arithmetic: 3.19 us -> 5.5 us
    all_to_all x1 -> x0, blocking collectives: 30.1 us -> none  [on_device(): lax.all_to_all(sent, 'tile', split_axis=0, concat_axis=0, tiled=True)]
    ppermute x1 -> x9, waiting for transfers between devices: 0.01 us -> 18 us  [the longest x2 11.7 us: on_device(): left = lax.ppermute(left, 'tile', behind)]
    ppermute x1 -> x9, starting transfers between devices: 1.75 us -> 12.3 us  [the longest x2 4.7 us: on_device(): right = lax.ppermute(right, 'tile', ahead)]
    pallas_call x2 -> x4, Pallas kernels: 37.3 us -> 28 us  [the longest x3 14.8 us: prepare_windows(): pl.pallas_call(window_kernel if previous is None else continue_kernel, gr...]
    unnamed x10 -> x11, local copies, waits for them, and re-layouts: 3.06 us -> 4.63 us
    concatenate x0 -> x2, other arithmetic: none -> 1.51 us  [the longest x1 1.46 us: on_device(): sources.extend((jnp.concatenate(pieces, axis=0) for pieces in others))]
  transfers between devices with their start and end apart: 3 -> 11, of which waited for: 1 -> 3; matrix products, arithmetic and copies ran while one was open for 4% -> 7% of each run, Pallas kernels for 9% -> 13%
where the time goes in v2:
time: 114 us; the launch traced here: 113 us
  Pallas kernels  31.9 us (28%)
  blocking collectives  31 us (27%)
  waiting for transfers between devices  21.6 us (19%)
  starting transfers between devices  16.7 us (15%)
  local copies, waits for them, and re-layouts  6.59 us (6%)
  other arithmetic  5.5 us (5%)
    all_to_all x1, blocking collectives, on_device(): lax.all_to_all(codes, ('tile', 'sub'), split_axis=0, concat_axis=0, tiled...  31 us
    pallas_call x3, Pallas kernels, prepare_windows(): pl.pallas_call(window_kernel if previous is None else continue_kernel, gr...  14.8 us
    pallas_call x1, Pallas kernels, score_windows(): pl.pallas_call(functools.partial(score_kernel, capacity), grid_spec=pltpu...  13.2 us
    ppermute x2, waiting for transfers between devices, on_device(): left = lax.ppermute(left, 'tile', behind)  11.7 us
    ppermute x1, waiting for transfers between devices, on_device(): right = left = lax.ppermute(right, 'tile', ahead + behind)  6.27 us
    ppermute x2, starting transfers between devices, on_device(): right = lax.ppermute(right, 'tile', ahead)  4.7 us
    unnamed x11, local copies, waits for them, and re-layouts  4.63 us
    pallas_call x1, Pallas kernels, average_scores(): pl.pallas_call(functools.partial(average_kernel, capacity, chip_amount),...  3.87 us
  transfers between devices with their start and end apart: 11, of which 3 were waited for; matrix products, arithmetic and copies ran while one was open for 7% of the time, Pallas kernels for 13%

profile of v2, /device:TPU:1, one launch (start us, length us, event | category | flops | bytes accessed | tf_op | source)
XLA Modules:
  0.0 113.5 jit_solution(14018869703545717542)
XLA Ops:
  0.0 1.0 copy.18
  1.0 4.0 %collective-permute-start = (bf16[32,32,128]{2,1,0:T(8,128)(2,1)S(1)}, bf16[32,32,128]{2,1,0:T(8,128)(2,1)S(1)}, u32[]{:S(2)}, u32[]{:S(2)}) collective-permute-start(bf16[32,32,128]{2,1,0:T(8,128)(2,1)S(1)} %bitcast.22), channel_id=1, source_target_pairs={{0,4},{4,8},{8,12},{1,5},{5,9},{9,13},{2,6},{6,10},{10,14},{3,7},{... | collective-permute-start | bytes 786440 | tf_op jit(solution)/shard_map/ppermute | solution.py:401
  5.0 1.3 %collective-permute-start.1 = (bf16[32,32,128]{2,1,0:T(8,128)(2,1)S(1)}, bf16[32,32,128]{2,1,0:T(8,128)(2,1)S(1)}, u32[]{:S(2)}, u32[]{:S(2)}) collective-permute-start(bf16[32,32,128]{2,1,0:T(8,128)(2,1)S(1)} %bitcast.23), channel_id=1, source_target_pairs={{4,0},{8,4},{12,8},{5,1},{9,5},{13,9},{6,2},{10,6},{14,10},{7,3},{... | collective-permute-start | bytes 786440 | tf_op jit(solution)/shard_map/ppermute | solution.py:402
  6.3 1.0 collective-permute-start.5
  7.4 3.5 %copy.17 = bf16[8,8,128,128]{3,2,1,0:T(8,128)(2,1)} copy(bf16[8,8,128,128]{3,1,2,0:T(8,128)(2,1)} %bitcast.21) | data formatting | bytes 4194304
  10.9 5.3 %window_spectra.3 = (f32[64,128,128]{2,1,0:T(8,128)}, f32[64,32,128]{2,1,0:T(8,128)}) custom-call(bf16[64,128,128]{2,1,0:T(8,128)(2,1)} %bitcast.18, bf16[320,128]{1,0:T(8,128)(2,1)} %constant.66.clone.window_rows.refs_1_, bf16[64,256]{1,0:T(8,128)(2,1)} %constant.67.clone.square_rows.refs_2_, bf16[256,256]{1,0:T(8,128)(2,1)} %constant.68.clone.window_lanes.refs_3_, ...), custom_call_target="tpu_custom_call" | custom-call | flops 2831155200 | bytes 2880000 | tf_op jit(solution)/shard_map/window_spectra/pallas_call | solution.py:298
  16.2 5.3 %window_spectra.4 = (f32[64,128,128]{2,1,0:T(8,128)}, f32[64,32,128]{2,1,0:T(8,128)}) custom-call(bf16[64,128,128]{2,1,0:T(8,128)(2,1)} %bitcast.19, bf16[320,128]{1,0:T(8,128)(2,1)} %constant.66.clone.window_rows.refs_1_, bf16[64,256]{1,0:T(8,128)(2,1)} %constant.67.clone.square_rows.refs_2_, ...), custom_call_target="tpu_custom_call", output_to_operand_aliasing={{0}: (5, {}), {1}: (6, {})} | custom-call | flops 2831155200 | bytes 2880000 | tf_op jit(solution)/shard_map/window_spectra/pallas_call | solution.py:298
  22.2 1.3 %collective-permute-start.3 = (bf16[32,32,128]{2,1,0:T(8,128)(2,1)S(1)}, bf16[32,32,128]{2,1,0:T(8,128)(2,1)S(1)}, u32[]{:S(2)}, u32[]{:S(2)}) collective-permute-start(bf16[32,32,128]{2,1,0:T(8,128)(2,1)S(1)} %collective-permute-done.1), channel_id=1, source_target_pairs={{4,0},{8,4},{5,1},{9,5},{6,2},{10,6},{7,3},{11,7},{20,16},{24,20},... | collective-permute-start | bytes 786440 | tf_op jit(solution)/shard_map/ppermute | solution.py:402
  23.7 11.7 %collective-permute-done.3 = bf16[32,32,128]{2,1,0:T(8,128)(2,1)S(1)} collective-permute-done((bf16[32,32,128]{2,1,0:T(8,128)(2,1)S(1)}, bf16[32,32,128]{2,1,0:T(8,128)(2,1)S(1)}, u32[]{:S(2)}, u32[]{:S(2)}) %collective-permute-start.3) | collective-permute-done | bytes 262176 | tf_op jit(solution)/shard_map/ppermute | solution.py:402
  36.2 1.3 %collective-permute-start.4 = (bf16[32,32,128]{2,1,0:T(8,128)(2,1)}, bf16[32,32,128]{2,1,0:T(8,128)(2,1)}, u32[]{:S(2)}, u32[]{:S(2)}) collective-permute-start(bf16[32,32,128]{2,1,0:T(8,128)(2,1)} %get-tuple-element.24), channel_id=1, source_target_pairs={{8,12},{4,0},{9,13},{5,1},{10,14},{6,2},{11,15},{7,3},{24,28},{20,... | collective-permute-start | bytes 786440 | tf_op jit(solution)/shard_map/ppermute | solution.py:398
  37.6 0.9 collective-permute-start.6
  39.1 6.3 %collective-permute-done.4 = bf16[32,32,128]{2,1,0:T(8,128)(2,1)} collective-permute-done((bf16[32,32,128]{2,1,0:T(8,128)(2,1)}, bf16[32,32,128]{2,1,0:T(8,128)(2,1)}, u32[]{:S(2)}, u32[]{:S(2)}) %collective-permute-start.4) | collective-permute-done | bytes 262176 | tf_op jit(solution)/shard_map/ppermute | solution.py:398
  45.4 1.7 %collective-permute-start.8 = (bf16[32,32,128]{2,1,0:T(8,128)(2,1)}, bf16[32,32,128]{2,1,0:T(8,128)(2,1)S(1)}, u32[]{:S(2)}, u32[]{:S(2)}) collective-permute-start(bf16[32,32,128]{2,1,0:T(8,128)(2,1)} %collective-permute-done.4), channel_id=1, source_target_pairs={{0,1},{1,0},{2,3},{3,2},{4,5},{5,4},{6,7},{7,6},{8,9},{9,8},{10,11... | collective-permute-start | bytes 786440 | tf_op jit(solution)/shard_map/ppermute | solution.py:390
  47.1 4.2 %window_spectra.5 = (f32[64,128,128]{2,1,0:T(8,128)}, f32[64,32,128]{2,1,0:T(8,128)}) custom-call(bf16[64,128,128]{2,1,0:T(8,128)(2,1)} %bitcast.20, bf16[320,128]{1,0:T(8,128)(2,1)} %constant.66.clone.window_rows.refs_1_, bf16[64,256]{1,0:T(8,128)(2,1)} %constant.67.clone.square_rows.refs_2_, ...), custom_call_target="tpu_custom_call", output_to_operand_aliasing={{0}: (5, {}), {1}: (6, {})} | custom-call | flops 1887436800 | bytes 1920000 | tf_op jit(solution)/shard_map/window_spectra/pallas_call | solution.py:298
  52.0 1.0 constant_dynamic-update-slice_fusion.rest_0_
  53.1 1.5 %pad_maximum_fusion.rest_1_ = bf16[160,32,128]{2,1,0:T(8,128)(2,1)} fusion(bf16[32,32,128]{2,1,0:T(8,128)(2,1)S(1)} %collective-permute-done.8, bf16[32,32,128]{2,1,0:T(8,128)(2,1)S(1)} %collective-permute-done.7, bf16[64,32,128]{2,1,0:T(8,128)(2,1)S(1)} %collective-permute-done.6, bf16[32,32,128]{2,1,0:T(8,128)(2,1)S(1)} %collective-permute-done.5), kind=kLoop, calls=%fused_computation | loop fusion | flops 1966080 | bytes 2621440 | tf_op jit(solution)/shard_map/concatenate | solution.py:416
  54.5 13.2 %scores.1 = s16[8,528,128]{2,1,0:T(8,128)(2,1)} custom-call(s32[64]{0:T(128)} %get-tuple-element.28.choice, s32[64]{0:T(128)} %get-tuple-element.27.place, s32[64]{0:T(128)} %bitcast.28, s32[64]{0:T(128)} %convert_reduce_fusion.ranks, s32[64]{0:T(128)} %bitcast.27, s32[1]{0:T(128)} %bitcast.2.position, f32[64,128,128]{2,1,0:T(8,128)} %get-tuple-element.18.spectra, ...), custom_call_target="tpu_custom_call" | custom-call | tf_op jit(solution)/shard_map/scores/pallas_call | solution.py:325
  67.8 31.0 %all_to_all.5.codes = s16[8,528,128]{2,1,0:T(8,128)(2,1)} all-to-all(s16[8,528,128]{2,1,0:T(8,128)(2,1)} %scores.1), channel_id=1, replica_groups=mesh['groups'=2,'tile'=4,'pair'=2,'sub'=2] {'tile','sub'}, dimensions={0} | all-to-all | bytes 2162688 | tf_op jit(solution)/shard_map/all_to_all | solution.py:432
  98.7 3.9 %average.1 = (f32[32,4096]{1,0:T(8,128)}, f32[8,4096]{1,0:T(8,128)}, f32[8,4096]{1,0:T(8,128)}) custom-call(s16[8,528,128]{2,1,0:T(8,128)(2,1)} %all_to_all.5.codes), custom_call_target="tpu_custom_call" | custom-call | tf_op jit(solution)/shard_map/average/pallas_call | solution.py:352
  102.6 2.5 %collective-permute-start.9 = (f32[8,4096]{1,0:T(8,128)}, f32[8,4096]{1,0:T(8,128)S(1)}, u32[]{:S(2)}, u32[]{:S(2)}) collective-permute-start(f32[8,4096]{1,0:T(8,128)} %get-tuple-element.21), channel_id=1, source_target_pairs={{0,1},{1,4},{4,5},{5,8},{8,9},{9,12},{12,13},{2,3},{3,6},{6,7},{7,... | collective-permute-start | bytes 393224 | tf_op jit(solution)/shard_map/ppermute | solution.py:436
  105.1 1.9 %collective-permute-start.10 = (f32[8,4096]{1,0:T(8,128)}, f32[8,4096]{1,0:T(8,128)S(1)}, u32[]{:S(2)}, u32[]{:S(2)}) collective-permute-start(f32[8,4096]{1,0:T(8,128)} %get-tuple-element.22), channel_id=1, source_target_pairs={{1,0},{4,1},{5,4},{8,5},{9,8},{12,9},{13,12},{3,2},{6,3},{7,6},{10... | collective-permute-start | bytes 393224 | tf_op jit(solution)/shard_map/ppermute | solution.py:437
  107.1 1.0 slice.10
  108.1 3.6 %collective-permute-done.10 = f32[8,4096]{1,0:T(8,128)S(1)} collective-permute-done((f32[8,4096]{1,0:T(8,128)}, f32[8,4096]{1,0:T(8,128)S(1)}, u32[]{:S(2)}, u32[]{:S(2)}) %collective-permute-start.10) | collective-permute-done | bytes 131104 | tf_op jit(solution)/shard_map/ppermute | solution.py:437
  111.6 1.0 multiply_add_fusion.1
  (24 shorter events, 3.9 us)
Async XLA Ops:
  1.0 20.5 %collective-permute-start = (bf16[32,32,128]{2,1,0:T(8,128)(2,1)S(1)}, bf16[32,32,128]{2,1,0:T(8,128)(2,1)S(1)}, u32[]{:S(2)}, u32[]{:S(2)}) collective-permute-start(bf16[32,32,128]{2,1,0:T(8,128)(2,1)S(1)} %bitcast.22), channel_id=1, source_target_pairs={{0,4},{4,8},{8,12},{1,5},{5,9},{9,13},{2,6},{6,10},{10,14},{3,7},{... | collective-permute-start | bytes 786440 | tf_op jit(solution)/shard_map/ppermute | solution.py:401
  5.0 17.2 %collective-permute-start.1 = (bf16[32,32,128]{2,1,0:T(8,128)(2,1)S(1)}, bf16[32,32,128]{2,1,0:T(8,128)(2,1)S(1)}, u32[]{:S(2)}, u32[]{:S(2)}) collective-permute-start(bf16[32,32,128]{2,1,0:T(8,128)(2,1)S(1)} %bitcast.23), channel_id=1, source_target_pairs={{4,0},{8,4},{12,8},{5,1},{9,5},{13,9},{6,2},{10,6},{14,10},{7,3},{... | collective-permute-start | bytes 786440 | tf_op jit(solution)/shard_map/ppermute | solution.py:402
  6.3 46.7 %collective-permute-start.5 = (bf16[32,32,128]{2,1,0:T(8,128)(2,1)S(1)}, bf16[32,32,128]{2,1,0:T(8,128)(2,1)S(1)}, u32[]{:S(2)}, u32[]{:S(2)}) collective-permute-start(bf16[32,32,128]{2,1,0:T(8,128)(2,1)S(1)} %bitcast.24), channel_id=1, source_target_pairs={{0,1},{1,0},{2,3},{3,2},{4,5},{5,4},{6,7},{7,6},{8,9},{9,8},{10,11... | collective-permute-start | bytes 786440 | tf_op jit(solution)/shard_map/ppermute | solution.py:390
  21.5 2.1 %collective-permute-start.2 = (bf16[32,32,128]{2,1,0:T(8,128)(2,1)S(1)}, bf16[32,32,128]{2,1,0:T(8,128)(2,1)S(1)}, u32[]{:S(2)}, u32[]{:S(2)}) collective-permute-start(bf16[32,32,128]{2,1,0:T(8,128)(2,1)S(1)} %collective-permute-done), channel_id=1, source_target_pairs={{4,8},{8,12},{5,9},{9,13},{6,10},{10,14},{7,11},{11,15},{20,24},{2... | collective-permute-start | bytes 786440 | tf_op jit(solution)/shard_map/ppermute | solution.py:401
  22.2 13.2 %collective-permute-start.3 = (bf16[32,32,128]{2,1,0:T(8,128)(2,1)S(1)}, bf16[32,32,128]{2,1,0:T(8,128)(2,1)S(1)}, u32[]{:S(2)}, u32[]{:S(2)}) collective-permute-start(bf16[32,32,128]{2,1,0:T(8,128)(2,1)S(1)} %collective-permute-done.1), channel_id=1, source_target_pairs={{4,0},{8,4},{5,1},{9,5},{6,2},{10,6},{7,3},{11,7},{20,16},{24,20},... | collective-permute-start | bytes 786440 | tf_op jit(solution)/shard_map/ppermute | solution.py:402
  23.6 14.9 %copy-start.1 = (s32[1,64]{1,0:T(1,128)S(1)}, s32[1,64]{1,0:T(1,128)}, u32[]{:S(2)}) copy-start(s32[1,64]{1,0:T(1,128)} %param.15) | copy-start | bytes 772
  23.6 14.9 %copy-start.2 = (s32[1,64,1]{1,2,0:T(1,128)S(1)}, s32[1,64,1]{1,2,0:T(1,128)}, u32[]{:S(2)}) copy-start(s32[1,64,1]{1,2,0:T(1,128)} %param.14) | copy-start | bytes 772
  36.2 9.2 %collective-permute-start.4 = (bf16[32,32,128]{2,1,0:T(8,128)(2,1)}, bf16[32,32,128]{2,1,0:T(8,128)(2,1)}, u32[]{:S(2)}, u32[]{:S(2)}) collective-permute-start(bf16[32,32,128]{2,1,0:T(8,128)(2,1)} %get-tuple-element.24), channel_id=1, source_target_pairs={{8,12},{4,0},{9,13},{5,1},{10,14},{6,2},{11,15},{7,3},{24,28},{20,... | collective-permute-start | bytes 786440 | tf_op jit(solution)/shard_map/ppermute | solution.py:398
  37.6 15.5 %collective-permute-start.6 = (bf16[64,32,128]{2,1,0:T(8,128)(2,1)S(1)}, bf16[64,32,128]{2,1,0:T(8,128)(2,1)S(1)}, u32[]{:S(2)}, u32[]{:S(2)}) collective-permute-start(bf16[64,32,128]{2,1,0:T(8,128)(2,1)S(1)} %pad_maximum_fusion.1), channel_id=1, source_target_pairs={{0,1},{1,0},{2,3},{3,2},{4,5},{5,4},{6,7},{7,6},{8,9},{9,8},{10,11... | collective-permute-start | bytes 1572872 | tf_op jit(solution)/shard_map/ppermute | solution.py:390
  39.1 13.9 %collective-permute-start.7 = (bf16[32,32,128]{2,1,0:T(8,128)(2,1)}, bf16[32,32,128]{2,1,0:T(8,128)(2,1)S(1)}, u32[]{:S(2)}, u32[]{:S(2)}) collective-permute-start(bf16[32,32,128]{2,1,0:T(8,128)(2,1)} %get-tuple-element.24), channel_id=1, source_target_pairs={{0,1},{1,0},{2,3},{3,2},{4,5},{5,4},{6,7},{7,6},{8,9},{9,8},{10,11... | collective-permute-start | bytes 786440 | tf_op jit(solution)/shard_map/ppermute | solution.py:390
  45.4 7.7 %collective-permute-start.8 = (bf16[32,32,128]{2,1,0:T(8,128)(2,1)}, bf16[32,32,128]{2,1,0:T(8,128)(2,1)S(1)}, u32[]{:S(2)}, u32[]{:S(2)}) collective-permute-start(bf16[32,32,128]{2,1,0:T(8,128)(2,1)} %collective-permute-done.4), channel_id=1, source_target_pairs={{0,1},{1,0},{2,3},{3,2},{4,5},{5,4},{6,7},{7,6},{8,9},{9,8},{10,11... | collective-permute-start | bytes 786440 | tf_op jit(solution)/shard_map/ppermute | solution.py:390
  53.0 1.5 %copy-start = (bf16[160,32,128]{2,1,0:T(8,128)(2,1)}, bf16[160,32,128]{2,1,0:T(8,128)(2,1)S(1)}, u32[]{:S(2)}) copy-start(bf16[160,32,128]{2,1,0:T(8,128)(2,1)S(1)} %constant_dynamic-update-slice_fusion.rest_0_) | copy-start | bytes 3932164
  102.6 5.5 %collective-permute-start.9 = (f32[8,4096]{1,0:T(8,128)}, f32[8,4096]{1,0:T(8,128)S(1)}, u32[]{:S(2)}, u32[]{:S(2)}) collective-permute-start(f32[8,4096]{1,0:T(8,128)} %get-tuple-element.21), channel_id=1, source_target_pairs={{0,1},{1,4},{4,5},{5,8},{8,9},{9,12},{12,13},{2,3},{3,6},{6,7},{7,... | collective-permute-start | bytes 393224 | tf_op jit(solution)/shard_map/ppermute | solution.py:436
  105.1 6.5 %collective-permute-start.10 = (f32[8,4096]{1,0:T(8,128)}, f32[8,4096]{1,0:T(8,128)S(1)}, u32[]{:S(2)}, u32[]{:S(2)}) collective-permute-start(f32[8,4096]{1,0:T(8,128)} %get-tuple-element.22), channel_id=1, source_target_pairs={{1,0},{4,1},{5,4},{8,5},{9,8},{12,9},{13,12},{3,2},{6,3},{7,6},{10... | collective-permute-start | bytes 393224 | tf_op jit(solution)/shard_map/ppermute | solution.py:437

commit v3 on v2

--- a/solution.py
+++ b/solution.py
@@ -18,6 +18,7 @@
 ROWS = OFF * OFF // WIN
 GROUP = 8
 SCORE_GROUP = 16
+VMEM_GRANT = 24 * 1024 * 1024
 CODE = 32767.0
 epsilon = 1e-06
 f32 = jnp.float32
@@ -104,6 +105,7 @@
 
 def window_kernel(windows, window_rows, square_rows, window_lanes, band_lanes, spectra, scale):
     group = windows.shape[0]
+    base = pl.program_id(0) * group
     for first in range(0, group, 2):
         image = jnp.concatenate([windows[first], windows[first + 1]], axis=1)
         rows = dot(window_rows[...], image)
@@ -116,7 +118,7 @@
             lanes = slice(part * WIN, (part + 1) * WIN)
             high, low = halves(spec_rows[:, lanes])
             both = dot(jnp.concatenate([high, low], axis=1), window_lanes[...])
-            spectra[first + part] = both[:, :WIN] + both[:, WIN:]
+            spectra[base + first + part] = both[:, :WIN] + both[:, WIN:]
             pieces = []
             for source in (sums, squares):
                 own = source[:, lanes]
@@ -127,7 +129,7 @@
             mean = (boxes[0] + boxes[1] + boxes[2]) * (1.0 / (CHIP * CHIP))
             second = (boxes[3] + boxes[4] + boxes[5]) * (1.0 / (CHIP * CHIP))
             variance = second - mean * mean
-            scale[first + part] = lax.rsqrt(variance + epsilon)
+            scale[base + first + part] = lax.rsqrt(variance + epsilon)
 
 
 def score_kernel(
@@ -136,7 +138,8 @@
 ):
     *sources, out, marks, lefts, lines, packs, pairs, products, backs = rest
     step = pl.program_id(0)
-    group = spectra.shape[0]
+    group = lefts.shape[0] // ROWS
+    base = step * group
     body = capacity * ROWS
     lane = lax.broadcasted_iota(jnp.int32, (8, WIN), 1)
     line = lax.broadcasted_iota(jnp.int32, (8, WIN), 0)
@@ -148,7 +151,7 @@
 
     raws = []
     for part in range(group):
-        window = step * group + part
+        window = base + part
         raw = sources[0][place[window]]
         for index in range(1, len(sources)):
             raw = jnp.where(choice[window] == index, sources[index][place[window]], raw)
@@ -176,7 +179,7 @@
         lanes = slice(part % 2 * WIN, (part % 2 + 1) * WIN)
         for row in range(0, HALF, 32):
             upper, lower = slice(row, row + 32), slice(HALF + row, HALF + row + 32)
-            own_c, own_s = spectra[part, upper], spectra[part, lower]
+            own_c, own_s = spectra[base + part, upper], spectra[base + part, lower]
             turned_c, turned_s = pltpu.roll(own_c, HALF, 1), pltpu.roll(own_s, HALF, 1)
             same_c, same_s = pairs[part, upper, :WIN], pairs[part, lower, :WIN]
             cross_c, cross_s = pairs[part, upper, WIN:], pairs[part, lower, WIN:]
@@ -215,13 +218,13 @@
     for part in range(group):
         own = slice(part * ROWS, (part + 1) * ROWS)
         numerator = both[own, :WIN] + both[own, WIN:]
-        scores.append(numerator * (scale[part] * gain[part:part + 1]))
+        scores.append(numerator * (scale[base + part] * gain[part:part + 1]))
     largest = jnp.concatenate([jnp.max(jnp.abs(score), axis=0, keepdims=True) for score in scores], axis=0)
     largest = jnp.max(largest, axis=1, keepdims=True)
     power = jnp.ceil(jnp.log2(jnp.maximum(largest, 1e-30)))
     shrink = jnp.exp2(-power).astype(bf16).astype(f32)
     for part in range(group):
-        window = step * group + part
+        window = base + part
         score = scores[part]
         size = jnp.maximum(jnp.abs(score) * shrink[part:part + 1], 1e-30)
         root = size * lax.rsqrt(size) * CODE
@@ -251,7 +254,8 @@
         notes = notes + codes[source, body:, :].astype(jnp.int32).astype(f32)
     for source in range(devices):
         wide = codes[source, :body, :].astype(jnp.int32).astype(f32)
-        values[source * body:(source + 1) * body, :] = wide * jnp.abs(wide)
+        turned = jnp.swapaxes((wide * jnp.abs(wide)).reshape(capacity, ROWS, WIN), 0, 1)
+        values[:, source * capacity:(source + 1) * capacity, :] = turned
     chip = lax.broadcasted_iota(jnp.int32, (chip_amount, WIN), 0)
     hit = (notes[0:1] - 1.0).astype(jnp.int32) == chip
     looks = jnp.sum(hit.astype(f32), axis=1, keepdims=True)
@@ -262,7 +266,7 @@
     column = chip % GC
     zero = jnp.zeros((GC, WIN), f32)
     for row in range(ROWS):
-        high, low = halves(values[pl.ds(row, slots, stride=ROWS), :])
+        high, low = halves(values[row])
         average = dot(weight, jnp.concatenate([high, low], axis=0)) * factor
         lanes = slice(row * WIN, (row + 1) * WIN)
         first[:, lanes] = average[:GC]
@@ -274,47 +278,33 @@
         smooth[:, lanes] = (4.0 * average + above + below + left + right) * 0.125
 
 
-def whole(array):
-    return pl.BlockSpec(array.shape, lambda *_: (0,) * array.ndim)
-
-
-def window_parts(amount, parts):
-    groups = amount // min(GROUP, amount)
-    parts = max(1, min(parts, groups))
-    sizes = [groups // parts + (1 if i < groups % parts else 0) for i in range(parts)]
-    return [(sum(sizes[:i]), sizes[i]) for i in range(parts)]
-
-
-def continue_kernel(*refs):
-    window_kernel(*refs[:5], *refs[7:])
-
-
-def prepare_windows(images, table, start, count, previous):
+def resident():
+    return pl.BlockSpec(memory_space=pltpu.VMEM)
+
+
+def near(array):
+    return pltpu.with_memory_space_constraint(array, pltpu.VMEM)
+
+
+def prepare_windows(images, table):
     amount = images.shape[0]
     group = min(GROUP, amount)
     constants = [jnp.asarray(table[k]) for k in ("window_rows", "square_rows", "window_lanes", "band_lanes")]
-    kept = [] if previous is None else list(previous)
-    done = count * group
     return pl.pallas_call(
-        window_kernel if previous is None else continue_kernel,
-        grid=(count,),
-        in_specs=[pl.BlockSpec((group, WIN, WIN), lambda i: (i + start, 0, 0))]
-        + [whole(c) for c in constants]
-        + [pl.BlockSpec(memory_space=pl.ANY) for _ in kept],
-        out_specs=[
-            pl.BlockSpec((group, WIN, WIN), lambda i: (i + start, 0, 0)),
-            pl.BlockSpec((group, ROWS, WIN), lambda i: (i + start, 0, 0)),
+        window_kernel,
+        grid=(amount // group,),
+        in_specs=[pl.BlockSpec((group, WIN, WIN), lambda i: (i, 0, 0))] + [resident() for _ in constants],
+        out_specs=[resident(), resident()],
+        out_shape=[
+            pltpu.VMEM((amount, WIN, WIN), f32),
+            pltpu.VMEM((amount, ROWS, WIN), f32),
         ],
-        out_shape=[
-            jax.ShapeDtypeStruct((amount, WIN, WIN), f32),
-            jax.ShapeDtypeStruct((amount, ROWS, WIN), f32),
-        ],
-        input_output_aliases={5: 0, 6: 1} if kept else {},
         cost_estimate=pl.CostEstimate(
-            flops=done * 2 * 900 * 65536, transcendentals=done * ROWS * WIN, bytes_accessed=done * 120000
+            flops=amount * 2 * 900 * 65536, transcendentals=amount * ROWS * WIN, bytes_accessed=amount * 120000
         ),
+        compiler_params=pltpu.CompilerParams(vmem_limit_bytes=VMEM_GRANT),
         name="window_spectra",
-    )(images, *constants, *kept)
+    )(images, *constants)
 
 
 def score_windows(spectra, scale, sources, scalars, table, devices, capacity):
@@ -328,10 +318,9 @@
             num_scalar_prefetch=len(scalars),
             grid=(amount // group,),
             in_specs=[
-                pl.BlockSpec((group, WIN, WIN), lambda i, *_: (i, 0, 0)),
-                pl.BlockSpec((group, ROWS, WIN), lambda i, *_: (i, 0, 0)),
-            ] + [whole(c) for c in constants] + [whole(s) for s in sources],
-            out_specs=pl.BlockSpec(shape, lambda i, *_: (0, 0, 0)),
+                resident(), resident(),
+            ] + [resident() for _ in constants] + [resident() for _ in sources],
+            out_specs=resident(),
             scratch_shapes=[
                 pltpu.VMEM((devices, 8, WIN), f32),
                 pltpu.VMEM((group * ROWS, 3 * WIN), bf16),
@@ -342,23 +331,48 @@
                 pltpu.VMEM((group // 2, OFF, 2 * WIN), f32),
             ],
         ),
-        out_shape=jax.ShapeDtypeStruct(shape, jnp.int16),
+        out_shape=pltpu.VMEM(shape, jnp.int16),
+        compiler_params=pltpu.CompilerParams(vmem_limit_bytes=VMEM_GRANT),
         name="scores",
-    )(*scalars, spectra, scale, *constants, *sources)
+    )(*scalars, near(spectra), near(scale), *constants, *[near(source) for source in sources])
 
 
 def average_scores(codes, capacity, chip_amount):
     devices = codes.shape[0]
     return pl.pallas_call(
         functools.partial(average_kernel, capacity, chip_amount),
+        in_specs=[resident()],
+        out_specs=[resident(), resident(), resident()],
         out_shape=[
-            jax.ShapeDtypeStruct((chip_amount, OFF * OFF), f32),
-            jax.ShapeDtypeStruct((GC, OFF * OFF), f32),
-            jax.ShapeDtypeStruct((GC, OFF * OFF), f32),
+            pltpu.VMEM((chip_amount, OFF * OFF), f32),
+            pltpu.VMEM((GC, OFF * OFF), f32),
+            pltpu.VMEM((GC, OFF * OFF), f32),
         ],
-        scratch_shapes=[pltpu.VMEM((devices * capacity * ROWS, WIN), f32)],
+        scratch_shapes=[pltpu.VMEM((ROWS, devices * capacity, WIN), f32)],
+        compiler_params=pltpu.CompilerParams(vmem_limit_bytes=VMEM_GRANT),
         name="average",
-    )(codes)
+    )(near(codes))
+
+
+def finish_kernel(turn, smooth, inner, outer, result):
+    edge = smooth.shape[0] - GC
+    result[...] = smooth[...]
+    for row in range(ROWS):
+        lanes = slice(row * WIN, (row + 1) * WIN)
+        near, far = inner[:, lanes], outer[:, lanes]
+        swap = turn[0] == 1
+        result[:GC, lanes] = smooth[:GC, lanes] + jnp.where(swap, near, far) * 0.125
+        result[edge:, lanes] = smooth[edge:, lanes] + jnp.where(swap, far, near) * 0.125
+
+
+def finish(smooth, inner, outer, turn):
+    return pl.pallas_call(
+        finish_kernel,
+        in_specs=[pl.BlockSpec(memory_space=pltpu.SMEM), resident(), resident(), resident()],
+        out_shape=jax.ShapeDtypeStruct(smooth.shape, f32),
+        compiler_params=pltpu.CompilerParams(vmem_limit_bytes=VMEM_GRANT),
+        name="finish",
+    )(jnp.full((1,), turn, jnp.int32), smooth, near(inner), near(outer))
 
 
 def on_device(ref_chips, search_windows, dest_block, dest_slot):
@@ -376,69 +390,39 @@
 
     block = chips.reshape(chip_amount, ROWS, WIN)
     images = windows.reshape(window_amount, WIN, WIN)
-    tile, sub = lax.axis_index("tile"), lax.axis_index("sub")
-    parts = window_parts(window_amount, tiles - 1)
-    prepared = None
-    others = [[] for _ in range(1, subs)]
-    own = []
-
-    def share(pieces):
-        own.extend(pieces)
-        joined = pieces[0] if len(pieces) == 1 else jnp.concatenate(pieces, axis=0)
-        for shift in range(1, subs):
-            ring = [(i, (i - shift) % subs) for i in range(subs)]
-            others[shift - 1].append(lax.ppermute(joined, "sub", ring))
-
-    right = left = block
-    fresh = [block]
-    for hop in range(1, tiles):
-        ahead = [(i, i + 1) for i in range(hop - 1, tiles - 1)]
-        behind = [(i + 1, i) for i in range(tiles - hop)]
-        if 2 * (hop - 1) >= tiles:
-            right = left = lax.ppermute(right, "tile", ahead + behind)
-            arrived = [right]
-        else:
-            right = lax.ppermute(right, "tile", ahead)
-            left = lax.ppermute(left, "tile", behind)
-            arrived = [right, left]
-            if 2 * hop >= tiles:
-                right = left = jnp.where(tile >= hop, right, left)
-                arrived = [right]
-        share(fresh)
-        if hop <= len(parts):
-            prepared = prepare_windows(images, table, *parts[hop - 1], prepared)
-        fresh = arrived
-    share(fresh)
-    if prepared is None:
-        prepared = prepare_windows(images, table, *parts[0], None)
-    spectra, scale = prepared
-    sources = [jnp.concatenate(own, axis=0)]
-    sources.extend(jnp.concatenate(pieces, axis=0) for pieces in others)
+    sub = lax.axis_index("sub")
+    sent = jnp.broadcast_to(block.reshape(1, chip_amount * ROWS, WIN), (tiles, chip_amount * ROWS, WIN))
+    gathered = lax.all_to_all(sent, "tile", split_axis=0, concat_axis=0, tiled=True)
+    gathered = gathered.reshape(tiles * chip_amount, ROWS, WIN)
+    spectra, scale = prepare_windows(images, table)
+    sources = [gathered]
+    for shift in range(1, subs):
+        ring = [(i, (i - shift) % subs) for i in range(subs)]
+        sources.append(lax.ppermute(gathered, "sub", ring))
 
     order = jnp.arange(window_amount, dtype=jnp.int32)
     matches = targets[:, None] == targets[None, :]
     earlier = order[:, None] > order[None, :]
     ranks = jnp.sum((matches & earlier).astype(jnp.int32), axis=1)
     choice = (targets % subs - sub) % subs
-    apart = targets // subs - tile
-    far = jnp.abs(apart)
-    single = (tiles + 1) // 2
-    arrival = jnp.where(far < single, 2 * far - (apart < 0), far + single - 1)
-    place = jnp.maximum(arrival, 0) * chip_amount + slots
+    place = (targets // subs) * chip_amount + slots
     position = jnp.full((1,), lax.axis_index(("tile", "sub")), jnp.int32)
     scalars = (choice, place, targets, ranks, slots, position)
     codes = score_windows(spectra, scale, sources, scalars, table, devices, capacity)
 
     received = lax.all_to_all(codes, ("tile", "sub"), split_axis=0, concat_axis=0, tiled=True)
     smooth, first, last = average_scores(received, capacity, chip_amount)
-    forward = [(i, i + 1) for i in range(devices - 1)]
-    backward = [(i + 1, i) for i in range(devices - 1)]
-    above = lax.ppermute(last, ("tile", "sub"), forward)
-    below = lax.ppermute(first, ("tile", "sub"), backward)
-    top = smooth[:GC] + above * 0.125
-    bottom = smooth[chip_amount - GC:] + below * 0.125
-    result = jnp.concatenate([top, smooth[GC:chip_amount - GC], bottom], axis=0)
-    return result[None]
+    if subs == 2:
+        inner = lax.ppermute(jnp.where(sub == 0, last, first), "sub", [(0, 1), (1, 0)])
+        ups = [(2 * i + 1, 2 * i + 2) for i in range(tiles - 1)]
+        downs = [(2 * i + 2, 2 * i + 1) for i in range(tiles - 1)]
+        outer = lax.ppermute(jnp.where(sub == 0, first, last), ("tile", "sub"), ups + downs)
+        turn = sub
+    else:
+        inner = lax.ppermute(first, ("tile", "sub"), [(i + 1, i) for i in range(devices - 1)])
+        outer = lax.ppermute(last, ("tile", "sub"), [(i, i + 1) for i in range(devices - 1)])
+        turn = 0
+    return finish(smooth, inner, outer, turn)[None]
 
 
 def solution(mesh):

time: 114 us -> 96.5 us (0.85)
  waiting for transfers between devices: 21.6 us -> 30.7 us
  Pallas kernels: 31.9 us -> 23.3 us
  starting transfers between devices: 16.7 us -> 8.2 us
  other arithmetic: 5.5 us -> 0.22 us
  local copies, waits for them, and re-layouts: 6.59 us -> 3.5 us
    all_to_all x0 -> x1, waiting for transfers between devices: none -> 26.3 us  [on_device(): lax.all_to_all(codes, ('tile', 'sub'), split_axis=0, concat_axis=0, tiled...]
    ppermute x11 -> x3, waiting for transfers between devices: 21.6 us -> 4.35 us  [the longest x1 4.35 us: on_device(): lax.ppermute(jnp.where(sub == 0, first, last), ('tile', 'sub'), ups + downs)]
    ppermute x11 -> x3, starting transfers between devices: 16.7 us -> 4.69 us  [the longest x1 1.91 us: on_device(): lax.ppermute(jnp.where(sub == 0, first, last), ('tile', 'sub'), ups + downs)]
    pallas_call x3 -> x2, Pallas kernels: 14.8 us -> 9.96 us  [the longest x1 9.12 us: prepare_windows(): pl.pallas_call(window_kernel, grid=(amount // group,), in_specs=[pl.Block...]
    all_to_all x0 -> x1, starting transfers between devices: none -> 3.51 us  [on_device(): lax.all_to_all(codes, ('tile', 'sub'), split_axis=0, concat_axis=0, tiled...]
    pallas_call x1, Pallas kernels: 3.87 us -> 1.29 us  [average_scores(): pl.pallas_call(functools.partial(average_kernel, capacity, chip_amount),...]
    unnamed x11 -> x21, local copies, waits for them, and re-layouts: 4.63 us -> 2.29 us
    add x2 -> x1, other arithmetic: 1.61 us -> 0.02 us  [on_device(): place = targets // subs * chip_amount + slots]
  transfers between devices with their start and end apart: 11 -> 4, of which waited for: 3 -> 2; matrix products, arithmetic and copies ran while one was open for 7% -> 3% of each run, Pallas kernels for 13% -> 9%
where the time goes in v3:
time: 96.5 us; the launch traced here: 96.2 us
  waiting for transfers between devices  30.7 us (32%)
  blocking collectives  30.1 us (31%)
  Pallas kernels  23.3 us (24%)
  starting transfers between devices  8.2 us (8%)
  local copies, waits for them, and re-layouts  3.5 us (4%)
    all_to_all x1, blocking collectives, on_device(): lax.all_to_all(sent, 'tile', split_axis=0, concat_axis=0, tiled=True)  30.1 us
    all_to_all x1, waiting for transfers between devices, on_device(): lax.all_to_all(codes, ('tile', 'sub'), split_axis=0, concat_axis=0, tiled...  26.3 us
    pallas_call x1, Pallas kernels, score_windows(): pl.pallas_call(functools.partial(score_kernel, capacity), grid_spec=pltpu...  12 us
    pallas_call x1, Pallas kernels, prepare_windows(): pl.pallas_call(window_kernel, grid=(amount // group,), in_specs=[pl.Block...  9.12 us
    ppermute x1, waiting for transfers between devices, on_device(): lax.ppermute(jnp.where(sub == 0, first, last), ('tile', 'sub'), ups + downs)  4.35 us
    all_to_all x1, starting transfers between devices, on_device(): lax.all_to_all(codes, ('tile', 'sub'), split_axis=0, concat_axis=0, tiled...  3.51 us
    unnamed x21, local copies, waits for them, and re-layouts  2.29 us
  transfers between devices with their start and end apart: 4, of which 2 were waited for; matrix products, arithmetic and copies ran while one was open for 3% of the time, Pallas kernels for 9%

profile of v3, /device:TPU:1, one launch (start us, length us, event | category | flops | bytes accessed | tf_op | source)
XLA Modules:
  0.0 96.2 jit_solution(13600735448301401004)
XLA Ops:
  0.0 1.1 %broadcast_in_dim.20 = bf16[1024,128]{1,0:T(8,128)(2,1)S(1)} reshape(bf16[1,32,4096]{2,1,0:T(8,128)(2,1)} %param.12) | data formatting | bytes 524288 | tf_op jit(solution)/shard_map/broadcast_in_dim | solution.py:394
  1.1 0.1 broadcast_in_dim.21
  1.2 30.1 %all_to_all.10 = bf16[4,1024,128]{2,1,0:T(8,128)(2,1)S(1)} all-to-all(bf16[4,1024,128]{2,1,0:T(8,128)(2,1)S(1)} %broadcast_in_dim.21), channel_id=1, replica_groups=mesh['groups'=2,'tile'=4,'pair'=2,'sub'=2] {'tile'}, dimensions={0} | all-to-all | bytes 2097152 | tf_op jit(solution)/shard_map/all_to_all | solution.py:395
  31.4 1.8 %collective-permute-start = (bf16[128,32,128]{2,1,0:T(8,128)(2,1)S(1)}, bf16[128,32,128]{2,1,0:T(8,128)(2,1)}, u32[]{:S(2)}, u32[]{:S(2)}) collective-permute-start(bf16[128,32,128]{2,1,0:T(8,128)(2,1)S(1)} %bitcast.16), channel_id=1, source_target_pairs={{0,1},{1,0},{2,3},{3,2},{4,5},{5,4},{6,7},{7,6},{8,9},{9,8},{10,11... | collective-permute-start | bytes 3145736 | tf_op jit(solution)/shard_map/ppermute | solution.py:401
  33.1 0.0 copy-start.8
  33.1 0.0 copy-start.9
  33.1 2.2 %copy.13 = bf16[8,8,128,128]{3,2,1,0:T(8,128)(2,1)S(1)} copy(bf16[8,8,128,128]{3,1,2,0:T(8,128)(2,1)} %bitcast.22) | data formatting | bytes 4194304
  35.4 0.2 convert_reduce_fusion.ranks
  35.6 0.0 copy-done.6
  35.7 0.0 copy-start
  35.7 0.0 copy-start.1
  35.7 0.0 copy-start.2
  35.7 0.0 copy-start.3
  35.7 9.1 %window_spectra.1 = (f32[64,128,128]{2,1,0:T(8,128)S(1)}, f32[64,32,128]{2,1,0:T(8,128)S(1)}) custom-call(bf16[64,128,128]{2,1,0:T(8,128)(2,1)S(1)} %bitcast.18, bf16[320,128]{1,0:T(8,128)(2,1)S(1)} %copy-done.7, bf16[64,256]{1,0:T(8,128)(2,1)S(1)} %copy-done.9, bf16[256,256]{1,0:T(8,128)(2,1)S(1)} %copy-done.6, bf16[256,128]{1,0:T(8,128)(2,1)S(1)} %copy-done.8), custom_call_target="tpu_custom_call" | custom-call | flops 7549747200 | bytes 7680000 | tf_op jit(solution)/shard_map/window_spectra/pallas_call | solution.py:293
  44.8 0.0 collective-permute-done.rest_1_
  44.9 12.0 %scores.1 = s16[8,528,128]{2,1,0:T(8,128)(2,1)} custom-call(s32[64]{0:T(128)S(1)} %get-tuple-element.18.choice, s32[64]{0:T(128)S(1)} %get-tuple-element.17.place, s32[64]{0:T(128)S(1)} %bitcast.21, s32[64]{0:T(128)S(1)} %convert_reduce_fusion.ranks, s32[64]{0:T(128)S(1)} %bitcast.19, s32[1]{0:T(128)} %bitcast.3.position, ...), custom_call_target="tpu_custom_call" | custom-call | tf_op jit(solution)/shard_map/scores/pallas_call | solution.py:315
  56.9 3.5 %all-to-all-start.1 = ((s16[8,528,128]{2,1,0:T(8,128)(2,1)}), s16[8,528,128]{2,1,0:T(8,128)(2,1)S(1)}, u32[]{:S(2)}, u32[]{:S(2)}) async-start(s16[8,528,128]{2,1,0:T(8,128)(2,1)} %scores.1), calls=%async_computation.1 | async-start | bytes 2162688 | tf_op jit(solution)/shard_map/all_to_all | solution.py:413
  60.5 26.3 %all-to-all-done.1.codes = s16[8,528,128]{2,1,0:T(8,128)(2,1)S(1)} async-done(((s16[8,528,128]{2,1,0:T(8,128)(2,1)}), s16[8,528,128]{2,1,0:T(8,128)(2,1)S(1)}, u32[]{:S(2)}, u32[]{:S(2)}) %all-to-all-start.1) | async-done | bytes 1081376 | tf_op jit(solution)/shard_map/all_to_all | solution.py:413
  86.8 1.3 %average.1 = (f32[32,4096]{1,0:T(8,128)S(1)}, f32[8,4096]{1,0:T(8,128)S(1)}, f32[8,4096]{1,0:T(8,128)S(1)}) custom-call(s16[8,528,128]{2,1,0:T(8,128)(2,1)S(1)} %all-to-all-done.1.codes), custom_call_target="tpu_custom_call" | custom-call | tf_op jit(solution)/shard_map/average/pallas_call | solution.py:342
  88.1 1.0 %collective-permute-start.1 = (f32[8,4096]{1,0:T(8,128)S(1)}, f32[8,4096]{1,0:T(8,128)S(1)}, u32[]{:S(2)}, u32[]{:S(2)}) collective-permute-start(f32[8,4096]{1,0:T(8,128)S(1)} %get-tuple-element.16), channel_id=1, source_target_pairs={{0,1},{1,0},{2,3},{3,2},{4,5},{5,4},{6,7},{7,6},{8,9},{9,8},{10,11... | collective-permute-start | bytes 393224 | tf_op jit(solution)/shard_map/ppermute | solution.py:416
  89.1 1.9 %collective-permute-start.2 = (f32[8,4096]{1,0:T(8,128)S(1)}, f32[8,4096]{1,0:T(8,128)S(1)}, u32[]{:S(2)}, u32[]{:S(2)}) collective-permute-start(f32[8,4096]{1,0:T(8,128)S(1)} %get-tuple-element.15), channel_id=1, source_target_pairs={{1,4},{5,8},{9,12},{4,1},{8,5},{12,9},{3,6},{7,10},{11,14},{6,3},{... | collective-permute-start | bytes 393224 | tf_op jit(solution)/shard_map/ppermute | solution.py:419
  91.0 0.0 collective-permute-done.1.inner
  91.0 4.3 %collective-permute-done.2.outer = f32[8,4096]{1,0:T(8,128)S(1)} collective-permute-done((f32[8,4096]{1,0:T(8,128)S(1)}, f32[8,4096]{1,0:T(8,128)S(1)}, u32[]{:S(2)}, u32[]{:S(2)}) %collective-permute-start.2) | collective-permute-done | bytes 131104 | tf_op jit(solution)/shard_map/ppermute | solution.py:419
  95.4 0.8 finish.1
  (15 shorter events, 0.1 us)
Async XLA Ops:
  31.4 13.5 %collective-permute-start = (bf16[128,32,128]{2,1,0:T(8,128)(2,1)S(1)}, bf16[128,32,128]{2,1,0:T(8,128)(2,1)}, u32[]{:S(2)}, u32[]{:S(2)}) collective-permute-start(bf16[128,32,128]{2,1,0:T(8,128)(2,1)S(1)} %bitcast.16), channel_id=1, source_target_pairs={{0,1},{1,0},{2,3},{3,2},{4,5},{5,4},{6,7},{7,6},{8,9},{9,8},{10,11... | collective-permute-start | bytes 3145736 | tf_op jit(solution)/shard_map/ppermute | solution.py:401
  33.1 2.3 %copy-start.5 = (s32[1,64,1]{1,2,0:T(1,128)S(1)}, s32[1,64,1]{1,2,0:T(1,128)}, u32[]{:S(2)}) copy-start(s32[1,64,1]{1,2,0:T(1,128)} %param.14) | copy-start | bytes 772
  33.1 2.5 %copy-start.4 = (s32[1,64]{1,0:T(1,128)S(1)}, s32[1,64]{1,0:T(1,128)}, u32[]{:S(2)}) copy-start(s32[1,64]{1,0:T(1,128)} %param.15) | copy-start | bytes 772
  33.1 2.5 %copy-start.6 = (bf16[256,256]{1,0:T(8,128)(2,1)S(1)}, bf16[256,256]{1,0:T(8,128)(2,1)}, u32[]{:S(2)}) copy-start(bf16[256,256]{1,0:T(8,128)(2,1)} %constant.61.clone.window_lanes) | copy-start | bytes 393220
  33.1 2.5 %copy-start.7 = (bf16[320,128]{1,0:T(8,128)(2,1)S(1)}, bf16[320,128]{1,0:T(8,128)(2,1)}, u32[]{:S(2)}) copy-start(bf16[320,128]{1,0:T(8,128)(2,1)} %constant.59.clone.window_rows) | copy-start | bytes 245764
  33.1 2.5 %copy-start.8 = (bf16[256,128]{1,0:T(8,128)(2,1)S(1)}, bf16[256,128]{1,0:T(8,128)(2,1)}, u32[]{:S(2)}) copy-start(bf16[256,128]{1,0:T(8,128)(2,1)} %constant.62.clone.band_lanes) | copy-start | bytes 196612
  33.1 2.5 %copy-start.9 = (bf16[64,256]{1,0:T(8,128)(2,1)S(1)}, bf16[64,256]{1,0:T(8,128)(2,1)}, u32[]{:S(2)}) copy-start(bf16[64,256]{1,0:T(8,128)(2,1)} %constant.60.clone.square_rows) | copy-start | bytes 98308
  35.7 9.2 %copy-start = (bf16[384,512]{1,0:T(8,128)(2,1)S(1)}, bf16[384,512]{1,0:T(8,128)(2,1)}, u32[]{:S(2)}) copy-start(bf16[384,512]{1,0:T(8,128)(2,1)} %constant.63.clone.chip_lanes) | copy-start | bytes 1179652
  35.7 9.2 %copy-start.1 = (bf16[512,256]{1,0:T(8,128)(2,1)S(1)}, bf16[512,256]{1,0:T(8,128)(2,1)}, u32[]{:S(2)}) copy-start(bf16[512,256]{1,0:T(8,128)(2,1)} %constant.66.clone.inverse_lanes) | copy-start | bytes 786436
  35.7 9.2 %copy-start.2 = (bf16[128,192]{1,0:T(8,128)(2,1)S(1)}, bf16[128,192]{1,0:T(8,128)(2,1)}, u32[]{:S(2)}) copy-start(bf16[128,192]{1,0:T(8,128)(2,1)} %constant.64.clone.chip_rows) | copy-start | bytes 147460
  35.7 9.2 %copy-start.3 = (bf16[128,256]{1,0:T(8,128)(2,1)S(1)}, bf16[128,256]{1,0:T(8,128)(2,1)}, u32[]{:S(2)}) copy-start(bf16[128,256]{1,0:T(8,128)(2,1)} %constant.65.clone.inverse_rows) | copy-start | bytes 196612
  56.9 29.8 %all-to-all-start.1 = ((s16[8,528,128]{2,1,0:T(8,128)(2,1)}), s16[8,528,128]{2,1,0:T(8,128)(2,1)S(1)}, u32[]{:S(2)}, u32[]{:S(2)}) async-start(s16[8,528,128]{2,1,0:T(8,128)(2,1)} %scores.1), calls=%async_computation.1 | async-start | bytes 2162688 | tf_op jit(solution)/shard_map/all_to_all | solution.py:413
  88.1 3.0 %collective-permute-start.1 = (f32[8,4096]{1,0:T(8,128)S(1)}, f32[8,4096]{1,0:T(8,128)S(1)}, u32[]{:S(2)}, u32[]{:S(2)}) collective-permute-start(f32[8,4096]{1,0:T(8,128)S(1)} %get-tuple-element.16), channel_id=1, source_target_pairs={{0,1},{1,0},{2,3},{3,2},{4,5},{5,4},{6,7},{7,6},{8,9},{9,8},{10,11... | collective-permute-start | bytes 393224 | tf_op jit(solution)/shard_map/ppermute | solution.py:416
  89.1 6.3 %collective-permute-start.2 = (f32[8,4096]{1,0:T(8,128)S(1)}, f32[8,4096]{1,0:T(8,128)S(1)}, u32[]{:S(2)}, u32[]{:S(2)}) collective-permute-start(f32[8,4096]{1,0:T(8,128)S(1)} %get-tuple-element.15), channel_id=1, source_target_pairs={{1,4},{5,8},{9,12},{4,1},{8,5},{12,9},{3,6},{7,10},{11,14},{6,3},{... | collective-permute-start | bytes 393224 | tf_op jit(solution)/shard_map/ppermute | solution.py:419

commit v4 on v3

--- a/solution.py
+++ b/solution.py
@@ -105,7 +105,6 @@
 
 def window_kernel(windows, window_rows, square_rows, window_lanes, band_lanes, spectra, scale):
     group = windows.shape[0]
-    base = pl.program_id(0) * group
     for first in range(0, group, 2):
         image = jnp.concatenate([windows[first], windows[first + 1]], axis=1)
         rows = dot(window_rows[...], image)
@@ -118,7 +117,7 @@
             lanes = slice(part * WIN, (part + 1) * WIN)
             high, low = halves(spec_rows[:, lanes])
             both = dot(jnp.concatenate([high, low], axis=1), window_lanes[...])
-            spectra[base + first + part] = both[:, :WIN] + both[:, WIN:]
+            spectra[first + part] = both[:, :WIN] + both[:, WIN:]
             pieces = []
             for source in (sums, squares):
                 own = source[:, lanes]
@@ -129,7 +128,7 @@
             mean = (boxes[0] + boxes[1] + boxes[2]) * (1.0 / (CHIP * CHIP))
             second = (boxes[3] + boxes[4] + boxes[5]) * (1.0 / (CHIP * CHIP))
             variance = second - mean * mean
-            scale[base + first + part] = lax.rsqrt(variance + epsilon)
+            scale[first + part] = lax.rsqrt(variance + epsilon)
 
 
 def score_kernel(
@@ -179,7 +178,7 @@
         lanes = slice(part % 2 * WIN, (part % 2 + 1) * WIN)
         for row in range(0, HALF, 32):
             upper, lower = slice(row, row + 32), slice(HALF + row, HALF + row + 32)
-            own_c, own_s = spectra[base + part, upper], spectra[base + part, lower]
+            own_c, own_s = spectra[part, upper], spectra[part, lower]
             turned_c, turned_s = pltpu.roll(own_c, HALF, 1), pltpu.roll(own_s, HALF, 1)
             same_c, same_s = pairs[part, upper, :WIN], pairs[part, lower, :WIN]
             cross_c, cross_s = pairs[part, upper, WIN:], pairs[part, lower, WIN:]
@@ -218,7 +217,7 @@
     for part in range(group):
         own = slice(part * ROWS, (part + 1) * ROWS)
         numerator = both[own, :WIN] + both[own, WIN:]
-        scores.append(numerator * (scale[base + part] * gain[part:part + 1]))
+        scores.append(numerator * (scale[part] * gain[part:part + 1]))
     largest = jnp.concatenate([jnp.max(jnp.abs(score), axis=0, keepdims=True) for score in scores], axis=0)
     largest = jnp.max(largest, axis=1, keepdims=True)
     power = jnp.ceil(jnp.log2(jnp.maximum(largest, 1e-30)))
@@ -282,8 +281,33 @@
     return pl.BlockSpec(memory_space=pltpu.VMEM)
 
 
+def away(array):
+    return pltpu.with_memory_space_constraint(array, pltpu.HBM)
+
+
 def near(array):
     return pltpu.with_memory_space_constraint(array, pltpu.VMEM)
+
+
+def spread_kernel(chips, sent):
+    chip_amount = chips.shape[0]
+    for first in range(0, chip_amount, 8):
+        for row in range(0, ROWS, 8):
+            lanes = [chips[first:first + 8, (row + i) * WIN:(row + i + 1) * WIN].astype(f32) for i in range(8)]
+            turned = jnp.swapaxes(jnp.stack(lanes, axis=0), 0, 1).astype(bf16)
+            for to in range(sent.shape[0]):
+                sent[to, first:first + 8, row:row + 8, :] = turned
+
+
+def spread(chips, tiles):
+    return pl.pallas_call(
+        spread_kernel,
+        in_specs=[resident()],
+        out_specs=resident(),
+        out_shape=pltpu.VMEM((tiles, chips.shape[0], ROWS, WIN), bf16),
+        compiler_params=pltpu.CompilerParams(vmem_limit_bytes=VMEM_GRANT),
+        name="spread",
+    )(chips)
 
 
 def prepare_windows(images, table):
@@ -294,10 +318,13 @@
         window_kernel,
         grid=(amount // group,),
         in_specs=[pl.BlockSpec((group, WIN, WIN), lambda i: (i, 0, 0))] + [resident() for _ in constants],
-        out_specs=[resident(), resident()],
+        out_specs=[
+            pl.BlockSpec((group, WIN, WIN), lambda i: (i, 0, 0)),
+            pl.BlockSpec((group, ROWS, WIN), lambda i: (i, 0, 0)),
+        ],
         out_shape=[
-            pltpu.VMEM((amount, WIN, WIN), f32),
-            pltpu.VMEM((amount, ROWS, WIN), f32),
+            pltpu.HBM((amount, WIN, WIN), f32),
+            pltpu.HBM((amount, ROWS, WIN), f32),
         ],
         cost_estimate=pl.CostEstimate(
             flops=amount * 2 * 900 * 65536, transcendentals=amount * ROWS * WIN, bytes_accessed=amount * 120000
@@ -318,7 +345,8 @@
             num_scalar_prefetch=len(scalars),
             grid=(amount // group,),
             in_specs=[
-                resident(), resident(),
+                pl.BlockSpec((group, WIN, WIN), lambda i, *_: (i, 0, 0)),
+                pl.BlockSpec((group, ROWS, WIN), lambda i, *_: (i, 0, 0)),
             ] + [resident() for _ in constants] + [resident() for _ in sources],
             out_specs=resident(),
             scratch_shapes=[
@@ -334,7 +362,7 @@
         out_shape=pltpu.VMEM(shape, jnp.int16),
         compiler_params=pltpu.CompilerParams(vmem_limit_bytes=VMEM_GRANT),
         name="scores",
-    )(*scalars, near(spectra), near(scale), *constants, *[near(source) for source in sources])
+    )(*scalars, away(spectra), away(scale), *[away(c) for c in constants], *[near(source) for source in sources])
 
 
 def average_scores(codes, capacity, chip_amount):
@@ -388,10 +416,9 @@
     devices = tiles * subs
     capacity = max(2, 2 * window_amount // devices)
 
-    block = chips.reshape(chip_amount, ROWS, WIN)
     images = windows.reshape(window_amount, WIN, WIN)
     sub = lax.axis_index("sub")
-    sent = jnp.broadcast_to(block.reshape(1, chip_amount * ROWS, WIN), (tiles, chip_amount * ROWS, WIN))
+    sent = spread(chips, tiles).reshape(tiles, chip_amount * ROWS, WIN)
     gathered = lax.all_to_all(sent, "tile", split_axis=0, concat_axis=0, tiled=True)
     gathered = gathered.reshape(tiles * chip_amount, ROWS, WIN)
     spectra, scale = prepare_windows(images, table)

time: 96.5 us -> 97.7 us (1.012)
  Pallas kernels: 23.3 us -> 24.8 us
    broadcast_in_dim x2 -> x0, local copies, waits for them, and re-layouts: 1.21 us -> none  [on_device(): jnp.broadcast_to(block.reshape(1, chip_amount * ROWS, WIN), (tiles, chip_...]
    unnamed x21 -> x15, local copies, waits for them, and re-layouts: 2.29 us -> 3.22 us
  transfers between devices with their start and end apart: 4 -> 4, of which waited for: 2 -> 2; matrix products, arithmetic and copies ran while one was open for 3% -> 2% of each run, Pallas kernels for 9% -> 10%
where the time goes in v4:
time: 97.7 us; the launch traced here: 97.4 us
  waiting for transfers between devices  30.7 us (31%)
  blocking collectives  30.1 us (31%)
  Pallas kernels  24.8 us (25%)
  starting transfers between devices  8.2 us (8%)
  local copies, waits for them, and re-layouts  3.22 us (3%)
    all_to_all x1, blocking collectives, on_device(): lax.all_to_all(sent, 'tile', split_axis=0, concat_axis=0, tiled=True)  30.1 us
    all_to_all x1, waiting for transfers between devices, on_device(): lax.all_to_all(codes, ('tile', 'sub'), split_axis=0, concat_axis=0, tiled...  26.3 us
    pallas_call x1, Pallas kernels, score_windows(): pl.pallas_call(functools.partial(score_kernel, capacity), grid_spec=pltpu...  12.6 us
    pallas_call x1, Pallas kernels, prepare_windows(): pl.pallas_call(window_kernel, grid=(amount // group,), in_specs=[pl.Block...  9.94 us
    ppermute x1, waiting for transfers between devices, on_device(): lax.ppermute(jnp.where(sub == 0, first, last), ('tile', 'sub'), ups + downs)  4.35 us
    all_to_all x1, starting transfers between devices, on_device(): lax.all_to_all(codes, ('tile', 'sub'), split_axis=0, concat_axis=0, tiled...  3.51 us
    unnamed x15, local copies, waits for them, and re-layouts  3.22 us
  transfers between devices with their start and end apart: 4, of which 2 were waited for; matrix products, arithmetic and copies ran while one was open for 2% of the time, Pallas kernels for 10%

profile of v4, /device:TPU:1, one launch (start us, length us, event | category | flops | bytes accessed | tf_op | source)
XLA Modules:
  0.0 97.4 jit_solution(14309803218768204762)
XLA Ops:
  0.0 0.9 copy-done
  1.0 0.2 spread.1
  1.1 30.1 %all_to_all.10 = bf16[4,1024,128]{2,1,0:T(8,128)(2,1)S(1)} all-to-all(bf16[4,1024,128]{2,1,0:T(8,128)(2,1)S(1)} %bitcast.18), channel_id=1, replica_groups=mesh['groups'=2,'tile'=4,'pair'=2,'sub'=2] {'tile'}, dimensions={0} | all-to-all | bytes 2097152 | tf_op jit(solution)/shard_map/all_to_all | solution.py:422
  31.3 1.8 %collective-permute-start = (bf16[128,32,128]{2,1,0:T(8,128)(2,1)S(1)}, bf16[128,32,128]{2,1,0:T(8,128)(2,1)}, u32[]{:S(2)}, u32[]{:S(2)}) collective-permute-start(bf16[128,32,128]{2,1,0:T(8,128)(2,1)S(1)} %bitcast.19), channel_id=1, source_target_pairs={{0,1},{1,0},{2,3},{3,2},{4,5},{5,4},{6,7},{7,6},{8,9},{9,8},{10,11... | collective-permute-start | bytes 3145736 | tf_op jit(solution)/shard_map/ppermute | solution.py:428
  33.0 0.0 copy-start.5
  33.0 0.0 copy-start.6
  33.0 2.2 %copy.13 = bf16[8,8,128,128]{3,2,1,0:T(8,128)(2,1)S(1)} copy(bf16[8,8,128,128]{3,1,2,0:T(8,128)(2,1)} %bitcast.26) | data formatting | bytes 4194304
  35.3 0.0 copy-done.2
  35.3 0.2 convert_reduce_fusion.ranks
  35.5 0.0 copy-done.1
  35.5 0.0 copy-done.3
  35.5 0.0 copy-done.4
  35.5 0.0 copy-done.5
  35.6 9.9 %window_spectra.1 = (f32[64,128,128]{2,1,0:T(8,128)}, f32[64,32,128]{2,1,0:T(8,128)}) custom-call(bf16[64,128,128]{2,1,0:T(8,128)(2,1)S(1)} %bitcast.21, bf16[320,128]{1,0:T(8,128)(2,1)S(1)} %copy-done.4, bf16[64,256]{1,0:T(8,128)(2,1)S(1)} %copy-done.6, bf16[256,256]{1,0:T(8,128)(2,1)S(1)} %copy-done.3, bf16[256,128]{1,0:T(8,128)(2,1)S(1)} %copy-done.5), custom_call_target="tpu_custom_call" | custom-call | flops 7549747200 | bytes 7680000 | tf_op jit(solution)/shard_map/window_spectra/pallas_call | solution.py:317
  45.5 0.0 collective-permute-done.rest_1_
  45.5 12.6 %scores.1 = s16[8,528,128]{2,1,0:T(8,128)(2,1)} custom-call(s32[64]{0:T(128)S(1)} %get-tuple-element.18.choice, s32[64]{0:T(128)S(1)} %get-tuple-element.17.place, s32[64]{0:T(128)S(1)} %bitcast.25, s32[64]{0:T(128)S(1)} %convert_reduce_fusion.ranks, s32[64]{0:T(128)S(1)} %bitcast.23, s32[1]{0:T(128)} %bitcast.3.position, ...), custom_call_target="tpu_custom_call" | custom-call | tf_op jit(solution)/shard_map/scores/pallas_call | solution.py:342
  58.1 3.5 %all-to-all-start.1 = ((s16[8,528,128]{2,1,0:T(8,128)(2,1)}), s16[8,528,128]{2,1,0:T(8,128)(2,1)S(1)}, u32[]{:S(2)}, u32[]{:S(2)}) async-start(s16[8,528,128]{2,1,0:T(8,128)(2,1)} %scores.1), calls=%async_computation.1 | async-start | bytes 2162688 | tf_op jit(solution)/shard_map/all_to_all | solution.py:440
  61.6 26.3 %all-to-all-done.1.codes = s16[8,528,128]{2,1,0:T(8,128)(2,1)S(1)} async-done(((s16[8,528,128]{2,1,0:T(8,128)(2,1)}), s16[8,528,128]{2,1,0:T(8,128)(2,1)S(1)}, u32[]{:S(2)}, u32[]{:S(2)}) %all-to-all-start.1) | async-done | bytes 1081376 | tf_op jit(solution)/shard_map/all_to_all | solution.py:440
  87.9 1.3 %average.1 = (f32[32,4096]{1,0:T(8,128)S(1)}, f32[8,4096]{1,0:T(8,128)S(1)}, f32[8,4096]{1,0:T(8,128)S(1)}) custom-call(s16[8,528,128]{2,1,0:T(8,128)(2,1)S(1)} %all-to-all-done.1.codes), custom_call_target="tpu_custom_call" | custom-call | tf_op jit(solution)/shard_map/average/pallas_call | solution.py:370
  89.2 1.0 %collective-permute-start.1 = (f32[8,4096]{1,0:T(8,128)S(1)}, f32[8,4096]{1,0:T(8,128)S(1)}, u32[]{:S(2)}, u32[]{:S(2)}) collective-permute-start(f32[8,4096]{1,0:T(8,128)S(1)} %get-tuple-element.16), channel_id=1, source_target_pairs={{0,1},{1,0},{2,3},{3,2},{4,5},{5,4},{6,7},{7,6},{8,9},{9,8},{10,11... | collective-permute-start | bytes 393224 | tf_op jit(solution)/shard_map/ppermute | solution.py:443
  90.3 1.9 %collective-permute-start.2 = (f32[8,4096]{1,0:T(8,128)S(1)}, f32[8,4096]{1,0:T(8,128)S(1)}, u32[]{:S(2)}, u32[]{:S(2)}) collective-permute-start(f32[8,4096]{1,0:T(8,128)S(1)} %get-tuple-element.15), channel_id=1, source_target_pairs={{1,4},{5,8},{9,12},{4,1},{8,5},{12,9},{3,6},{7,10},{11,14},{6,3},{... | collective-permute-start | bytes 393224 | tf_op jit(solution)/shard_map/ppermute | solution.py:446
  92.2 0.0 collective-permute-done.1.inner
  92.2 4.3 %collective-permute-done.2.outer = f32[8,4096]{1,0:T(8,128)S(1)} collective-permute-done((f32[8,4096]{1,0:T(8,128)S(1)}, f32[8,4096]{1,0:T(8,128)S(1)}, u32[]{:S(2)}, u32[]{:S(2)}) %collective-permute-start.2) | collective-permute-done | bytes 131104 | tf_op jit(solution)/shard_map/ppermute | solution.py:446
  96.6 0.8 finish.1
  (8 shorter events, 0.1 us)
Async XLA Ops:
  0.0 0.9 copy-start
  31.3 14.2 %collective-permute-start = (bf16[128,32,128]{2,1,0:T(8,128)(2,1)S(1)}, bf16[128,32,128]{2,1,0:T(8,128)(2,1)}, u32[]{:S(2)}, u32[]{:S(2)}) collective-permute-start(bf16[128,32,128]{2,1,0:T(8,128)(2,1)S(1)} %bitcast.19), channel_id=1, source_target_pairs={{0,1},{1,0},{2,3},{3,2},{4,5},{5,4},{6,7},{7,6},{8,9},{9,8},{10,11... | collective-permute-start | bytes 3145736 | tf_op jit(solution)/shard_map/ppermute | solution.py:428
  33.0 2.3 %copy-start.2 = (s32[1,64,1]{1,2,0:T(1,128)S(1)}, s32[1,64,1]{1,2,0:T(1,128)}, u32[]{:S(2)}) copy-start(s32[1,64,1]{1,2,0:T(1,128)} %param.14) | copy-start | bytes 772
  33.0 2.5 %copy-start.1 = (s32[1,64]{1,0:T(1,128)S(1)}, s32[1,64]{1,0:T(1,128)}, u32[]{:S(2)}) copy-start(s32[1,64]{1,0:T(1,128)} %param.15) | copy-start | bytes 772
  33.0 2.5 %copy-start.3 = (bf16[256,256]{1,0:T(8,128)(2,1)S(1)}, bf16[256,256]{1,0:T(8,128)(2,1)}, u32[]{:S(2)}) copy-start(bf16[256,256]{1,0:T(8,128)(2,1)} %constant.61.clone.window_lanes) | copy-start | bytes 393220
  33.0 2.5 %copy-start.4 = (bf16[320,128]{1,0:T(8,128)(2,1)S(1)}, bf16[320,128]{1,0:T(8,128)(2,1)}, u32[]{:S(2)}) copy-start(bf16[320,128]{1,0:T(8,128)(2,1)} %constant.59.clone.window_rows) | copy-start | bytes 245764
  33.0 2.5 %copy-start.5 = (bf16[256,128]{1,0:T(8,128)(2,1)S(1)}, bf16[256,128]{1,0:T(8,128)(2,1)}, u32[]{:S(2)}) copy-start(bf16[256,128]{1,0:T(8,128)(2,1)} %constant.62.clone.band_lanes) | copy-start | bytes 196612
  33.0 2.5 %copy-start.6 = (bf16[64,256]{1,0:T(8,128)(2,1)S(1)}, bf16[64,256]{1,0:T(8,128)(2,1)}, u32[]{:S(2)}) copy-start(bf16[64,256]{1,0:T(8,128)(2,1)} %constant.60.clone.square_rows) | copy-start | bytes 98308
  58.1 29.8 %all-to-all-start.1 = ((s16[8,528,128]{2,1,0:T(8,128)(2,1)}), s16[8,528,128]{2,1,0:T(8,128)(2,1)S(1)}, u32[]{:S(2)}, u32[]{:S(2)}) async-start(s16[8,528,128]{2,1,0:T(8,128)(2,1)} %scores.1), calls=%async_computation.1 | async-start | bytes 2162688 | tf_op jit(solution)/shard_map/all_to_all | solution.py:440
  89.2 3.0 %collective-permute-start.1 = (f32[8,4096]{1,0:T(8,128)S(1)}, f32[8,4096]{1,0:T(8,128)S(1)}, u32[]{:S(2)}, u32[]{:S(2)}) collective-permute-start(f32[8,4096]{1,0:T(8,128)S(1)} %get-tuple-element.16), channel_id=1, source_target_pairs={{0,1},{1,0},{2,3},{3,2},{4,5},{5,4},{6,7},{7,6},{8,9},{9,8},{10,11... | collective-permute-start | bytes 393224 | tf_op jit(solution)/shard_map/ppermute | solution.py:443
  90.3 6.3 %collective-permute-start.2 = (f32[8,4096]{1,0:T(8,128)S(1)}, f32[8,4096]{1,0:T(8,128)S(1)}, u32[]{:S(2)}, u32[]{:S(2)}) collective-permute-start(f32[8,4096]{1,0:T(8,128)S(1)} %get-tuple-element.15), channel_id=1, source_target_pairs={{1,4},{5,8},{9,12},{4,1},{8,5},{12,9},{3,6},{7,10},{11,14},{6,3},{... | collective-permute-start | bytes 393224 | tf_op jit(solution)/shard_map/ppermute | solution.py:446

commit v5 on v4

--- a/solution.py
+++ b/solution.py
@@ -103,10 +103,11 @@
     return (high, middle, low)
 
 
-def window_kernel(windows, window_rows, square_rows, window_lanes, band_lanes, spectra, scale):
-    group = windows.shape[0]
+def window_kernel(order, windows, window_rows, square_rows, window_lanes, band_lanes, spectra, scale):
+    group = spectra.shape[0]
+    base = pl.program_id(0) * group
     for first in range(0, group, 2):
-        image = jnp.concatenate([windows[first], windows[first + 1]], axis=1)
+        image = jnp.concatenate([windows[order[base + first]], windows[order[base + first + 1]]], axis=1)
         rows = dot(window_rows[...], image)
         spec_rows = rows[:WIN] + rows[WIN:2 * WIN]
         sums = rows[2 * WIN:]
@@ -131,29 +132,51 @@
             scale[first + part] = lax.rsqrt(variance + epsilon)
 
 
-def score_kernel(
-    capacity, choice, place, target, ranks, slots, position,
-    spectra, scale, chip_lanes, chip_rows, inverse_rows, inverse_lanes, *rest,
-):
+def score_kernel(capacity, subs, opening, closing, *refs):
+    (choice, spots, target, ranks, slots, position, limits,
+     spectra, scale, chip_lanes, chip_rows, inverse_rows, inverse_lanes, *rest) = refs
     *sources, out, marks, lefts, lines, packs, pairs, products, backs = rest
     step = pl.program_id(0)
+    kept = () if opening else sources[-2:]
+    sources = sources if opening else sources[:-2]
+
+    @pl.when(step == 0)
+    def _():
+        out[...] = jnp.zeros_like(out) if opening else kept[0][...]
+        marks[...] = jnp.zeros_like(marks) if opening else kept[1][...]
+
+    @pl.when((step >= limits[0]) & (step < limits[1]))
+    def _():
+        score_group(
+            capacity, subs, step, choice, spots, target, ranks, slots, position, spectra, scale,
+            chip_lanes, chip_rows, inverse_rows, inverse_lanes, sources,
+            out, marks, lefts, lines, packs, pairs, products, backs,
+        )
+
+    if closing:
+        @pl.when(step == pl.num_programs(0) - 1)
+        def _():
+            for to in range(out.shape[0]):
+                notes = marks[to]
+                notes = jnp.concatenate([notes, jnp.zeros_like(notes)], axis=0)
+                out[to, capacity * ROWS:, :] = notes.astype(jnp.int32).astype(jnp.int16)
+
+
+def score_group(
+    capacity, subs, step, choice, spots, target, ranks, slots, position, spectra, scale,
+    chip_lanes, chip_rows, inverse_rows, inverse_lanes, sources,
+    out, marks, lefts, lines, packs, pairs, products, backs,
+):
     group = lefts.shape[0] // ROWS
     base = step * group
-    body = capacity * ROWS
     lane = lax.broadcasted_iota(jnp.int32, (8, WIN), 1)
     line = lax.broadcasted_iota(jnp.int32, (8, WIN), 0)
-
-    @pl.when(step == 0)
-    def _():
-        out[...] = jnp.zeros_like(out)
-        marks[...] = jnp.zeros_like(marks)
-
     raws = []
     for part in range(group):
         window = base + part
-        raw = sources[0][place[window]]
+        raw = sources[0][spots[0, window]]
         for index in range(1, len(sources)):
-            raw = jnp.where(choice[window] == index, sources[index][place[window]], raw)
+            raw = jnp.where(choice[window] == index, sources[index][spots[index // subs, window]], raw)
         raws.append(raw.astype(f32))
     total = jnp.concatenate([jnp.sum(raw, axis=0, keepdims=True) for raw in raws], axis=0)
     mean = jnp.sum(total, axis=1, keepdims=True) * (1.0 / (CHIP * CHIP))
@@ -234,14 +257,7 @@
         here = lane == position[0] * capacity + ranks[window]
         named = (slots[window] + 1).astype(f32)
         mark = jnp.where(line == 0, named, jnp.where(line == 1, power[part:part + 1], 0.0))
-        marks[to] = marks[to] + jnp.where(here, mark, 0.0)
-
-    @pl.when(step == pl.num_programs(0) - 1)
-    def _():
-        for to in range(out.shape[0]):
-            notes = marks[to]
-            notes = jnp.concatenate([notes, jnp.zeros_like(notes)], axis=0)
-            out[to, body:, :] = notes.astype(jnp.int32).astype(jnp.int16)
+        marks[to] = jnp.where(here & (line < 2), mark, marks[to])
 
 
 def average_kernel(capacity, chip_amount, codes, smooth, first, last, values):
@@ -289,39 +305,46 @@
     return pltpu.with_memory_space_constraint(array, pltpu.VMEM)
 
 
-def spread_kernel(chips, sent):
-    chip_amount = chips.shape[0]
-    for first in range(0, chip_amount, 8):
+def spread_kernel(chips, *parts):
+    for first in range(0, chips.shape[0], 8):
         for row in range(0, ROWS, 8):
             lanes = [chips[first:first + 8, (row + i) * WIN:(row + i + 1) * WIN].astype(f32) for i in range(8)]
             turned = jnp.swapaxes(jnp.stack(lanes, axis=0), 0, 1).astype(bf16)
-            for to in range(sent.shape[0]):
-                sent[to, first:first + 8, row:row + 8, :] = turned
-
-
-def spread(chips, tiles):
+            own = first - parts[0].shape[1]
+            if own >= 0:
+                parts[1][own:own + 8, row:row + 8, :] = turned
+            else:
+                for to in range(parts[0].shape[0]):
+                    parts[0][to, first:first + 8, row:row + 8, :] = turned
+
+
+def spread(chips, tiles, cut):
+    shapes = [(tiles, cut, ROWS, WIN), (chips.shape[0] - cut, ROWS, WIN)]
     return pl.pallas_call(
         spread_kernel,
         in_specs=[resident()],
-        out_specs=resident(),
-        out_shape=pltpu.VMEM((tiles, chips.shape[0], ROWS, WIN), bf16),
+        out_specs=[resident(), resident()],
+        out_shape=[pltpu.VMEM(shape, bf16) for shape in shapes],
         compiler_params=pltpu.CompilerParams(vmem_limit_bytes=VMEM_GRANT),
         name="spread",
     )(chips)
 
 
-def prepare_windows(images, table):
+def prepare_windows(images, order, table):
     amount = images.shape[0]
     group = min(GROUP, amount)
     constants = [jnp.asarray(table[k]) for k in ("window_rows", "square_rows", "window_lanes", "band_lanes")]
     return pl.pallas_call(
         window_kernel,
-        grid=(amount // group,),
-        in_specs=[pl.BlockSpec((group, WIN, WIN), lambda i: (i, 0, 0))] + [resident() for _ in constants],
-        out_specs=[
-            pl.BlockSpec((group, WIN, WIN), lambda i: (i, 0, 0)),
-            pl.BlockSpec((group, ROWS, WIN), lambda i: (i, 0, 0)),
-        ],
+        grid_spec=pltpu.PrefetchScalarGridSpec(
+            num_scalar_prefetch=1,
+            grid=(amount // group,),
+            in_specs=[resident()] + [resident() for _ in constants],
+            out_specs=[
+                pl.BlockSpec((group, WIN, WIN), lambda i, _: (i, 0, 0)),
+                pl.BlockSpec((group, ROWS, WIN), lambda i, _: (i, 0, 0)),
+            ],
+        ),
         out_shape=[
             pltpu.HBM((amount, WIN, WIN), f32),
             pltpu.HBM((amount, ROWS, WIN), f32),
@@ -331,26 +354,31 @@
         ),
         compiler_params=pltpu.CompilerParams(vmem_limit_bytes=VMEM_GRANT),
         name="window_spectra",
-    )(images, *constants)
-
-
-def score_windows(spectra, scale, sources, scalars, table, devices, capacity):
+    )(order, near(images), *constants)
+
+
+def score_windows(spectra, scale, sources, scalars, table, devices, capacity, subs, earlier, closing):
     amount = spectra.shape[0]
     group = min(SCORE_GROUP, amount)
     constants = [jnp.asarray(table[k]) for k in ("chip_lanes", "chip_rows", "inverse_rows", "inverse_lanes")]
-    shape = (devices, capacity * ROWS + 16, WIN)
+    shapes = [(devices, capacity * ROWS + 16, WIN), (devices, 8, WIN)]
+    count = len(scalars)
+    kept = [] if earlier is None else [near(e) for e in earlier]
+    steps = amount // group
+
+    def block(i, *prefetched):
+        limits = prefetched[-1]
+        return (jnp.clip(i, jnp.minimum(limits[0], steps - 1), jnp.maximum(limits[1] - 1, 0)), 0, 0)
+
     return pl.pallas_call(
-        functools.partial(score_kernel, capacity),
+        functools.partial(score_kernel, capacity, subs, earlier is None, closing),
         grid_spec=pltpu.PrefetchScalarGridSpec(
-            num_scalar_prefetch=len(scalars),
-            grid=(amount // group,),
-            in_specs=[
-                pl.BlockSpec((group, WIN, WIN), lambda i, *_: (i, 0, 0)),
-                pl.BlockSpec((group, ROWS, WIN), lambda i, *_: (i, 0, 0)),
-            ] + [resident() for _ in constants] + [resident() for _ in sources],
-            out_specs=resident(),
+            num_scalar_prefetch=count,
+            grid=(steps,),
+            in_specs=[pl.BlockSpec((group, WIN, WIN), block), pl.BlockSpec((group, ROWS, WIN), block)]
+            + [resident() for _ in constants] + [resident() for _ in sources] + [resident() for _ in kept],
+            out_specs=[resident(), resident()],
             scratch_shapes=[
-                pltpu.VMEM((devices, 8, WIN), f32),
                 pltpu.VMEM((group * ROWS, 3 * WIN), bf16),
                 pltpu.VMEM((group * ROWS, 4 * WIN), f32),
                 pltpu.VMEM((group * ROWS, 4 * WIN), bf16),
@@ -359,10 +387,13 @@
                 pltpu.VMEM((group // 2, OFF, 2 * WIN), f32),
             ],
         ),
-        out_shape=pltpu.VMEM(shape, jnp.int16),
+        out_shape=[pltpu.VMEM(shapes[0], jnp.int16), pltpu.VMEM(shapes[1], f32)],
+        cost_estimate=pl.CostEstimate(
+            flops=amount * 800 * 65536, transcendentals=amount * ROWS * WIN, bytes_accessed=amount * 60000
+        ),
         compiler_params=pltpu.CompilerParams(vmem_limit_bytes=VMEM_GRANT),
         name="scores",
-    )(*scalars, away(spectra), away(scale), *[away(c) for c in constants], *[near(source) for source in sources])
+    )(*scalars, away(spectra), away(scale), *[near(c) for c in constants], *[near(p) for p in sources], *kept)
 
 
 def average_scores(codes, capacity, chip_amount):
@@ -418,24 +449,51 @@
 
     images = windows.reshape(window_amount, WIN, WIN)
     sub = lax.axis_index("sub")
-    sent = spread(chips, tiles).reshape(tiles, chip_amount * ROWS, WIN)
-    gathered = lax.all_to_all(sent, "tile", split_axis=0, concat_axis=0, tiled=True)
-    gathered = gathered.reshape(tiles * chip_amount, ROWS, WIN)
-    spectra, scale = prepare_windows(images, table)
-    sources = [gathered]
-    for shift in range(1, subs):
-        ring = [(i, (i - shift) % subs) for i in range(subs)]
-        sources.append(lax.ppermute(gathered, "sub", ring))
+    cut = chip_amount * 3 // 4 // 8 * 8
+    first_part, rest_part = spread(chips, tiles, cut)
+    got = lax.all_to_all(first_part.reshape(tiles, cut * ROWS, WIN), "tile", split_axis=0, concat_axis=0, tiled=True)
+    rests = [rest_part]
+    for hop in range(1, tiles):
+        rests.append(lax.ppermute(rest_part, "tile", [(i, (i + hop) % tiles) for i in range(tiles)]))
+    gathered = [got.reshape(tiles * cut, ROWS, WIN), jnp.concatenate(rests, axis=0)]
+    sources = []
+    for index, part in enumerate(gathered):
+        sources.append([part])
+        for shift in range(1, subs):
+            ring = [(i, (i - shift) % subs) for i in range(subs)]
+            sources[index].append(lax.ppermute(part, "sub", ring))
 
     order = jnp.arange(window_amount, dtype=jnp.int32)
+    late = (slots >= cut).astype(jnp.int32)
+    before = order[:, None] > order[None, :]
     matches = targets[:, None] == targets[None, :]
-    earlier = order[:, None] > order[None, :]
-    ranks = jnp.sum((matches & earlier).astype(jnp.int32), axis=1)
-    choice = (targets % subs - sub) % subs
-    place = (targets // subs) * chip_amount + slots
+    ranks = jnp.sum((matches & before).astype(jnp.int32), axis=1)
+    ahead = (late[None, :] < late[:, None]) | ((late[None, :] == late[:, None]) & before)
+    rows_at = jnp.sum(ahead.astype(jnp.int32), axis=1)
+    chosen = rows_at[None, :] == order[:, None]
+
+    def sort(values):
+        return jnp.sum(jnp.where(chosen, values[None, :], 0), axis=1)
+
+    group = min(SCORE_GROUP, window_amount)
+    split = lax.div(window_amount - jnp.sum(late), group)
+    place = (targets // subs) * cut + jnp.minimum(slots, cut - 1)
+    turn = (lax.axis_index("tile") - targets // subs) % tiles
+    place_late = turn * (chip_amount - cut) + jnp.maximum(slots - cut, 0)
+    choice = (targets % subs - sub) % subs + late * subs
     position = jnp.full((1,), lax.axis_index(("tile", "sub")), jnp.int32)
-    scalars = (choice, place, targets, ranks, slots, position)
-    codes = score_windows(spectra, scale, sources, scalars, table, devices, capacity)
+    listing = sort(order)
+    spectra, scale = prepare_windows(images, listing, table)
+    spots = jnp.stack([sort(place), sort(place_late)])
+    scalars = (sort(choice), spots, sort(targets), sort(ranks), sort(slots), position)
+    settings = (table, devices, capacity, subs)
+    zero = jnp.zeros_like(split)
+    limits = jnp.stack([zero, split])
+    partial = score_windows(spectra, scale, sources[0], (*scalars, limits), *settings, None, False)
+    limits = jnp.stack([split, zero + window_amount // group])
+    codes, _ = score_windows(
+        spectra, scale, sources[0] + sources[1], (*scalars, limits), *settings, partial, True
+    )
 
     received = lax.all_to_all(codes, ("tile", "sub"), split_axis=0, concat_axis=0, tiled=True)
     smooth, first, last = average_scores(received, capacity, chip_amount)

time: 97.7 us -> 94.2 us (0.964)
  blocking collectives: 30.1 us -> 0 us
  starting transfers between devices: 8.2 us -> 19.1 us
  local copies, waits for them, and re-layouts: 3.22 us -> 10 us
  other arithmetic: 0.22 us -> 5.06 us
  Pallas kernels: 24.8 us -> 27.8 us
    all_to_all x1 -> x0, blocking collectives: 30.1 us -> none  [on_device(): lax.all_to_all(sent, 'tile', split_axis=0, concat_axis=0, tiled=True)]
    unnamed x15 -> x26, local copies, waits for them, and re-layouts: 3.22 us -> 9.14 us
    ppermute x1 -> x5, starting transfers between devices: 1.75 us -> 7.08 us  [the longest x3 5.49 us: on_device(): lax.ppermute(rest_part, 'tile', [(i, (i + hop) % tiles) for i in range(ti...]
    all_to_all x0 -> x1, starting transfers between devices: none -> 3.49 us  [on_device(): lax.all_to_all(first_part.reshape(tiles, cut * ROWS, WIN), 'tile', split_...]
    pallas_call x3 -> x4, Pallas kernels: 22.7 us -> 25.7 us  [the longest x2 14.2 us: score_windows(): pl.pallas_call(functools.partial(score_kernel, capacity, subs, earlier is...]
    all_to_all x1, starting transfers between devices: 3.51 us -> 5.54 us  [on_device(): lax.all_to_all(codes, ('tile', 'sub'), split_axis=0, concat_axis=0, tiled...]
    reduce_sum x1 -> x3, other arithmetic: 0.17 us -> 2.21 us  [the longest x1 1.29 us: on_device(): split = lax.div(window_amount - jnp.sum(late), group)]
  transfers between devices with their start and end apart: 4 -> 9, of which waited for: 2 -> 2; matrix products, arithmetic and copies ran while one was open for 2% -> 10% of each run, Pallas kernels for 10% -> 21%
where the time goes in v5:
time: 94.2 us; the launch traced here: 93.4 us
  waiting for transfers between devices  30.7 us (33%)
  Pallas kernels  27.8 us (30%)
  starting transfers between devices  19.1 us (20%)
  local copies, waits for them, and re-layouts  10 us (11%)
  other arithmetic  5.06 us (5%)
    all_to_all x1, waiting for transfers between devices, on_device(): lax.all_to_all(codes, ('tile', 'sub'), split_axis=0, concat_axis=0, tiled...  26.3 us
    pallas_call x2, Pallas kernels, score_windows(): pl.pallas_call(functools.partial(score_kernel, capacity, subs, earlier is...  14.2 us
    pallas_call x1, Pallas kernels, prepare_windows(): pl.pallas_call(window_kernel, grid_spec=pltpu.PrefetchScalarGridSpec(num_...  10.5 us
    unnamed x26, local copies, waits for them, and re-layouts  9.14 us
    all_to_all x1, starting transfers between devices, on_device(): lax.all_to_all(codes, ('tile', 'sub'), split_axis=0, concat_axis=0, tiled...  5.54 us
    ppermute x3, starting transfers between devices, on_device(): lax.ppermute(rest_part, 'tile', [(i, (i + hop) % tiles) for i in range(ti...  5.49 us
    ppermute x1, waiting for transfers between devices, on_device(): lax.ppermute(jnp.where(sub == 0, first, last), ('tile', 'sub'), ups + downs)  4.35 us
    all_to_all x1, starting transfers between devices, on_device(): lax.all_to_all(first_part.reshape(tiles, cut * ROWS, WIN), 'tile', split_...  3.49 us
  transfers between devices with their start and end apart: 9, of which 2 were waited for; matrix products, arithmetic and copies ran while one was open for 10% of the time, Pallas kernels for 21%

profile of v5, /device:TPU:1, one launch (start us, length us, event | category | flops | bytes accessed | tf_op | source)
XLA Modules:
  0.0 93.4 jit_solution(9614119460313018143)
XLA Ops:
  0.0 0.9 %copy-done = bf16[1,32,4096]{2,1,0:T(8,128)(2,1)S(1)} copy-done((bf16[1,32,4096]{2,1,0:T(8,128)(2,1)S(1)}, bf16[1,32,4096]{2,1,0:T(8,128)(2,1)}, u32[]{:S(2)}) %copy-start) | copy-done | bytes 262168
  1.0 1.0 %spread.1 = (bf16[4,24,32,128]{3,2,1,0:T(8,128)(2,1)}, bf16[8,32,128]{2,1,0:T(8,128)(2,1)S(1)}) custom-call(bf16[32,4096]{1,0:T(8,128)(2,1)S(1)} %bitcast.45), custom_call_target="tpu_custom_call" | custom-call | tf_op jit(solution)/shard_map/spread/pallas_call | solution.py:323
  2.0 2.1 %collective-permute-start.1 = (bf16[8,32,128]{2,1,0:T(8,128)(2,1)S(1)}, bf16[8,32,128]{2,1,0:T(8,128)(2,1)}, u32[]{:S(2)}, u32[]{:S(2)}) collective-permute-start(bf16[8,32,128]{2,1,0:T(8,128)(2,1)S(1)} %get-tuple-element.18), channel_id=1, source_target_pairs={{0,4},{4,8},{8,12},{12,0},{1,5},{5,9},{9,13},{13,1},{2,6},{6,10},{... | collective-permute-start | bytes 196616 | tf_op jit(solution)/shard_map/ppermute | solution.py:457
  4.1 2.3 %collective-permute-start.2 = (bf16[8,32,128]{2,1,0:T(8,128)(2,1)S(1)}, bf16[8,32,128]{2,1,0:T(8,128)(2,1)}, u32[]{:S(2)}, u32[]{:S(2)}) collective-permute-start(bf16[8,32,128]{2,1,0:T(8,128)(2,1)S(1)} %get-tuple-element.18), channel_id=1, source_target_pairs={{0,8},{4,12},{8,0},{12,4},{1,9},{5,13},{9,1},{13,5},{2,10},{6,14},... | collective-permute-start | bytes 196616 | tf_op jit(solution)/shard_map/ppermute | solution.py:457
  6.4 1.1 %collective-permute-start.3 = (bf16[8,32,128]{2,1,0:T(8,128)(2,1)S(1)}, bf16[8,32,128]{2,1,0:T(8,128)(2,1)}, u32[]{:S(2)}, u32[]{:S(2)}) collective-permute-start(bf16[8,32,128]{2,1,0:T(8,128)(2,1)S(1)} %get-tuple-element.18), channel_id=1, source_target_pairs={{0,12},{4,0},{8,4},{12,8},{1,13},{5,1},{9,5},{13,9},{2,14},{6,2},{... | collective-permute-start | bytes 196616 | tf_op jit(solution)/shard_map/ppermute | solution.py:457
  7.5 3.5 %all-to-all-start = ((bf16[4,768,128]{2,1,0:T(8,128)(2,1)}), bf16[4,768,128]{2,1,0:T(8,128)(2,1)S(1)}, u32[]{:S(2)}, u32[]{:S(2)}) async-start(bf16[4,768,128]{2,1,0:T(8,128)(2,1)} %bitcast.13), calls=%async_computation | async-start | bytes 1572864 | tf_op jit(solution)/shard_map/all_to_all | solution.py:454
  13.0 1.3 %fusion.12 = s32[]{:T(128)} fusion(s32[1,64]{1,0:T(1,128)} %param.15), kind=kLoop, calls=%fused_computation.48 | loop fusion | flops 191 | bytes 260 | tf_op jit(solution)/shard_map/reduce_sum | solution.py:479
  14.3 2.2 %copy.13 = bf16[8,8,128,128]{3,2,1,0:T(8,128)(2,1)S(1)} copy(bf16[8,8,128,128]{3,1,2,0:T(8,128)(2,1)} %bitcast.46) | data formatting | bytes 4194304
  18.1 0.9 copy-done.4
  20.6 10.5 %window_spectra.1 = (f32[64,128,128]{2,1,0:T(8,128)}, f32[64,32,128]{2,1,0:T(8,128)}) custom-call(s32[64]{0:T(128)S(1)} %get-tuple-element.25.order, bf16[64,128,128]{2,1,0:T(8,128)(2,1)S(1)} %bitcast.41, bf16[320,128]{1,0:T(8,128)(2,1)S(1)} %copy-done.4, bf16[64,256]{1,0:T(8,128)(2,1)S(1)} %copy-done.8, bf16[256,256]{1,0:T(8,128)(2,1)S(1)} %copy-done.3, ...), custom_call_target="tpu_custom_call" | custom-call | flops 7549747200 | bytes 7680000 | tf_op jit(solution)/shard_map/window_spectra/pallas_call | solution.py:337
  31.1 1.5 %collective-permute-start = (bf16[96,32,128]{2,1,0:T(8,128)(2,1)S(1)}, bf16[96,32,128]{2,1,0:T(8,128)(2,1)S(1)}, u32[]{:S(2)}, u32[]{:S(2)}) collective-permute-start(bf16[96,32,128]{2,1,0:T(8,128)(2,1)S(1)} %bitcast.42), channel_id=1, source_target_pairs={{0,1},{1,0},{2,3},{3,2},{4,5},{5,4},{6,7},{7,6},{8,9},{9,8},{10,11... | collective-permute-start | bytes 2359304 | tf_op jit(solution)/shard_map/ppermute | solution.py:464
  33.4 0.9 constant_dynamic-update-slice_fusion.2
  34.3 0.9 constant_dynamic-update-slice_fusion.1
  35.1 0.9 constant_dynamic-update-slice_fusion.refs_15_
  36.1 0.9 %copy-done.2 = bf16[512,256]{1,0:T(8,128)(2,1)S(1)} copy-done((bf16[512,256]{1,0:T(8,128)(2,1)S(1)}, bf16[512,256]{1,0:T(8,128)(2,1)}, u32[]{:S(2)}) %copy-start.2) | copy-done | bytes 262168
  37.9 8.8 %scores.2 = (s16[8,528,128]{2,1,0:T(8,128)(2,1)S(1)}, f32[8,8,128]{2,1,0:T(8,128)S(1)}) custom-call(s32[64]{0:T(128)S(1)} %get-tuple-element.31.refs_0_, s32[2,64]{1,0:T(2,128)S(1)} %pad_add_fusion.refs_1_, s32[64]{0:T(128)S(1)} %get-tuple-element.28.refs_2_, s32[64]{0:T(128)S(1)} %get-tuple-element.27.refs_3_, s32[64]{0:T(128)S(1)} %get-tuple-element.26.refs_4_, ...), custom_call_target="tpu_custom_call" | custom-call | flops 3355443200 | bytes 3840000 | tf_op jit(solution)/shard_map/scores/pallas_call | solution.py:373
  46.7 5.4 %scores.3 = (s16[8,528,128]{2,1,0:T(8,128)(2,1)}, f32[8,8,128]{2,1,0:T(8,128)}) custom-call(s32[64]{0:T(128)S(1)} %get-tuple-element.31.refs_0_, s32[2,64]{1,0:T(2,128)S(1)} %pad_add_fusion.refs_1_, s32[64]{0:T(128)S(1)} %get-tuple-element.28.refs_2_, s32[64]{0:T(128)S(1)} %get-tuple-element.27.refs_3_, s32[64]{0:T(128)S(1)} %get-tuple-element.26.refs_4_, ...), custom_call_target="tpu_custom_call" | custom-call | flops 3355443200 | bytes 3840000 | tf_op jit(solution)/shard_map/scores/pallas_call | solution.py:373
  52.1 5.5 %all-to-all-start.1 = ((s16[8,528,128]{2,1,0:T(8,128)(2,1)}), s16[8,528,128]{2,1,0:T(8,128)(2,1)S(1)}, u32[]{:S(2)}, u32[]{:S(2)}) async-start(s16[8,528,128]{2,1,0:T(8,128)(2,1)} %get-tuple-element.21), calls=%async_computation.1 | async-start | bytes 2162688 | tf_op jit(solution)/shard_map/all_to_all | solution.py:498
  57.7 26.3 %all-to-all-done.1.codes = s16[8,528,128]{2,1,0:T(8,128)(2,1)S(1)} async-done(((s16[8,528,128]{2,1,0:T(8,128)(2,1)}), s16[8,528,128]{2,1,0:T(8,128)(2,1)S(1)}, u32[]{:S(2)}, u32[]{:S(2)}) %all-to-all-start.1) | async-done | bytes 1081376 | tf_op jit(solution)/shard_map/all_to_all | solution.py:498
  84.0 1.3 %average.1 = (f32[32,4096]{1,0:T(8,128)S(1)}, f32[8,4096]{1,0:T(8,128)S(1)}, f32[8,4096]{1,0:T(8,128)S(1)}) custom-call(s16[8,528,128]{2,1,0:T(8,128)(2,1)S(1)} %all-to-all-done.1.codes), custom_call_target="tpu_custom_call" | custom-call | tf_op jit(solution)/shard_map/average/pallas_call | solution.py:401
  85.3 1.0 %collective-permute-start.5 = (f32[8,4096]{1,0:T(8,128)S(1)}, f32[8,4096]{1,0:T(8,128)S(1)}, u32[]{:S(2)}, u32[]{:S(2)}) collective-permute-start(f32[8,4096]{1,0:T(8,128)S(1)} %get-tuple-element.35), channel_id=1, source_target_pairs={{0,1},{1,0},{2,3},{3,2},{4,5},{5,4},{6,7},{7,6},{8,9},{9,8},{10,11... | collective-permute-start | bytes 393224 | tf_op jit(solution)/shard_map/ppermute | solution.py:501
  86.3 1.9 %collective-permute-start.6 = (f32[8,4096]{1,0:T(8,128)S(1)}, f32[8,4096]{1,0:T(8,128)S(1)}, u32[]{:S(2)}, u32[]{:S(2)}) collective-permute-start(f32[8,4096]{1,0:T(8,128)S(1)} %get-tuple-element.34), channel_id=1, source_target_pairs={{1,4},{5,8},{9,12},{4,1},{8,5},{12,9},{3,6},{7,10},{11,14},{6,3},{... | collective-permute-start | bytes 393224 | tf_op jit(solution)/shard_map/ppermute | solution.py:504
  88.3 4.3 %collective-permute-done.6.outer = f32[8,4096]{1,0:T(8,128)S(1)} collective-permute-done((f32[8,4096]{1,0:T(8,128)S(1)}, f32[8,4096]{1,0:T(8,128)S(1)}, u32[]{:S(2)}, u32[]{:S(2)}) %collective-permute-start.6) | collective-permute-done | bytes 131104 | tf_op jit(solution)/shard_map/ppermute | solution.py:504
  92.6 0.8 finish.1
  (38 shorter events, 6.3 us)
Async XLA Ops:
  0.0 0.9 %copy-start = (bf16[1,32,4096]{2,1,0:T(8,128)(2,1)S(1)}, bf16[1,32,4096]{2,1,0:T(8,128)(2,1)}, u32[]{:S(2)}) copy-start(bf16[1,32,4096]{2,1,0:T(8,128)(2,1)} %param.12) | copy-start | bytes 786436
  2.0 31.5 %collective-permute-start.1 = (bf16[8,32,128]{2,1,0:T(8,128)(2,1)S(1)}, bf16[8,32,128]{2,1,0:T(8,128)(2,1)}, u32[]{:S(2)}, u32[]{:S(2)}) collective-permute-start(bf16[8,32,128]{2,1,0:T(8,128)(2,1)S(1)} %get-tuple-element.18), channel_id=1, source_target_pairs={{0,4},{4,8},{8,12},{12,0},{1,5},{5,9},{9,13},{13,1},{2,6},{6,10},{... | collective-permute-start | bytes 196616 | tf_op jit(solution)/shard_map/ppermute | solution.py:457
  4.1 30.2 %collective-permute-start.2 = (bf16[8,32,128]{2,1,0:T(8,128)(2,1)S(1)}, bf16[8,32,128]{2,1,0:T(8,128)(2,1)}, u32[]{:S(2)}, u32[]{:S(2)}) collective-permute-start(bf16[8,32,128]{2,1,0:T(8,128)(2,1)S(1)} %get-tuple-element.18), channel_id=1, source_target_pairs={{0,8},{4,12},{8,0},{12,4},{1,9},{5,13},{9,1},{13,5},{2,10},{6,14},... | collective-permute-start | bytes 196616 | tf_op jit(solution)/shard_map/ppermute | solution.py:457
  6.4 28.7 %collective-permute-start.3 = (bf16[8,32,128]{2,1,0:T(8,128)(2,1)S(1)}, bf16[8,32,128]{2,1,0:T(8,128)(2,1)}, u32[]{:S(2)}, u32[]{:S(2)}) collective-permute-start(bf16[8,32,128]{2,1,0:T(8,128)(2,1)S(1)} %get-tuple-element.18), channel_id=1, source_target_pairs={{0,12},{4,0},{8,4},{12,8},{1,13},{5,1},{9,5},{13,9},{2,14},{6,2},{... | collective-permute-start | bytes 196616 | tf_op jit(solution)/shard_map/ppermute | solution.py:457
  7.5 23.6 %all-to-all-start = ((bf16[4,768,128]{2,1,0:T(8,128)(2,1)}), bf16[4,768,128]{2,1,0:T(8,128)(2,1)S(1)}, u32[]{:S(2)}, u32[]{:S(2)}) async-start(bf16[4,768,128]{2,1,0:T(8,128)(2,1)} %bitcast.13), calls=%async_computation | async-start | bytes 1572864 | tf_op jit(solution)/shard_map/all_to_all | solution.py:454
  14.3 2.9 %copy-start.9 = (s32[1,64,1]{1,2,0:T(1,128)S(1)}, s32[1,64,1]{1,2,0:T(1,128)}, u32[]{:S(2)}) copy-start(s32[1,64,1]{1,2,0:T(1,128)} %param.14) | copy-start | bytes 772
  14.3 3.1 %copy-start.10 = (s32[1,64]{1,0:T(1,128)S(1)}, s32[1,64]{1,0:T(1,128)}, u32[]{:S(2)}) copy-start(s32[1,64]{1,0:T(1,128)} %param.15) | copy-start | bytes 772
  14.3 3.8 %copy-start.3 = (bf16[256,256]{1,0:T(8,128)(2,1)S(1)}, bf16[256,256]{1,0:T(8,128)(2,1)}, u32[]{:S(2)}) copy-start(bf16[256,256]{1,0:T(8,128)(2,1)} %constant.92.clone.window_lanes) | copy-start | bytes 393220
  18.1 0.9 copy-start.4
  19.0 0.8 copy-start.7
  19.8 0.8 copy-start.8
  20.6 15.5 %copy-start.1 = (bf16[384,512]{1,0:T(8,128)(2,1)S(1)}, bf16[384,512]{1,0:T(8,128)(2,1)}, u32[]{:S(2)}) copy-start(bf16[384,512]{1,0:T(8,128)(2,1)} %constant.94.clone.refs_9_) | copy-start | bytes 1179652
  20.6 15.5 %copy-start.5 = (bf16[128,192]{1,0:T(8,128)(2,1)S(1)}, bf16[128,192]{1,0:T(8,128)(2,1)}, u32[]{:S(2)}) copy-start(bf16[128,192]{1,0:T(8,128)(2,1)} %constant.95.clone.refs_10_) | copy-start | bytes 147460
  31.1 5.0 %collective-permute-start = (bf16[96,32,128]{2,1,0:T(8,128)(2,1)S(1)}, bf16[96,32,128]{2,1,0:T(8,128)(2,1)S(1)}, u32[]{:S(2)}, u32[]{:S(2)}) collective-permute-start(bf16[96,32,128]{2,1,0:T(8,128)(2,1)S(1)} %bitcast.42), channel_id=1, source_target_pairs={{0,1},{1,0},{2,3},{3,2},{4,5},{5,4},{6,7},{7,6},{8,9},{9,8},{10,11... | collective-permute-start | bytes 2359304 | tf_op jit(solution)/shard_map/ppermute | solution.py:464
  36.0 10.7 %collective-permute-start.4 = (bf16[32,32,128]{2,1,0:T(8,128)(2,1)S(1)}, bf16[32,32,128]{2,1,0:T(8,128)(2,1)S(1)}, u32[]{:S(2)}, u32[]{:S(2)}) collective-permute-start(bf16[32,32,128]{2,1,0:T(8,128)(2,1)S(1)} %constant_dynamic-update-slice_fusion.refs_15_), channel_id=1, source_target_pairs={{0,1},{1,0},{2,3},{3,2},{4,5},{5,4},{6,7},{7,6},{8,9},{9,8},{10,11... | collective-permute-start | bytes 786440 | tf_op jit(solution)/shard_map/ppermute | solution.py:464
  36.1 1.0 %copy-start.2 = (bf16[512,256]{1,0:T(8,128)(2,1)S(1)}, bf16[512,256]{1,0:T(8,128)(2,1)}, u32[]{:S(2)}) copy-start(bf16[512,256]{1,0:T(8,128)(2,1)} %constant.97.clone.refs_12_) | copy-start | bytes 786436
  37.1 0.8 copy-start.6
  52.1 31.8 %all-to-all-start.1 = ((s16[8,528,128]{2,1,0:T(8,128)(2,1)}), s16[8,528,128]{2,1,0:T(8,128)(2,1)S(1)}, u32[]{:S(2)}, u32[]{:S(2)}) async-start(s16[8,528,128]{2,1,0:T(8,128)(2,1)} %get-tuple-element.21), calls=%async_computation.1 | async-start | bytes 2162688 | tf_op jit(solution)/shard_map/all_to_all | solution.py:498
  85.3 3.0 %collective-permute-start.5 = (f32[8,4096]{1,0:T(8,128)S(1)}, f32[8,4096]{1,0:T(8,128)S(1)}, u32[]{:S(2)}, u32[]{:S(2)}) collective-permute-start(f32[8,4096]{1,0:T(8,128)S(1)} %get-tuple-element.35), channel_id=1, source_target_pairs={{0,1},{1,0},{2,3},{3,2},{4,5},{5,4},{6,7},{7,6},{8,9},{9,8},{10,11... | collective-permute-start | bytes 393224 | tf_op jit(solution)/shard_map/ppermute | solution.py:501
  86.3 6.3 %collective-permute-start.6 = (f32[8,4096]{1,0:T(8,128)S(1)}, f32[8,4096]{1,0:T(8,128)S(1)}, u32[]{:S(2)}, u32[]{:S(2)}) collective-permute-start(f32[8,4096]{1,0:T(8,128)S(1)} %get-tuple-element.34), channel_id=1, source_target_pairs={{1,4},{5,8},{9,12},{4,1},{8,5},{12,9},{3,6},{7,10},{11,14},{6,3},{... | collective-permute-start | bytes 393224 | tf_op jit(solution)/shard_map/ppermute | solution.py:504

commit v6 on v4

--- a/solution.py
+++ b/solution.py
@@ -145,7 +145,6 @@
 
     @pl.when(step == 0)
     def _():
-        out[...] = jnp.zeros_like(out)
         marks[...] = jnp.zeros_like(marks)
 
     raws = []
@@ -239,9 +238,7 @@
     @pl.when(step == pl.num_programs(0) - 1)
     def _():
         for to in range(out.shape[0]):
-            notes = marks[to]
-            notes = jnp.concatenate([notes, jnp.zeros_like(notes)], axis=0)
-            out[to, body:, :] = notes.astype(jnp.int32).astype(jnp.int16)
+            out[to, body:, :] = marks[to].astype(jnp.int32).astype(jnp.int16)
 
 
 def average_kernel(capacity, chip_amount, codes, smooth, first, last, values):
@@ -290,24 +287,24 @@
 
 
 def spread_kernel(chips, sent):
-    chip_amount = chips.shape[0]
-    for first in range(0, chip_amount, 8):
-        for row in range(0, ROWS, 8):
-            lanes = [chips[first:first + 8, (row + i) * WIN:(row + i + 1) * WIN].astype(f32) for i in range(8)]
-            turned = jnp.swapaxes(jnp.stack(lanes, axis=0), 0, 1).astype(bf16)
-            for to in range(sent.shape[0]):
-                sent[to, first:first + 8, row:row + 8, :] = turned
+    base = pl.program_id(0) * 8
+    for row in range(0, ROWS, 8):
+        lanes = [chips[:, (row + i) * WIN:(row + i + 1) * WIN].astype(f32) for i in range(8)]
+        turned = jnp.swapaxes(jnp.stack(lanes, axis=0), 0, 1).astype(bf16)
+        for to in range(sent.shape[0]):
+            sent[to, pl.ds(base, 8), row:row + 8, :] = turned
 
 
 def spread(chips, tiles):
     return pl.pallas_call(
         spread_kernel,
-        in_specs=[resident()],
+        grid=(chips.shape[0] // 8,),
+        in_specs=[pl.BlockSpec((8, chips.shape[1]), lambda i: (i, 0))],
         out_specs=resident(),
         out_shape=pltpu.VMEM((tiles, chips.shape[0], ROWS, WIN), bf16),
         compiler_params=pltpu.CompilerParams(vmem_limit_bytes=VMEM_GRANT),
         name="spread",
-    )(chips)
+    )(away(chips))
 
 
 def prepare_windows(images, table):
@@ -338,7 +335,7 @@
     amount = spectra.shape[0]
     group = min(SCORE_GROUP, amount)
     constants = [jnp.asarray(table[k]) for k in ("chip_lanes", "chip_rows", "inverse_rows", "inverse_lanes")]
-    shape = (devices, capacity * ROWS + 16, WIN)
+    shape = (devices, capacity * ROWS + 8, WIN)
     return pl.pallas_call(
         functools.partial(score_kernel, capacity),
         grid_spec=pltpu.PrefetchScalarGridSpec(
@@ -362,7 +359,7 @@
         out_shape=pltpu.VMEM(shape, jnp.int16),
         compiler_params=pltpu.CompilerParams(vmem_limit_bytes=VMEM_GRANT),
         name="scores",
-    )(*scalars, away(spectra), away(scale), *[away(c) for c in constants], *[near(source) for source in sources])
+    )(*scalars, away(spectra), away(scale), *[near(c) for c in constants], *[near(source) for source in sources])
 
 
 def average_scores(codes, capacity, chip_amount):

time: 97.7 us -> 97.9 us (level)
  Pallas kernels: 24.8 us -> 26.2 us
    pallas_call x1, Pallas kernels: 0.16 us -> 1.87 us  [spread(): pl.pallas_call(spread_kernel, grid=(chips.shape[0] // 8,), in_specs=[pl.B...]
    unnamed x15 -> x21, local copies, waits for them, and re-layouts: 3.22 us -> 2.29 us
where the time goes in v6:
time: 97.9 us; the launch traced here: 97.6 us
  waiting for transfers between devices  30.3 us (31%)
  blocking collectives  30.1 us (31%)
  Pallas kernels  26.2 us (27%)
  starting transfers between devices  8.2 us (8%)
  local copies, waits for them, and re-layouts  2.29 us (2%)
    all_to_all x1, blocking collectives, on_device(): lax.all_to_all(sent, 'tile', split_axis=0, concat_axis=0, tiled=True)  30.1 us
    all_to_all x1, waiting for transfers between devices, on_device(): lax.all_to_all(codes, ('tile', 'sub'), split_axis=0, concat_axis=0, tiled...  26 us
    pallas_call x1, Pallas kernels, score_windows(): pl.pallas_call(functools.partial(score_kernel, capacity), grid_spec=pltpu...  12.3 us
    pallas_call x1, Pallas kernels, prepare_windows(): pl.pallas_call(window_kernel, grid=(amount // group,), in_specs=[pl.Block...  9.97 us
    ppermute x1, waiting for transfers between devices, on_device(): lax.ppermute(jnp.where(sub == 0, first, last), ('tile', 'sub'), ups + downs)  4.35 us
    all_to_all x1, starting transfers between devices, on_device(): lax.all_to_all(codes, ('tile', 'sub'), split_axis=0, concat_axis=0, tiled...  3.51 us
    unnamed x21, local copies, waits for them, and re-layouts  2.29 us
  transfers between devices with their start and end apart: 4, of which 2 were waited for; matrix products, arithmetic and copies ran while one was open for 2% of the time, Pallas kernels for 10%

profile of v6, /device:TPU:1, one launch (start us, length us, event | category | flops | bytes accessed | tf_op | source)
XLA Modules:
  0.0 97.6 jit_solution(10042385525284646892)
XLA Ops:
  0.0 1.9 %spread.1 = bf16[4,32,32,128]{3,2,1,0:T(8,128)(2,1)S(1)} custom-call(bf16[32,4096]{1,0:T(8,128)(2,1)} %bitcast.26), custom_call_target="tpu_custom_call" | custom-call | tf_op jit(solution)/shard_map/spread/pallas_call | solution.py:299
  1.9 30.1 %all_to_all.10 = bf16[4,1024,128]{2,1,0:T(8,128)(2,1)S(1)} all-to-all(bf16[4,1024,128]{2,1,0:T(8,128)(2,1)S(1)} %bitcast.18), channel_id=1, replica_groups=mesh['groups'=2,'tile'=4,'pair'=2,'sub'=2] {'tile'}, dimensions={0} | all-to-all | bytes 2097152 | tf_op jit(solution)/shard_map/all_to_all | solution.py:419
  32.0 1.8 %collective-permute-start = (bf16[128,32,128]{2,1,0:T(8,128)(2,1)S(1)}, bf16[128,32,128]{2,1,0:T(8,128)(2,1)}, u32[]{:S(2)}, u32[]{:S(2)}) collective-permute-start(bf16[128,32,128]{2,1,0:T(8,128)(2,1)S(1)} %bitcast.19), channel_id=1, source_target_pairs={{0,1},{1,0},{2,3},{3,2},{4,5},{5,4},{6,7},{7,6},{8,9},{9,8},{10,11... | collective-permute-start | bytes 3145736 | tf_op jit(solution)/shard_map/ppermute | solution.py:425
  33.8 0.0 copy-start.8
  33.8 0.0 copy-start.9
  33.8 2.2 %copy.13 = bf16[8,8,128,128]{3,2,1,0:T(8,128)(2,1)S(1)} copy(bf16[8,8,128,128]{3,1,2,0:T(8,128)(2,1)} %bitcast.25) | data formatting | bytes 4194304
  36.1 0.0 copy-done.5
  36.1 0.2 convert_reduce_fusion.ranks
  36.2 0.0 copy-done.4
  36.3 0.0 copy-start
  36.3 0.0 copy-start.1
  36.3 0.0 copy-start.2
  36.4 0.0 copy-start.3
  36.4 10.0 %window_spectra.1 = (f32[64,128,128]{2,1,0:T(8,128)}, f32[64,32,128]{2,1,0:T(8,128)}) custom-call(bf16[64,128,128]{2,1,0:T(8,128)(2,1)S(1)} %bitcast.21, bf16[320,128]{1,0:T(8,128)(2,1)S(1)} %copy-done.7, bf16[64,256]{1,0:T(8,128)(2,1)S(1)} %copy-done.9, bf16[256,256]{1,0:T(8,128)(2,1)S(1)} %copy-done.6, bf16[256,128]{1,0:T(8,128)(2,1)S(1)} %copy-done.8), custom_call_target="tpu_custom_call" | custom-call | flops 7549747200 | bytes 7680000 | tf_op jit(solution)/shard_map/window_spectra/pallas_call | solution.py:314
  46.3 0.0 collective-permute-done.rest_1_
  46.4 12.3 %scores.1 = s16[8,520,128]{2,1,0:T(8,128)(2,1)} custom-call(s32[64]{0:T(128)S(1)} %get-tuple-element.18.choice, s32[64]{0:T(128)S(1)} %get-tuple-element.17.place, s32[64]{0:T(128)S(1)} %bitcast.24, s32[64]{0:T(128)S(1)} %convert_reduce_fusion.ranks, s32[64]{0:T(128)S(1)} %bitcast.22, s32[1]{0:T(128)} %bitcast.3.position, ...), custom_call_target="tpu_custom_call" | custom-call | tf_op jit(solution)/shard_map/scores/pallas_call | solution.py:339
  58.6 3.5 %all-to-all-start.1 = ((s16[8,520,128]{2,1,0:T(8,128)(2,1)}), s16[8,520,128]{2,1,0:T(8,128)(2,1)S(1)}, u32[]{:S(2)}, u32[]{:S(2)}) async-start(s16[8,520,128]{2,1,0:T(8,128)(2,1)} %scores.1), calls=%async_computation.1 | async-start | bytes 2129920 | tf_op jit(solution)/shard_map/all_to_all | solution.py:437
  62.2 26.0 %all-to-all-done.1.codes = s16[8,520,128]{2,1,0:T(8,128)(2,1)S(1)} async-done(((s16[8,520,128]{2,1,0:T(8,128)(2,1)}), s16[8,520,128]{2,1,0:T(8,128)(2,1)S(1)}, u32[]{:S(2)}, u32[]{:S(2)}) %all-to-all-start.1) | async-done | bytes 1064992 | tf_op jit(solution)/shard_map/all_to_all | solution.py:437
  88.1 1.3 %average.1 = (f32[32,4096]{1,0:T(8,128)S(1)}, f32[8,4096]{1,0:T(8,128)S(1)}, f32[8,4096]{1,0:T(8,128)S(1)}) custom-call(s16[8,520,128]{2,1,0:T(8,128)(2,1)S(1)} %all-to-all-done.1.codes), custom_call_target="tpu_custom_call" | custom-call | tf_op jit(solution)/shard_map/average/pallas_call | solution.py:367
  89.4 1.0 %collective-permute-start.1 = (f32[8,4096]{1,0:T(8,128)S(1)}, f32[8,4096]{1,0:T(8,128)S(1)}, u32[]{:S(2)}, u32[]{:S(2)}) collective-permute-start(f32[8,4096]{1,0:T(8,128)S(1)} %get-tuple-element.16), channel_id=1, source_target_pairs={{0,1},{1,0},{2,3},{3,2},{4,5},{5,4},{6,7},{7,6},{8,9},{9,8},{10,11... | collective-permute-start | bytes 393224 | tf_op jit(solution)/shard_map/ppermute | solution.py:440
  90.5 1.9 %collective-permute-start.2 = (f32[8,4096]{1,0:T(8,128)S(1)}, f32[8,4096]{1,0:T(8,128)S(1)}, u32[]{:S(2)}, u32[]{:S(2)}) collective-permute-start(f32[8,4096]{1,0:T(8,128)S(1)} %get-tuple-element.15), channel_id=1, source_target_pairs={{1,4},{5,8},{9,12},{4,1},{8,5},{12,9},{3,6},{7,10},{11,14},{6,3},{... | collective-permute-start | bytes 393224 | tf_op jit(solution)/shard_map/ppermute | solution.py:443
  92.4 0.0 collective-permute-done.1.inner
  92.4 4.3 %collective-permute-done.2.outer = f32[8,4096]{1,0:T(8,128)S(1)} collective-permute-done((f32[8,4096]{1,0:T(8,128)S(1)}, f32[8,4096]{1,0:T(8,128)S(1)}, u32[]{:S(2)}, u32[]{:S(2)}) %collective-permute-start.2) | collective-permute-done | bytes 131104 | tf_op jit(solution)/shard_map/ppermute | solution.py:443
  96.7 0.8 finish.1
  (14 shorter events, 0.1 us)
Async XLA Ops:
  32.0 14.3 %collective-permute-start = (bf16[128,32,128]{2,1,0:T(8,128)(2,1)S(1)}, bf16[128,32,128]{2,1,0:T(8,128)(2,1)}, u32[]{:S(2)}, u32[]{:S(2)}) collective-permute-start(bf16[128,32,128]{2,1,0:T(8,128)(2,1)S(1)} %bitcast.19), channel_id=1, source_target_pairs={{0,1},{1,0},{2,3},{3,2},{4,5},{5,4},{6,7},{7,6},{8,9},{9,8},{10,11... | collective-permute-start | bytes 3145736 | tf_op jit(solution)/shard_map/ppermute | solution.py:425
  33.8 2.3 %copy-start.5 = (s32[1,64,1]{1,2,0:T(1,128)S(1)}, s32[1,64,1]{1,2,0:T(1,128)}, u32[]{:S(2)}) copy-start(s32[1,64,1]{1,2,0:T(1,128)} %param.14) | copy-start | bytes 772
  33.8 2.5 %copy-start.4 = (s32[1,64]{1,0:T(1,128)S(1)}, s32[1,64]{1,0:T(1,128)}, u32[]{:S(2)}) copy-start(s32[1,64]{1,0:T(1,128)} %param.15) | copy-start | bytes 772
  33.8 2.5 %copy-start.6 = (bf16[256,256]{1,0:T(8,128)(2,1)S(1)}, bf16[256,256]{1,0:T(8,128)(2,1)}, u32[]{:S(2)}) copy-start(bf16[256,256]{1,0:T(8,128)(2,1)} %constant.61.clone.window_lanes) | copy-start | bytes 393220
  33.8 2.5 %copy-start.7 = (bf16[320,128]{1,0:T(8,128)(2,1)S(1)}, bf16[320,128]{1,0:T(8,128)(2,1)}, u32[]{:S(2)}) copy-start(bf16[320,128]{1,0:T(8,128)(2,1)} %constant.59.clone.window_rows) | copy-start | bytes 245764
  33.8 2.5 %copy-start.8 = (bf16[256,128]{1,0:T(8,128)(2,1)S(1)}, bf16[256,128]{1,0:T(8,128)(2,1)}, u32[]{:S(2)}) copy-start(bf16[256,128]{1,0:T(8,128)(2,1)} %constant.62.clone.band_lanes) | copy-start | bytes 196612
  33.8 2.5 %copy-start.9 = (bf16[64,256]{1,0:T(8,128)(2,1)S(1)}, bf16[64,256]{1,0:T(8,128)(2,1)}, u32[]{:S(2)}) copy-start(bf16[64,256]{1,0:T(8,128)(2,1)} %constant.60.clone.square_rows) | copy-start | bytes 98308
  36.3 10.0 %copy-start = (bf16[384,512]{1,0:T(8,128)(2,1)S(1)}, bf16[384,512]{1,0:T(8,128)(2,1)}, u32[]{:S(2)}) copy-start(bf16[384,512]{1,0:T(8,128)(2,1)} %constant.63.clone.chip_lanes) | copy-start | bytes 1179652
  36.3 10.0 %copy-start.1 = (bf16[512,256]{1,0:T(8,128)(2,1)S(1)}, bf16[512,256]{1,0:T(8,128)(2,1)}, u32[]{:S(2)}) copy-start(bf16[512,256]{1,0:T(8,128)(2,1)} %constant.66.clone.inverse_lanes) | copy-start | bytes 786436
  36.3 10.0 %copy-start.2 = (bf16[128,192]{1,0:T(8,128)(2,1)S(1)}, bf16[128,192]{1,0:T(8,128)(2,1)}, u32[]{:S(2)}) copy-start(bf16[128,192]{1,0:T(8,128)(2,1)} %constant.64.clone.chip_rows) | copy-start | bytes 147460
  36.4 10.0 %copy-start.3 = (bf16[128,256]{1,0:T(8,128)(2,1)S(1)}, bf16[128,256]{1,0:T(8,128)(2,1)}, u32[]{:S(2)}) copy-start(bf16[128,256]{1,0:T(8,128)(2,1)} %constant.65.clone.inverse_rows) | copy-start | bytes 196612
  58.6 29.5 %all-to-all-start.1 = ((s16[8,520,128]{2,1,0:T(8,128)(2,1)}), s16[8,520,128]{2,1,0:T(8,128)(2,1)S(1)}, u32[]{:S(2)}, u32[]{:S(2)}) async-start(s16[8,520,128]{2,1,0:T(8,128)(2,1)} %scores.1), calls=%async_computation.1 | async-start | bytes 2129920 | tf_op jit(solution)/shard_map/all_to_all | solution.py:437
  89.4 3.0 %collective-permute-start.1 = (f32[8,4096]{1,0:T(8,128)S(1)}, f32[8,4096]{1,0:T(8,128)S(1)}, u32[]{:S(2)}, u32[]{:S(2)}) collective-permute-start(f32[8,4096]{1,0:T(8,128)S(1)} %get-tuple-element.16), channel_id=1, source_target_pairs={{0,1},{1,0},{2,3},{3,2},{4,5},{5,4},{6,7},{7,6},{8,9},{9,8},{10,11... | collective-permute-start | bytes 393224 | tf_op jit(solution)/shard_map/ppermute | solution.py:440
  90.5 6.3 %collective-permute-start.2 = (f32[8,4096]{1,0:T(8,128)S(1)}, f32[8,4096]{1,0:T(8,128)S(1)}, u32[]{:S(2)}, u32[]{:S(2)}) collective-permute-start(f32[8,4096]{1,0:T(8,128)S(1)} %get-tuple-element.15), channel_id=1, source_target_pairs={{1,4},{5,8},{9,12},{4,1},{8,5},{12,9},{3,6},{7,10},{11,14},{6,3},{... | collective-permute-start | bytes 393224 | tf_op jit(solution)/shard_map/ppermute | solution.py:443

commit v7 on v4

--- a/solution.py
+++ b/solution.py
@@ -103,10 +103,11 @@
     return (high, middle, low)
 
 
-def window_kernel(windows, window_rows, square_rows, window_lanes, band_lanes, spectra, scale):
-    group = windows.shape[0]
+def window_kernel(order, windows, window_rows, square_rows, window_lanes, band_lanes, spectra, scale):
+    group = spectra.shape[0]
+    base = pl.program_id(0) * group
     for first in range(0, group, 2):
-        image = jnp.concatenate([windows[first], windows[first + 1]], axis=1)
+        image = jnp.concatenate([windows[order[base + first]], windows[order[base + first + 1]]], axis=1)
         rows = dot(window_rows[...], image)
         spec_rows = rows[:WIN] + rows[WIN:2 * WIN]
         sums = rows[2 * WIN:]
@@ -131,22 +132,28 @@
             scale[first + part] = lax.rsqrt(variance + epsilon)
 
 
-def score_kernel(
-    capacity, choice, place, target, ranks, slots, position,
-    spectra, scale, chip_lanes, chip_rows, inverse_rows, inverse_lanes, *rest,
-):
-    *sources, out, marks, lefts, lines, packs, pairs, products, backs = rest
+def score_kernel(capacity, quick, opening, *refs):
+    (choice, place, target, ranks, slots, position,
+     spectra, scale, chip_lanes, chip_rows, inverse_rows, inverse_lanes, *rest) = refs
+    *rest, lefts, lines, packs, pairs, products, backs, marks, stage, note_stage, sems, note_sem = rest
+    if opening:
+        *sources, early_codes, late_codes, marks_out = rest
+    else:
+        *sources, _, marks_in, late_codes = rest
     step = pl.program_id(0)
+    steps = pl.num_programs(0)
     group = lefts.shape[0] // ROWS
-    base = step * group
-    body = capacity * ROWS
+    devices = late_codes.shape[0]
+    first_step = 0 if opening else position[1]
+    base = (step + first_step) * group
     lane = lax.broadcasted_iota(jnp.int32, (8, WIN), 1)
     line = lax.broadcasted_iota(jnp.int32, (8, WIN), 0)
 
     @pl.when(step == 0)
     def _():
-        out[...] = jnp.zeros_like(out)
         marks[...] = jnp.zeros_like(marks)
+        if not opening:
+            marks[devices:] = marks_in[...]
 
     raws = []
     for part in range(group):
@@ -229,32 +236,56 @@
         root = size * lax.rsqrt(size) * CODE
         root = jnp.minimum(root, CODE)
         code = jnp.round(jnp.where(score < 0, -root, root)).astype(jnp.int32).astype(jnp.int16)
-        to = target[window]
-        out[to, pl.ds(pl.multiple_of(ranks[window] * ROWS, ROWS), ROWS), :] = code
-        here = lane == position[0] * capacity + ranks[window]
+        stage[step * group + part] = code
+        to = target[window] + jnp.where(ranks[window] < quick, 0, devices)
+        here = (lane == position[0] * capacity + ranks[window]) & (line < 2)
         named = (slots[window] + 1).astype(f32)
-        mark = jnp.where(line == 0, named, jnp.where(line == 1, power[part:part + 1], 0.0))
-        marks[to] = marks[to] + jnp.where(here, mark, 0.0)
-
-    @pl.when(step == pl.num_programs(0) - 1)
+        mark = jnp.where(line == 0, named, power[part:part + 1])
+        marks[to] = jnp.where(here, mark, marks[to])
+
+    def copy_out(part, codes, rank):
+        rows = pl.ds(pl.multiple_of(rank * ROWS, ROWS), ROWS)
+        index = step * group + part
+        return pltpu.make_async_copy(stage.at[index], codes.at[target[base + part], rows, :], sems.at[index])
+
+    for part in range(group):
+        rank = ranks[base + part]
+        if opening:
+            @pl.when(rank < quick)
+            def _():
+                copy_out(part, early_codes, rank).start()
+
+            @pl.when(rank >= quick)
+            def _():
+                copy_out(part, late_codes, rank - quick).start()
+        else:
+            copy_out(part, late_codes, rank - quick).start()
+
+    @pl.when(step == steps - 1)
     def _():
-        for to in range(out.shape[0]):
-            notes = marks[to]
-            notes = jnp.concatenate([notes, jnp.zeros_like(notes)], axis=0)
-            out[to, body:, :] = notes.astype(jnp.int32).astype(jnp.int16)
-
-
-def average_kernel(capacity, chip_amount, codes, smooth, first, last, values):
-    devices = codes.shape[0]
-    body = capacity * ROWS
+        codes = early_codes if opening else late_codes
+        own = marks[:devices] if opening else marks[devices:]
+        note_stage[...] = own.astype(jnp.int32).astype(jnp.int16)
+        if opening:
+            marks_out[...] = marks[devices:]
+        count = codes.shape[1] - 8
+        notes = pltpu.make_async_copy(note_stage, codes.at[:, count:, :], note_sem)
+        notes.start()
+        for index in range(stage.shape[0]):
+            pltpu.make_async_copy(stage.at[index], late_codes.at[0, :ROWS, :], sems.at[index]).wait()
+        notes.wait()
+
+
+def average_kernel(capacity, quick, chip_amount, early_codes, late_codes, smooth, first, last, values):
+    devices = early_codes.shape[0]
     slots = devices * capacity
-    notes = codes[0, body:, :].astype(jnp.int32).astype(f32)
-    for source in range(1, devices):
-        notes = notes + codes[source, body:, :].astype(jnp.int32).astype(f32)
-    for source in range(devices):
-        wide = codes[source, :body, :].astype(jnp.int32).astype(f32)
-        turned = jnp.swapaxes((wide * jnp.abs(wide)).reshape(capacity, ROWS, WIN), 0, 1)
-        values[:, source * capacity:(source + 1) * capacity, :] = turned
+    notes = jnp.zeros((8, WIN), f32)
+    for codes, start, count in ((early_codes, 0, quick), (late_codes, quick, capacity - quick)):
+        for source in range(devices):
+            notes = notes + codes[source, count * ROWS:, :].astype(jnp.int32).astype(f32)
+            wide = codes[source, :count * ROWS, :].astype(jnp.int32).astype(f32)
+            turned = jnp.swapaxes((wide * jnp.abs(wide)).reshape(count, ROWS, WIN), 0, 1)
+            values[:, source * capacity + start:source * capacity + start + count, :] = turned
     chip = lax.broadcasted_iota(jnp.int32, (chip_amount, WIN), 0)
     hit = (notes[0:1] - 1.0).astype(jnp.int32) == chip
     looks = jnp.sum(hit.astype(f32), axis=1, keepdims=True)
@@ -310,18 +341,21 @@
     )(chips)
 
 
-def prepare_windows(images, table):
+def prepare_windows(images, order, table):
     amount = images.shape[0]
     group = min(GROUP, amount)
     constants = [jnp.asarray(table[k]) for k in ("window_rows", "square_rows", "window_lanes", "band_lanes")]
     return pl.pallas_call(
         window_kernel,
-        grid=(amount // group,),
-        in_specs=[pl.BlockSpec((group, WIN, WIN), lambda i: (i, 0, 0))] + [resident() for _ in constants],
-        out_specs=[
-            pl.BlockSpec((group, WIN, WIN), lambda i: (i, 0, 0)),
-            pl.BlockSpec((group, ROWS, WIN), lambda i: (i, 0, 0)),
-        ],
+        grid_spec=pltpu.PrefetchScalarGridSpec(
+            num_scalar_prefetch=1,
+            grid=(amount // group,),
+            in_specs=[resident()] + [resident() for _ in constants],
+            out_specs=[
+                pl.BlockSpec((group, WIN, WIN), lambda i, _: (i, 0, 0)),
+                pl.BlockSpec((group, ROWS, WIN), lambda i, _: (i, 0, 0)),
+            ],
+        ),
         out_shape=[
             pltpu.HBM((amount, WIN, WIN), f32),
             pltpu.HBM((amount, ROWS, WIN), f32),
@@ -331,45 +365,73 @@
         ),
         compiler_params=pltpu.CompilerParams(vmem_limit_bytes=VMEM_GRANT),
         name="window_spectra",
-    )(images, *constants)
-
-
-def score_windows(spectra, scale, sources, scalars, table, devices, capacity):
+    )(order, near(images), *constants)
+
+
+def score_windows(spectra, scale, sources, scalars, table, devices, capacity, quick, half, earlier):
     amount = spectra.shape[0]
-    group = min(SCORE_GROUP, amount)
+    group = min(SCORE_GROUP, half)
+    opening = earlier is None
+    steps = (half if opening else amount - half) // group
+    start = 0 if opening else half // group
     constants = [jnp.asarray(table[k]) for k in ("chip_lanes", "chip_rows", "inverse_rows", "inverse_lanes")]
-    shape = (devices, capacity * ROWS + 16, WIN)
+    count = len(scalars)
+    anywhere = pl.BlockSpec(memory_space=pl.ANY)
+    late = jax.ShapeDtypeStruct((devices, (capacity - quick) * ROWS + 8, WIN), jnp.int16)
+    if opening:
+        kept, kept_specs = [], []
+        out_specs = [anywhere, anywhere, resident()]
+        out_shape = [
+            jax.ShapeDtypeStruct((devices, quick * ROWS + 8, WIN), jnp.int16),
+            late,
+            jax.ShapeDtypeStruct((devices, 8, WIN), f32),
+        ]
+        aliases = {}
+    else:
+        kept, kept_specs = list(earlier), [anywhere, resident()]
+        out_specs, out_shape = [anywhere], [late]
+        aliases = {count + 6 + len(sources): 0}
+
+    def block(i, *_):
+        return (i + start, 0, 0)
+
     return pl.pallas_call(
-        functools.partial(score_kernel, capacity),
+        functools.partial(score_kernel, capacity, quick, opening),
         grid_spec=pltpu.PrefetchScalarGridSpec(
-            num_scalar_prefetch=len(scalars),
-            grid=(amount // group,),
-            in_specs=[
-                pl.BlockSpec((group, WIN, WIN), lambda i, *_: (i, 0, 0)),
-                pl.BlockSpec((group, ROWS, WIN), lambda i, *_: (i, 0, 0)),
-            ] + [resident() for _ in constants] + [resident() for _ in sources],
-            out_specs=resident(),
+            num_scalar_prefetch=count,
+            grid=(steps,),
+            in_specs=[pl.BlockSpec((group, WIN, WIN), block), pl.BlockSpec((group, ROWS, WIN), block)]
+            + [resident() for _ in constants] + [resident() for _ in sources] + kept_specs,
+            out_specs=out_specs,
             scratch_shapes=[
-                pltpu.VMEM((devices, 8, WIN), f32),
                 pltpu.VMEM((group * ROWS, 3 * WIN), bf16),
                 pltpu.VMEM((group * ROWS, 4 * WIN), f32),
                 pltpu.VMEM((group * ROWS, 4 * WIN), bf16),
                 pltpu.VMEM((group, WIN, 2 * WIN), f32),
                 pltpu.VMEM((group // 2, 2 * WIN, 2 * WIN), bf16),
                 pltpu.VMEM((group // 2, OFF, 2 * WIN), f32),
+                pltpu.VMEM((2 * devices, 8, WIN), f32),
+                pltpu.VMEM((steps * group, ROWS, WIN), jnp.int16),
+                pltpu.VMEM((devices, 8, WIN), jnp.int16),
+                pltpu.SemaphoreType.DMA((steps * group,)),
+                pltpu.SemaphoreType.DMA,
             ],
         ),
-        out_shape=pltpu.VMEM(shape, jnp.int16),
+        out_shape=out_shape,
+        input_output_aliases=aliases,
+        cost_estimate=pl.CostEstimate(
+            flops=steps * group * 1600 * 65536, transcendentals=0, bytes_accessed=steps * group * 90000
+        ),
         compiler_params=pltpu.CompilerParams(vmem_limit_bytes=VMEM_GRANT),
         name="scores",
-    )(*scalars, away(spectra), away(scale), *[away(c) for c in constants], *[near(source) for source in sources])
-
-
-def average_scores(codes, capacity, chip_amount):
-    devices = codes.shape[0]
+    )(*scalars, away(spectra), away(scale), *[near(c) for c in constants], *[near(p) for p in sources], *kept)
+
+
+def average_scores(early_codes, late_codes, capacity, quick, chip_amount):
+    devices = early_codes.shape[0]
     return pl.pallas_call(
-        functools.partial(average_kernel, capacity, chip_amount),
-        in_specs=[resident()],
+        functools.partial(average_kernel, capacity, quick, chip_amount),
+        in_specs=[resident(), resident()],
         out_specs=[resident(), resident(), resident()],
         out_shape=[
             pltpu.VMEM((chip_amount, OFF * OFF), f32),
@@ -379,7 +441,7 @@
         scratch_shapes=[pltpu.VMEM((ROWS, devices * capacity, WIN), f32)],
         compiler_params=pltpu.CompilerParams(vmem_limit_bytes=VMEM_GRANT),
         name="average",
-    )(near(codes))
+    )(near(early_codes), near(late_codes))
 
 
 def finish_kernel(turn, smooth, inner, outer, result):
@@ -421,24 +483,38 @@
     sent = spread(chips, tiles).reshape(tiles, chip_amount * ROWS, WIN)
     gathered = lax.all_to_all(sent, "tile", split_axis=0, concat_axis=0, tiled=True)
     gathered = gathered.reshape(tiles * chip_amount, ROWS, WIN)
-    spectra, scale = prepare_windows(images, table)
     sources = [gathered]
     for shift in range(1, subs):
         ring = [(i, (i - shift) % subs) for i in range(subs)]
         sources.append(lax.ppermute(gathered, "sub", ring))
 
+    group = min(SCORE_GROUP, window_amount // 2)
+    half = window_amount // group // 2 * group
+    quick = max(1, min(capacity - 1, half // devices))
     order = jnp.arange(window_amount, dtype=jnp.int32)
+    before = order[:, None] > order[None, :]
     matches = targets[:, None] == targets[None, :]
-    earlier = order[:, None] > order[None, :]
-    ranks = jnp.sum((matches & earlier).astype(jnp.int32), axis=1)
-    choice = (targets % subs - sub) % subs
-    place = (targets // subs) * chip_amount + slots
-    position = jnp.full((1,), lax.axis_index(("tile", "sub")), jnp.int32)
-    scalars = (choice, place, targets, ranks, slots, position)
-    codes = score_windows(spectra, scale, sources, scalars, table, devices, capacity)
-
-    received = lax.all_to_all(codes, ("tile", "sub"), split_axis=0, concat_axis=0, tiled=True)
-    smooth, first, last = average_scores(received, capacity, chip_amount)
+    ranks = jnp.sum((matches & before).astype(jnp.int32), axis=1)
+    late = (ranks >= quick).astype(jnp.int32)
+    ahead = (late[None, :] < late[:, None]) | ((late[None, :] == late[:, None]) & before)
+    chosen = jnp.sum(ahead.astype(jnp.int32), axis=1)[None, :] == order[:, None]
+
+    def sort(values):
+        return jnp.sum(jnp.where(chosen, values[None, :], 0), axis=1)
+
+    place = sort((targets // subs) * chip_amount + slots)
+    choice = sort((targets % subs - sub) % subs)
+    listing = sort(order)
+    spectra, scale = prepare_windows(images, listing, table)
+    own = lax.axis_index(("tile", "sub")).astype(jnp.int32)
+    position = jnp.stack([own, jnp.full_like(own, half // group)])
+    scalars = (choice, place, sort(targets), sort(ranks), sort(slots), position)
+    settings = (table, devices, capacity, quick, half)
+    early_codes, partial, marks = score_windows(spectra, scale, sources, scalars, *settings, None)
+    early_codes = lax.all_to_all(early_codes, ("tile", "sub"), split_axis=0, concat_axis=0, tiled=True)
+    (late_codes,) = score_windows(spectra, scale, sources, scalars, *settings, (partial, marks))
+    late_codes = lax.all_to_all(late_codes, ("tile", "sub"), split_axis=0, concat_axis=0, tiled=True)
+    smooth, first, last = average_scores(early_codes, late_codes, capacity, quick, chip_amount)
     if subs == 2:
         inner = lax.ppermute(jnp.where(sub == 0, last, first), "sub", [(0, 1), (1, 0)])
         ups = [(2 * i + 1, 2 * i + 2) for i in range(tiles - 1)]

time: 97.7 us -> 102 us (1.044)
  blocking collectives: 30.1 us -> 0 us
  waiting for transfers between devices: 30.7 us -> 51.2 us
  starting transfers between devices: 8.2 us -> 17.6 us
  Pallas kernels: 24.8 us -> 28.8 us
    all_to_all x1 -> x0, blocking collectives: 30.1 us -> none  [on_device(): lax.all_to_all(sent, 'tile', split_axis=0, concat_axis=0, tiled=True)]
    all_to_all x1 -> x3, waiting for transfers between devices: 26.3 us -> 46.8 us  [the longest x1 24.9 us: on_device(): lax.all_to_all(sent, 'tile', split_axis=0, concat_axis=0, tiled=True)]
    all_to_all x1 -> x3, starting transfers between devices: 3.51 us -> 13.3 us  [the longest x1 5.41 us: on_device(): lax.all_to_all(sent, 'tile', split_axis=0, concat_axis=0, tiled=True)]
    pallas_call x3 -> x4, Pallas kernels: 23.8 us -> 26.8 us  [the longest x2 14.8 us: score_windows(): pl.pallas_call(functools.partial(score_kernel, capacity, quick, opening),...]
    unnamed x15 -> x23, local copies, waits for them, and re-layouts: 3.22 us -> 3.22 us
  transfers between devices with their start and end apart: 4 -> 6, of which waited for: 2 -> 4; matrix products, arithmetic and copies ran while one was open for 2% -> 3% of each run, Pallas kernels for 10% -> 18%
where the time goes in v7:
time: 102 us
  waiting for transfers between devices  51.2 us (50%)
  Pallas kernels  28.8 us (28%)
  starting transfers between devices  17.6 us (17%)
  local copies, waits for them, and re-layouts  3.22 us (3%)
    all_to_all x1, waiting for transfers between devices, on_device(): lax.all_to_all(sent, 'tile', split_axis=0, concat_axis=0, tiled=True)  24.9 us
    all_to_all x1, waiting for transfers between devices, on_device(): lax.all_to_all(late_codes, ('tile', 'sub'), split_axis=0, concat_axis=0,...  20.4 us
    pallas_call x2, Pallas kernels, score_windows(): pl.pallas_call(functools.partial(score_kernel, capacity, quick, opening),...  14.8 us
    pallas_call x1, Pallas kernels, prepare_windows(): pl.pallas_call(window_kernel, grid_spec=pltpu.PrefetchScalarGridSpec(num_...  10.5 us
    all_to_all x1, starting transfers between devices, on_device(): lax.all_to_all(sent, 'tile', split_axis=0, concat_axis=0, tiled=True)  5.41 us
    all_to_all x1, starting transfers between devices, on_device(): lax.all_to_all(late_codes, ('tile', 'sub'), split_axis=0, concat_axis=0,...  4.51 us
    ppermute x1, waiting for transfers between devices, on_device(): lax.ppermute(jnp.where(sub == 0, first, last), ('tile', 'sub'), ups + downs)  4.35 us
    all_to_all x1, starting transfers between devices, on_device(): lax.all_to_all(early_codes, ('tile', 'sub'), split_axis=0, concat_axis=0,...  3.38 us
  transfers between devices with their start and end apart: 6, of which 4 were waited for; matrix products, arithmetic and copies ran while one was open for 3% of the time, Pallas kernels for 18%

profile of v7, /device:TPU:1, one launch (start us, length us, event | category | flops | bytes accessed | tf_op | source)
XLA Modules:
  0.0 101.7 jit_solution(14780956633538979233)
XLA Ops:
  0.0 1.0 copy-done
  1.0 1.1 %spread.1 = bf16[4,32,32,128]{3,2,1,0:T(8,128)(2,1)} custom-call(bf16[32,4096]{1,0:T(8,128)(2,1)S(1)} %bitcast.28), custom_call_target="tpu_custom_call" | custom-call | tf_op jit(solution)/shard_map/spread/pallas_call | solution.py:334
  2.1 5.4 %all-to-all-start = ((bf16[4,1024,128]{2,1,0:T(8,128)(2,1)}), bf16[4,1024,128]{2,1,0:T(8,128)(2,1)S(1)}, u32[]{:S(2)}, u32[]{:S(2)}) async-start(bf16[4,1024,128]{2,1,0:T(8,128)(2,1)} %bitcast.7), calls=%async_computation | async-start | bytes 2097152 | tf_op jit(solution)/shard_map/all_to_all | solution.py:484
  7.5 0.2 convert_reduce_fusion.1
  7.7 0.2 convert_reduce_fusion
  7.9 24.9 %all-to-all-done = bf16[4,1024,128]{2,1,0:T(8,128)(2,1)S(1)} async-done(((bf16[4,1024,128]{2,1,0:T(8,128)(2,1)}), bf16[4,1024,128]{2,1,0:T(8,128)(2,1)S(1)}, u32[]{:S(2)}, u32[]{:S(2)}) %all-to-all-start) | async-done | bytes 1048608 | tf_op jit(solution)/shard_map/all_to_all | solution.py:484
  32.8 1.4 %collective-permute-start = (bf16[128,32,128]{2,1,0:T(8,128)(2,1)S(1)}, bf16[128,32,128]{2,1,0:T(8,128)(2,1)S(1)}, u32[]{:S(2)}, u32[]{:S(2)}) collective-permute-start(bf16[128,32,128]{2,1,0:T(8,128)(2,1)S(1)} %bitcast.25), channel_id=1, source_target_pairs={{0,1},{1,0},{2,3},{3,2},{4,5},{5,4},{6,7},{7,6},{8,9},{9,8},{10,11... | collective-permute-start | bytes 3145736 | tf_op jit(solution)/shard_map/ppermute | solution.py:489
  34.2 0.1 pad_add_fusion.refs_5_
  34.3 0.0 copy-start.8
  34.3 2.2 %copy.14 = bf16[8,8,128,128]{3,2,1,0:T(8,128)(2,1)S(1)} copy(bf16[8,8,128,128]{3,1,2,0:T(8,128)(2,1)} %bitcast.29) | data formatting | bytes 4194304
  36.5 0.2 select_reduce_fusion
  36.8 0.0 copy-start.1
  36.8 10.5 %window_spectra.1 = (f32[64,128,128]{2,1,0:T(8,128)}, f32[64,32,128]{2,1,0:T(8,128)}) custom-call(s32[64]{0:T(128)S(1)} %get-tuple-element.21.order, bf16[64,128,128]{2,1,0:T(8,128)(2,1)S(1)} %bitcast.24, bf16[320,128]{1,0:T(8,128)(2,1)S(1)} %copy-done.4, bf16[64,256]{1,0:T(8,128)(2,1)S(1)} %copy-done.8, bf16[256,256]{1,0:T(8,128)(2,1)S(1)} %copy-done.3, ...), custom_call_target="tpu_custom_call" | custom-call | flops 7549747200 | bytes 7680000 | tf_op jit(solution)/shard_map/window_spectra/pallas_call | solution.py:348
  47.3 7.4 %scores.2 = (s16[8,136,128]{2,1,0:T(8,128)(2,1)}, s16[8,392,128]{2,1,0:T(8,128)(2,1)}, f32[8,8,128]{2,1,0:T(8,128)S(1)}) custom-call(s32[64]{0:T(128)S(1)} %get-tuple-element.26.refs_0_, s32[64]{0:T(128)S(1)} %get-tuple-element.25.refs_1_, s32[64]{0:T(128)S(1)} %get-tuple-element.24.refs_2_, s32[64]{0:T(128)S(1)} %get-tuple-element.23.refs_3_, ...), custom_call_target="tpu_custom_call" | custom-call | flops 3355443200 | bytes 2880000 | tf_op jit(solution)/shard_map/scores/pallas_call | solution.py:398
  54.8 3.4 %all-to-all-start.1 = ((s16[8,136,128]{2,1,0:T(8,128)(2,1)}), s16[8,136,128]{2,1,0:T(8,128)(2,1)S(1)}, u32[]{:S(2)}, u32[]{:S(2)}) async-start(s16[8,136,128]{2,1,0:T(8,128)(2,1)} %get-tuple-element.15), calls=%async_computation.1 | async-start | bytes 557056 | tf_op jit(solution)/shard_map/all_to_all | solution.py:514
  58.1 7.4 %scores.3 = s16[8,392,128]{2,1,0:T(8,128)(2,1)} custom-call(s32[64]{0:T(128)S(1)} %get-tuple-element.26.refs_0_, s32[64]{0:T(128)S(1)} %get-tuple-element.25.refs_1_, s32[64]{0:T(128)S(1)} %get-tuple-element.24.refs_2_, s32[64]{0:T(128)S(1)} %get-tuple-element.23.refs_3_, s32[64]{0:T(128)S(1)} %get-tuple-element.22.refs_4_, ...), custom_call_target="tpu_custom_call", output_to_operand_aliasing={{}: (14, {})} | custom-call | flops 3355443200 | bytes 2880000 | tf_op jit(solution)/shard_map/scores/pallas_call | solution.py:398
  65.5 1.6 %all-to-all-done.1.early_codes = s16[8,136,128]{2,1,0:T(8,128)(2,1)S(1)} async-done(((s16[8,136,128]{2,1,0:T(8,128)(2,1)}), s16[8,136,128]{2,1,0:T(8,128)(2,1)S(1)}, u32[]{:S(2)}, u32[]{:S(2)}) %all-to-all-start.1) | async-done | bytes 278560 | tf_op jit(solution)/shard_map/all_to_all | solution.py:514
  67.1 4.5 %all-to-all-start.2 = ((s16[8,392,128]{2,1,0:T(8,128)(2,1)}), s16[8,392,128]{2,1,0:T(8,128)(2,1)S(1)}, u32[]{:S(2)}, u32[]{:S(2)}) async-start(s16[8,392,128]{2,1,0:T(8,128)(2,1)} %scores.3), calls=%async_computation.2 | async-start | bytes 1605632 | tf_op jit(solution)/shard_map/all_to_all | solution.py:516
  71.6 20.4 %all-to-all-done.2.late_codes = s16[8,392,128]{2,1,0:T(8,128)(2,1)S(1)} async-done(((s16[8,392,128]{2,1,0:T(8,128)(2,1)}), s16[8,392,128]{2,1,0:T(8,128)(2,1)S(1)}, u32[]{:S(2)}, u32[]{:S(2)}) %all-to-all-start.2) | async-done | bytes 802848 | tf_op jit(solution)/shard_map/all_to_all | solution.py:516
  92.0 1.5 %average.1 = (f32[32,4096]{1,0:T(8,128)S(1)}, f32[8,4096]{1,0:T(8,128)S(1)}, f32[8,4096]{1,0:T(8,128)S(1)}) custom-call(s16[8,136,128]{2,1,0:T(8,128)(2,1)S(1)} %all-to-all-done.1.early_codes, s16[8,392,128]{2,1,0:T(8,128)(2,1)S(1)} %all-to-all-done.2.late_codes), custom_call_target="tpu_custom_call" | custom-call | tf_op jit(solution)/shard_map/average/pallas_call | solution.py:432
  93.5 1.0 %collective-permute-start.1 = (f32[8,4096]{1,0:T(8,128)S(1)}, f32[8,4096]{1,0:T(8,128)S(1)}, u32[]{:S(2)}, u32[]{:S(2)}) collective-permute-start(f32[8,4096]{1,0:T(8,128)S(1)} %get-tuple-element.28), channel_id=1, source_target_pairs={{0,1},{1,0},{2,3},{3,2},{4,5},{5,4},{6,7},{7,6},{8,9},{9,8},{10,11... | collective-permute-start | bytes 393224 | tf_op jit(solution)/shard_map/ppermute | solution.py:519
  94.5 1.9 %collective-permute-start.2 = (f32[8,4096]{1,0:T(8,128)S(1)}, f32[8,4096]{1,0:T(8,128)S(1)}, u32[]{:S(2)}, u32[]{:S(2)}) collective-permute-start(f32[8,4096]{1,0:T(8,128)S(1)} %get-tuple-element.27), channel_id=1, source_target_pairs={{1,4},{5,8},{9,12},{4,1},{8,5},{12,9},{3,6},{7,10},{11,14},{6,3},{... | collective-permute-start | bytes 393224 | tf_op jit(solution)/shard_map/ppermute | solution.py:522
  96.5 4.3 %collective-permute-done.2.outer = f32[8,4096]{1,0:T(8,128)S(1)} collective-permute-done((f32[8,4096]{1,0:T(8,128)S(1)}, f32[8,4096]{1,0:T(8,128)S(1)}, u32[]{:S(2)}, u32[]{:S(2)}) %collective-permute-start.2) | collective-permute-done | bytes 131104 | tf_op jit(solution)/shard_map/ppermute | solution.py:522
  100.8 0.8 finish.1
  (25 shorter events, 0.1 us)
Async XLA Ops:
  0.0 7.5 %copy-start.9 = (s32[1,64,1]{1,2,0:T(1,128)S(1)}, s32[1,64,1]{1,2,0:T(1,128)}, u32[]{:S(2)}) copy-start(s32[1,64,1]{1,2,0:T(1,128)} %param.14) | copy-start | bytes 772
  0.0 1.0 copy-start
  2.1 30.7 %all-to-all-start = ((bf16[4,1024,128]{2,1,0:T(8,128)(2,1)}), bf16[4,1024,128]{2,1,0:T(8,128)(2,1)S(1)}, u32[]{:S(2)}, u32[]{:S(2)}) async-start(bf16[4,1024,128]{2,1,0:T(8,128)(2,1)} %bitcast.7), calls=%async_computation | async-start | bytes 2097152 | tf_op jit(solution)/shard_map/all_to_all | solution.py:484
  32.8 14.5 %collective-permute-start = (bf16[128,32,128]{2,1,0:T(8,128)(2,1)S(1)}, bf16[128,32,128]{2,1,0:T(8,128)(2,1)S(1)}, u32[]{:S(2)}, u32[]{:S(2)}) collective-permute-start(bf16[128,32,128]{2,1,0:T(8,128)(2,1)S(1)} %bitcast.25), channel_id=1, source_target_pairs={{0,1},{1,0},{2,3},{3,2},{4,5},{5,4},{6,7},{7,6},{8,9},{9,8},{10,11... | collective-permute-start | bytes 3145736 | tf_op jit(solution)/shard_map/ppermute | solution.py:489
  34.3 2.2 %copy-start.10 = (s32[1,64]{1,0:T(1,128)S(1)}, s32[1,64]{1,0:T(1,128)}, u32[]{:S(2)}) copy-start(s32[1,64]{1,0:T(1,128)} %param.15) | copy-start | bytes 772
  34.3 2.5 %copy-start.3 = (bf16[256,256]{1,0:T(8,128)(2,1)S(1)}, bf16[256,256]{1,0:T(8,128)(2,1)}, u32[]{:S(2)}) copy-start(bf16[256,256]{1,0:T(8,128)(2,1)} %constant.65.clone.window_lanes) | copy-start | bytes 393220
  34.3 2.5 %copy-start.4 = (bf16[320,128]{1,0:T(8,128)(2,1)S(1)}, bf16[320,128]{1,0:T(8,128)(2,1)}, u32[]{:S(2)}) copy-start(bf16[320,128]{1,0:T(8,128)(2,1)} %constant.63.clone.window_rows) | copy-start | bytes 245764
  34.3 2.5 %copy-start.7 = (bf16[256,128]{1,0:T(8,128)(2,1)S(1)}, bf16[256,128]{1,0:T(8,128)(2,1)}, u32[]{:S(2)}) copy-start(bf16[256,128]{1,0:T(8,128)(2,1)} %constant.66.clone.band_lanes) | copy-start | bytes 196612
  34.3 2.5 %copy-start.8 = (bf16[64,256]{1,0:T(8,128)(2,1)S(1)}, bf16[64,256]{1,0:T(8,128)(2,1)}, u32[]{:S(2)}) copy-start(bf16[64,256]{1,0:T(8,128)(2,1)} %constant.64.clone.square_rows) | copy-start | bytes 98308
  36.8 10.5 %copy-start.1 = (bf16[384,512]{1,0:T(8,128)(2,1)S(1)}, bf16[384,512]{1,0:T(8,128)(2,1)}, u32[]{:S(2)}) copy-start(bf16[384,512]{1,0:T(8,128)(2,1)} %constant.67.clone.refs_8_) | copy-start | bytes 1179652
  36.8 10.5 %copy-start.2 = (bf16[512,256]{1,0:T(8,128)(2,1)S(1)}, bf16[512,256]{1,0:T(8,128)(2,1)}, u32[]{:S(2)}) copy-start(bf16[512,256]{1,0:T(8,128)(2,1)} %constant.70.clone.refs_11_) | copy-start | bytes 786436
  36.8 10.5 %copy-start.5 = (bf16[128,192]{1,0:T(8,128)(2,1)S(1)}, bf16[128,192]{1,0:T(8,128)(2,1)}, u32[]{:S(2)}) copy-start(bf16[128,192]{1,0:T(8,128)(2,1)} %constant.68.clone.refs_9_) | copy-start | bytes 147460
  36.8 10.5 %copy-start.6 = (bf16[128,256]{1,0:T(8,128)(2,1)S(1)}, bf16[128,256]{1,0:T(8,128)(2,1)}, u32[]{:S(2)}) copy-start(bf16[128,256]{1,0:T(8,128)(2,1)} %constant.69.clone.refs_10_) | copy-start | bytes 196612
  54.8 12.4 %all-to-all-start.1 = ((s16[8,136,128]{2,1,0:T(8,128)(2,1)}), s16[8,136,128]{2,1,0:T(8,128)(2,1)S(1)}, u32[]{:S(2)}, u32[]{:S(2)}) async-start(s16[8,136,128]{2,1,0:T(8,128)(2,1)} %get-tuple-element.15), calls=%async_computation.1 | async-start | bytes 557056 | tf_op jit(solution)/shard_map/all_to_all | solution.py:514
  67.1 24.9 %all-to-all-start.2 = ((s16[8,392,128]{2,1,0:T(8,128)(2,1)}), s16[8,392,128]{2,1,0:T(8,128)(2,1)S(1)}, u32[]{:S(2)}, u32[]{:S(2)}) async-start(s16[8,392,128]{2,1,0:T(8,128)(2,1)} %scores.3), calls=%async_computation.2 | async-start | bytes 1605632 | tf_op jit(solution)/shard_map/all_to_all | solution.py:516
  93.5 3.0 %collective-permute-start.1 = (f32[8,4096]{1,0:T(8,128)S(1)}, f32[8,4096]{1,0:T(8,128)S(1)}, u32[]{:S(2)}, u32[]{:S(2)}) collective-permute-start(f32[8,4096]{1,0:T(8,128)S(1)} %get-tuple-element.28), channel_id=1, source_target_pairs={{0,1},{1,0},{2,3},{3,2},{4,5},{5,4},{6,7},{7,6},{8,9},{9,8},{10,11... | collective-permute-start | bytes 393224 | tf_op jit(solution)/shard_map/ppermute | solution.py:519
  94.5 6.3 %collective-permute-start.2 = (f32[8,4096]{1,0:T(8,128)S(1)}, f32[8,4096]{1,0:T(8,128)S(1)}, u32[]{:S(2)}, u32[]{:S(2)}) collective-permute-start(f32[8,4096]{1,0:T(8,128)S(1)} %get-tuple-element.27), channel_id=1, source_target_pairs={{1,4},{5,8},{9,12},{4,1},{8,5},{12,9},{3,6},{7,10},{11,14},{6,3},{... | collective-permute-start | bytes 393224 | tf_op jit(solution)/shard_map/ppermute | solution.py:522

commit v8 on v4

--- a/solution.py
+++ b/solution.py
@@ -135,18 +135,34 @@
     capacity, choice, place, target, ranks, slots, position,
     spectra, scale, chip_lanes, chip_rows, inverse_rows, inverse_lanes, *rest,
 ):
-    *sources, out, marks, lefts, lines, packs, pairs, products, backs = rest
+    (*sources, out, marks, lefts, lines, packs, pairs, products, backs,
+     images, levels, stage, note_stage, in_sems, out_sems, note_sem) = rest
     step = pl.program_id(0)
+    steps = pl.num_programs(0)
     group = lefts.shape[0] // ROWS
     base = step * group
+    slot = step % 2
     body = capacity * ROWS
     lane = lax.broadcasted_iota(jnp.int32, (8, WIN), 1)
     line = lax.broadcasted_iota(jnp.int32, (8, WIN), 0)
 
+    def incoming(index, to):
+        rows = pl.ds(pl.multiple_of(index * group, group), group)
+        return (
+            pltpu.make_async_copy(spectra.at[rows], images.at[to], in_sems.at[to, 0]),
+            pltpu.make_async_copy(scale.at[rows], levels.at[to], in_sems.at[to, 1]),
+        )
+
     @pl.when(step == 0)
     def _():
-        out[...] = jnp.zeros_like(out)
+        for copy in incoming(0, 0):
+            copy.start()
         marks[...] = jnp.zeros_like(marks)
+
+    @pl.when(step < steps - 1)
+    def _():
+        for copy in incoming(step + 1, 1 - slot):
+            copy.start()
 
     raws = []
     for part in range(group):
@@ -178,7 +194,7 @@
         lanes = slice(part % 2 * WIN, (part % 2 + 1) * WIN)
         for row in range(0, HALF, 32):
             upper, lower = slice(row, row + 32), slice(HALF + row, HALF + row + 32)
-            own_c, own_s = spectra[part, upper], spectra[part, lower]
+            own_c, own_s = images[slot, part, upper], images[slot, part, lower]
             turned_c, turned_s = pltpu.roll(own_c, HALF, 1), pltpu.roll(own_s, HALF, 1)
             same_c, same_s = pairs[part, upper, :WIN], pairs[part, lower, :WIN]
             cross_c, cross_s = pairs[part, upper, WIN:], pairs[part, lower, WIN:]
@@ -203,6 +219,8 @@
             packs[own, 2 * WIN:3 * WIN] = low[:ROWS]
             packs[own, 3 * WIN:] = low[ROWS:]
 
+    for copy in incoming(step, slot):
+        copy.wait()
     for part in range(group + 4):
         if part < group:
             chip_spectrum(part)
@@ -217,7 +235,7 @@
     for part in range(group):
         own = slice(part * ROWS, (part + 1) * ROWS)
         numerator = both[own, :WIN] + both[own, WIN:]
-        scores.append(numerator * (scale[part] * gain[part:part + 1]))
+        scores.append(numerator * (levels[slot, part] * gain[part:part + 1]))
     largest = jnp.concatenate([jnp.max(jnp.abs(score), axis=0, keepdims=True) for score in scores], axis=0)
     largest = jnp.max(largest, axis=1, keepdims=True)
     power = jnp.ceil(jnp.log2(jnp.maximum(largest, 1e-30)))
@@ -230,18 +248,24 @@
         root = jnp.minimum(root, CODE)
         code = jnp.round(jnp.where(score < 0, -root, root)).astype(jnp.int32).astype(jnp.int16)
         to = target[window]
-        out[to, pl.ds(pl.multiple_of(ranks[window] * ROWS, ROWS), ROWS), :] = code
+        stage[window] = code
         here = lane == position[0] * capacity + ranks[window]
         named = (slots[window] + 1).astype(f32)
         mark = jnp.where(line == 0, named, jnp.where(line == 1, power[part:part + 1], 0.0))
         marks[to] = marks[to] + jnp.where(here, mark, 0.0)
-
-    @pl.when(step == pl.num_programs(0) - 1)
+    for part in range(group):
+        window = base + part
+        rows = pl.ds(pl.multiple_of(ranks[window] * ROWS, ROWS), ROWS)
+        pltpu.make_async_copy(stage.at[window], out.at[target[window], rows, :], out_sems.at[window]).start()
+
+    @pl.when(step == steps - 1)
     def _():
-        for to in range(out.shape[0]):
-            notes = marks[to]
-            notes = jnp.concatenate([notes, jnp.zeros_like(notes)], axis=0)
-            out[to, body:, :] = notes.astype(jnp.int32).astype(jnp.int16)
+        note_stage[...] = marks[...].astype(jnp.int32).astype(jnp.int16)
+        notes = pltpu.make_async_copy(note_stage, out.at[:, body:, :], note_sem)
+        notes.start()
+        for window in range(stage.shape[0]):
+            pltpu.make_async_copy(stage.at[window], out.at[0, :ROWS, :], out_sems.at[window]).wait()
+        notes.wait()
 
 
 def average_kernel(capacity, chip_amount, codes, smooth, first, last, values):
@@ -338,17 +362,16 @@
     amount = spectra.shape[0]
     group = min(SCORE_GROUP, amount)
     constants = [jnp.asarray(table[k]) for k in ("chip_lanes", "chip_rows", "inverse_rows", "inverse_lanes")]
-    shape = (devices, capacity * ROWS + 16, WIN)
+    shape = (devices, capacity * ROWS + 8, WIN)
     return pl.pallas_call(
         functools.partial(score_kernel, capacity),
         grid_spec=pltpu.PrefetchScalarGridSpec(
             num_scalar_prefetch=len(scalars),
             grid=(amount // group,),
             in_specs=[
-                pl.BlockSpec((group, WIN, WIN), lambda i, *_: (i, 0, 0)),
-                pl.BlockSpec((group, ROWS, WIN), lambda i, *_: (i, 0, 0)),
+                pl.BlockSpec(memory_space=pl.ANY), pl.BlockSpec(memory_space=pl.ANY),
             ] + [resident() for _ in constants] + [resident() for _ in sources],
-            out_specs=resident(),
+            out_specs=pl.BlockSpec(memory_space=pl.ANY),
             scratch_shapes=[
                 pltpu.VMEM((devices, 8, WIN), f32),
                 pltpu.VMEM((group * ROWS, 3 * WIN), bf16),
@@ -357,12 +380,19 @@
                 pltpu.VMEM((group, WIN, 2 * WIN), f32),
                 pltpu.VMEM((group // 2, 2 * WIN, 2 * WIN), bf16),
                 pltpu.VMEM((group // 2, OFF, 2 * WIN), f32),
+                pltpu.VMEM((2, group, WIN, WIN), f32),
+                pltpu.VMEM((2, group, ROWS, WIN), f32),
+                pltpu.VMEM((amount, ROWS, WIN), jnp.int16),
+                pltpu.VMEM((devices, 8, WIN), jnp.int16),
+                pltpu.SemaphoreType.DMA((2, 2)),
+                pltpu.SemaphoreType.DMA((amount,)),
+                pltpu.SemaphoreType.DMA,
             ],
         ),
-        out_shape=pltpu.VMEM(shape, jnp.int16),
+        out_shape=jax.ShapeDtypeStruct(shape, jnp.int16),
         compiler_params=pltpu.CompilerParams(vmem_limit_bytes=VMEM_GRANT),
         name="scores",
-    )(*scalars, away(spectra), away(scale), *[away(c) for c in constants], *[near(source) for source in sources])
+    )(*scalars, away(spectra), away(scale), *[near(c) for c in constants], *[near(source) for source in sources])
 
 
 def average_scores(codes, capacity, chip_amount):

time: 97.7 us -> 98.5 us (level)
  Pallas kernels: 24.8 us -> 25.9 us
    pallas_call x1, Pallas kernels: 12.6 us -> 13.6 us  [score_windows(): pl.pallas_call(functools.partial(score_kernel, capacity), grid_spec=pltpu...]
    unnamed x15 -> x23, local copies, waits for them, and re-layouts: 3.22 us -> 3.24 us
where the time goes in v8:
time: 98.5 us; the launch traced here: 98.2 us
  waiting for transfers between devices  30.3 us (31%)
  blocking collectives  30.1 us (31%)
  Pallas kernels  25.9 us (26%)
  starting transfers between devices  8.21 us (8%)
  local copies, waits for them, and re-layouts  3.24 us (3%)
    all_to_all x1, blocking collectives, on_device(): lax.all_to_all(sent, 'tile', split_axis=0, concat_axis=0, tiled=True)  30.1 us
    all_to_all x1, waiting for transfers between devices, on_device(): lax.all_to_all(codes, ('tile', 'sub'), split_axis=0, concat_axis=0, tiled...  26 us
    pallas_call x1, Pallas kernels, score_windows(): pl.pallas_call(functools.partial(score_kernel, capacity), grid_spec=pltpu...  13.6 us
    pallas_call x1, Pallas kernels, prepare_windows(): pl.pallas_call(window_kernel, grid=(amount // group,), in_specs=[pl.Block...  9.96 us
    ppermute x1, waiting for transfers between devices, on_device(): lax.ppermute(jnp.where(sub == 0, first, last), ('tile', 'sub'), ups + downs)  4.35 us
    all_to_all x1, starting transfers between devices, on_device(): lax.all_to_all(codes, ('tile', 'sub'), split_axis=0, concat_axis=0, tiled...  3.52 us
    unnamed x23, local copies, waits for them, and re-layouts  3.24 us
  transfers between devices with their start and end apart: 4, of which 2 were waited for; matrix products, arithmetic and copies ran while one was open for 2% of the time, Pallas kernels for 10%

profile of v8, /device:TPU:1, one launch (start us, length us, event | category | flops | bytes accessed | tf_op | source)
XLA Modules:
  0.0 98.2 jit_solution(11754226122661318176)
XLA Ops:
  0.0 0.9 copy-done.1
  1.0 0.2 spread.1
  1.1 30.1 %all_to_all.10 = bf16[4,1024,128]{2,1,0:T(8,128)(2,1)S(1)} all-to-all(bf16[4,1024,128]{2,1,0:T(8,128)(2,1)S(1)} %bitcast.18), channel_id=1, replica_groups=mesh['groups'=2,'tile'=4,'pair'=2,'sub'=2] {'tile'}, dimensions={0} | all-to-all | bytes 2097152 | tf_op jit(solution)/shard_map/all_to_all | solution.py:452
  31.3 1.8 %collective-permute-start = (bf16[128,32,128]{2,1,0:T(8,128)(2,1)S(1)}, bf16[128,32,128]{2,1,0:T(8,128)(2,1)}, u32[]{:S(2)}, u32[]{:S(2)}) collective-permute-start(bf16[128,32,128]{2,1,0:T(8,128)(2,1)S(1)} %bitcast.19), channel_id=1, source_target_pairs={{0,1},{1,0},{2,3},{3,2},{4,5},{5,4},{6,7},{7,6},{8,9},{9,8},{10,11... | collective-permute-start | bytes 3145736 | tf_op jit(solution)/shard_map/ppermute | solution.py:458
  33.0 0.0 copy-start.9
  33.0 0.0 copy-start.10
  33.0 2.2 %copy.13 = bf16[8,8,128,128]{3,2,1,0:T(8,128)(2,1)S(1)} copy(bf16[8,8,128,128]{3,1,2,0:T(8,128)(2,1)} %bitcast.26) | data formatting | bytes 4194304
  35.3 0.0 copy-done.6
  35.3 0.2 convert_reduce_fusion.ranks
  35.6 0.0 copy-start
  35.6 0.0 copy-start.2
  35.6 0.0 copy-start.3
  35.6 0.0 copy-start.4
  35.6 10.0 %window_spectra.1 = (f32[64,128,128]{2,1,0:T(8,128)}, f32[64,32,128]{2,1,0:T(8,128)}) custom-call(bf16[64,128,128]{2,1,0:T(8,128)(2,1)S(1)} %bitcast.21, bf16[320,128]{1,0:T(8,128)(2,1)S(1)} %copy-done.8, bf16[64,256]{1,0:T(8,128)(2,1)S(1)} %copy-done.10, bf16[256,256]{1,0:T(8,128)(2,1)S(1)} %copy-done.7, bf16[256,128]{1,0:T(8,128)(2,1)S(1)} %copy-done.9), custom_call_target="tpu_custom_call" | custom-call | flops 7549747200 | bytes 7680000 | tf_op jit(solution)/shard_map/window_spectra/pallas_call | solution.py:341
  45.6 0.0 collective-permute-done.rest_1_
  45.6 13.6 %scores.1 = s16[8,520,128]{2,1,0:T(8,128)(2,1)} custom-call(s32[64]{0:T(128)S(1)} %get-tuple-element.18.choice, s32[64]{0:T(128)S(1)} %get-tuple-element.17.place, s32[64]{0:T(128)S(1)} %bitcast.25, s32[64]{0:T(128)S(1)} %convert_reduce_fusion.ranks, s32[64]{0:T(128)S(1)} %bitcast.23, s32[1]{0:T(128)} %bitcast.3.position, ...), custom_call_target="tpu_custom_call" | custom-call | tf_op jit(solution)/shard_map/scores/pallas_call | solution.py:366
  59.2 3.5 %all-to-all-start.1 = ((s16[8,520,128]{2,1,0:T(8,128)(2,1)}), s16[8,520,128]{2,1,0:T(8,128)(2,1)S(1)}, u32[]{:S(2)}, u32[]{:S(2)}) async-start(s16[8,520,128]{2,1,0:T(8,128)(2,1)} %scores.1), calls=%async_computation.1 | async-start | bytes 2129920 | tf_op jit(solution)/shard_map/all_to_all | solution.py:470
  62.8 26.0 %all-to-all-done.1.codes = s16[8,520,128]{2,1,0:T(8,128)(2,1)S(1)} async-done(((s16[8,520,128]{2,1,0:T(8,128)(2,1)}), s16[8,520,128]{2,1,0:T(8,128)(2,1)S(1)}, u32[]{:S(2)}, u32[]{:S(2)}) %all-to-all-start.1) | async-done | bytes 1064992 | tf_op jit(solution)/shard_map/all_to_all | solution.py:470
  88.7 1.3 %average.1 = (f32[32,4096]{1,0:T(8,128)S(1)}, f32[8,4096]{1,0:T(8,128)S(1)}, f32[8,4096]{1,0:T(8,128)S(1)}) custom-call(s16[8,520,128]{2,1,0:T(8,128)(2,1)S(1)} %all-to-all-done.1.codes), custom_call_target="tpu_custom_call" | custom-call | tf_op jit(solution)/shard_map/average/pallas_call | solution.py:400
  90.0 1.0 %collective-permute-start.1 = (f32[8,4096]{1,0:T(8,128)S(1)}, f32[8,4096]{1,0:T(8,128)S(1)}, u32[]{:S(2)}, u32[]{:S(2)}) collective-permute-start(f32[8,4096]{1,0:T(8,128)S(1)} %get-tuple-element.16), channel_id=1, source_target_pairs={{0,1},{1,0},{2,3},{3,2},{4,5},{5,4},{6,7},{7,6},{8,9},{9,8},{10,11... | collective-permute-start | bytes 393224 | tf_op jit(solution)/shard_map/ppermute | solution.py:473
  91.1 1.9 %collective-permute-start.2 = (f32[8,4096]{1,0:T(8,128)S(1)}, f32[8,4096]{1,0:T(8,128)S(1)}, u32[]{:S(2)}, u32[]{:S(2)}) collective-permute-start(f32[8,4096]{1,0:T(8,128)S(1)} %get-tuple-element.15), channel_id=1, source_target_pairs={{1,4},{5,8},{9,12},{4,1},{8,5},{12,9},{3,6},{7,10},{11,14},{6,3},{... | collective-permute-start | bytes 393224 | tf_op jit(solution)/shard_map/ppermute | solution.py:476
  93.0 0.0 collective-permute-done.1.inner
  93.0 4.3 %collective-permute-done.2.outer = f32[8,4096]{1,0:T(8,128)S(1)} collective-permute-done((f32[8,4096]{1,0:T(8,128)S(1)}, f32[8,4096]{1,0:T(8,128)S(1)}, u32[]{:S(2)}, u32[]{:S(2)}) %collective-permute-start.2) | collective-permute-done | bytes 131104 | tf_op jit(solution)/shard_map/ppermute | solution.py:476
  97.3 0.8 finish.1
  (16 shorter events, 0.1 us)
Async XLA Ops:
  0.0 0.9 copy-start.1
  31.3 14.3 %collective-permute-start = (bf16[128,32,128]{2,1,0:T(8,128)(2,1)S(1)}, bf16[128,32,128]{2,1,0:T(8,128)(2,1)}, u32[]{:S(2)}, u32[]{:S(2)}) collective-permute-start(bf16[128,32,128]{2,1,0:T(8,128)(2,1)S(1)} %bitcast.19), channel_id=1, source_target_pairs={{0,1},{1,0},{2,3},{3,2},{4,5},{5,4},{6,7},{7,6},{8,9},{9,8},{10,11... | collective-permute-start | bytes 3145736 | tf_op jit(solution)/shard_map/ppermute | solution.py:458
  33.0 2.3 %copy-start.6 = (s32[1,64,1]{1,2,0:T(1,128)S(1)}, s32[1,64,1]{1,2,0:T(1,128)}, u32[]{:S(2)}) copy-start(s32[1,64,1]{1,2,0:T(1,128)} %param.14) | copy-start | bytes 772
  33.0 2.5 %copy-start.5 = (s32[1,64]{1,0:T(1,128)S(1)}, s32[1,64]{1,0:T(1,128)}, u32[]{:S(2)}) copy-start(s32[1,64]{1,0:T(1,128)} %param.15) | copy-start | bytes 772
  33.0 2.5 %copy-start.7 = (bf16[256,256]{1,0:T(8,128)(2,1)S(1)}, bf16[256,256]{1,0:T(8,128)(2,1)}, u32[]{:S(2)}) copy-start(bf16[256,256]{1,0:T(8,128)(2,1)} %constant.61.clone.window_lanes) | copy-start | bytes 393220
  33.0 2.5 %copy-start.8 = (bf16[320,128]{1,0:T(8,128)(2,1)S(1)}, bf16[320,128]{1,0:T(8,128)(2,1)}, u32[]{:S(2)}) copy-start(bf16[320,128]{1,0:T(8,128)(2,1)} %constant.59.clone.window_rows) | copy-start | bytes 245764
  33.0 2.5 %copy-start.9 = (bf16[256,128]{1,0:T(8,128)(2,1)S(1)}, bf16[256,128]{1,0:T(8,128)(2,1)}, u32[]{:S(2)}) copy-start(bf16[256,128]{1,0:T(8,128)(2,1)} %constant.62.clone.band_lanes) | copy-start | bytes 196612
  33.0 2.5 %copy-start.10 = (bf16[64,256]{1,0:T(8,128)(2,1)S(1)}, bf16[64,256]{1,0:T(8,128)(2,1)}, u32[]{:S(2)}) copy-start(bf16[64,256]{1,0:T(8,128)(2,1)} %constant.60.clone.square_rows) | copy-start | bytes 98308
  35.6 10.0 %copy-start = (bf16[384,512]{1,0:T(8,128)(2,1)S(1)}, bf16[384,512]{1,0:T(8,128)(2,1)}, u32[]{:S(2)}) copy-start(bf16[384,512]{1,0:T(8,128)(2,1)} %constant.63.clone.chip_lanes) | copy-start | bytes 1179652
  35.6 10.0 %copy-start.2 = (bf16[512,256]{1,0:T(8,128)(2,1)S(1)}, bf16[512,256]{1,0:T(8,128)(2,1)}, u32[]{:S(2)}) copy-start(bf16[512,256]{1,0:T(8,128)(2,1)} %constant.66.clone.inverse_lanes) | copy-start | bytes 786436
  35.6 10.0 %copy-start.3 = (bf16[128,192]{1,0:T(8,128)(2,1)S(1)}, bf16[128,192]{1,0:T(8,128)(2,1)}, u32[]{:S(2)}) copy-start(bf16[128,192]{1,0:T(8,128)(2,1)} %constant.64.clone.chip_rows) | copy-start | bytes 147460
  35.6 10.0 %copy-start.4 = (bf16[128,256]{1,0:T(8,128)(2,1)S(1)}, bf16[128,256]{1,0:T(8,128)(2,1)}, u32[]{:S(2)}) copy-start(bf16[128,256]{1,0:T(8,128)(2,1)} %constant.65.clone.inverse_rows) | copy-start | bytes 196612
  59.2 29.5 %all-to-all-start.1 = ((s16[8,520,128]{2,1,0:T(8,128)(2,1)}), s16[8,520,128]{2,1,0:T(8,128)(2,1)S(1)}, u32[]{:S(2)}, u32[]{:S(2)}) async-start(s16[8,520,128]{2,1,0:T(8,128)(2,1)} %scores.1), calls=%async_computation.1 | async-start | bytes 2129920 | tf_op jit(solution)/shard_map/all_to_all | solution.py:470
  90.0 2.9 %collective-permute-start.1 = (f32[8,4096]{1,0:T(8,128)S(1)}, f32[8,4096]{1,0:T(8,128)S(1)}, u32[]{:S(2)}, u32[]{:S(2)}) collective-permute-start(f32[8,4096]{1,0:T(8,128)S(1)} %get-tuple-element.16), channel_id=1, source_target_pairs={{0,1},{1,0},{2,3},{3,2},{4,5},{5,4},{6,7},{7,6},{8,9},{9,8},{10,11... | collective-permute-start | bytes 393224 | tf_op jit(solution)/shard_map/ppermute | solution.py:473
  91.1 6.3 %collective-permute-start.2 = (f32[8,4096]{1,0:T(8,128)S(1)}, f32[8,4096]{1,0:T(8,128)S(1)}, u32[]{:S(2)}, u32[]{:S(2)}) collective-permute-start(f32[8,4096]{1,0:T(8,128)S(1)} %get-tuple-element.15), channel_id=1, source_target_pairs={{1,4},{5,8},{9,12},{4,1},{8,5},{12,9},{3,6},{7,10},{11,14},{6,3},{... | collective-permute-start | bytes 393224 | tf_op jit(solution)/shard_map/ppermute | solution.py:476

commit v9 on v4

--- a/solution.py
+++ b/solution.py
@@ -68,8 +68,11 @@
     chip_rows = np.concatenate([pair_of(high), pair_of(high), pair_of(low)], axis=1)
     same = np.concatenate([cosine, cosine], axis=0)[:, :CHIP].T
     cross = np.concatenate([sine, -sine], axis=0)[:, :CHIP].T
-    lane_high, lane_low = split_table(twice(np.concatenate([same, cross], axis=1)))
-    chip_lanes = np.concatenate([lane_high, lane_high, lane_low], axis=0)
+    lane_high, lane_low = split_table(np.concatenate([same, cross], axis=1))
+    none = np.zeros_like(lane_low)
+    even_lanes = np.concatenate([lane_high, lane_high, lane_low, none], axis=0)
+    odd_lanes = np.concatenate([none, lane_low, lane_high, lane_high], axis=0)
+    chip_lanes = np.concatenate([even_lanes, odd_lanes], axis=1)
     weight = np.full((2 * HALF, 1), 2.0 / PERIOD)
     weight[0] = 1.0 / PERIOD
     inverse = (forward * weight)[:, :OFF].T
@@ -145,9 +148,9 @@
 
     @pl.when(step == 0)
     def _():
-        out[...] = jnp.zeros_like(out)
         marks[...] = jnp.zeros_like(marks)
 
+    even = lax.broadcasted_iota(jnp.int32, (ROWS, WIN), 1) < CHIP
     raws = []
     for part in range(group):
         window = base + part
@@ -163,11 +166,13 @@
     gain = lax.rsqrt(power + epsilon) * (1.0 / CHIP)
     for part in range(group):
         own = slice(part * ROWS, (part + 1) * ROWS)
-        high, low = halves(raws[part])
-        lefts[own, :WIN] = high
-        lefts[own, WIN:2 * WIN] = low
-        lefts[own, 2 * WIN:] = high
-    lines[...] = dot(lefts[...], chip_lanes[...])
+        high = raws[part].astype(bf16).astype(f32)
+        low = raws[part] - high
+        lefts[own, :WIN] = jnp.where(even, high, pltpu.roll(low, CHIP, 1)).astype(bf16)
+        lefts[own, WIN:2 * WIN] = high.astype(bf16)
+        lefts[own, 2 * WIN:] = jnp.where(even, pltpu.roll(high, CHIP, 1), low).astype(bf16)
+    lines[:, :2 * WIN] = dot(lefts[:, :2 * WIN], chip_lanes[:, :2 * WIN])
+    lines[:, 2 * WIN:] = dot(lefts[:, WIN:], chip_lanes[:, 2 * WIN:])
 
     def chip_spectrum(part):
         high, low = halves(lines[part * ROWS:(part + 1) * ROWS, :])
@@ -239,9 +244,7 @@
     @pl.when(step == pl.num_programs(0) - 1)
     def _():
         for to in range(out.shape[0]):
-            notes = marks[to]
-            notes = jnp.concatenate([notes, jnp.zeros_like(notes)], axis=0)
-            out[to, body:, :] = notes.astype(jnp.int32).astype(jnp.int16)
+            out[to, body:, :] = marks[to].astype(jnp.int32).astype(jnp.int16)
 
 
 def average_kernel(capacity, chip_amount, codes, smooth, first, last, values):
@@ -338,7 +341,7 @@
     amount = spectra.shape[0]
     group = min(SCORE_GROUP, amount)
     constants = [jnp.asarray(table[k]) for k in ("chip_lanes", "chip_rows", "inverse_rows", "inverse_lanes")]
-    shape = (devices, capacity * ROWS + 16, WIN)
+    shape = (devices, capacity * ROWS + 8, WIN)
     return pl.pallas_call(
         functools.partial(score_kernel, capacity),
         grid_spec=pltpu.PrefetchScalarGridSpec(
@@ -362,7 +365,7 @@
         out_shape=pltpu.VMEM(shape, jnp.int16),
         compiler_params=pltpu.CompilerParams(vmem_limit_bytes=VMEM_GRANT),
         name="scores",
-    )(*scalars, away(spectra), away(scale), *[away(c) for c in constants], *[near(source) for source in sources])
+    )(*scalars, away(spectra), away(scale), *[near(c) for c in constants], *[near(source) for source in sources])
 
 
 def average_scores(codes, capacity, chip_amount):

time: 97.7 us -> 96.9 us (level)
    unnamed x15 -> x23, local copies, waits for them, and re-layouts: 3.22 us -> 3.24 us
  transfers between devices with their start and end apart: 4 -> 4, of which waited for: 2 -> 2; matrix products, arithmetic and copies ran while one was open for 2% -> 3% of each run, Pallas kernels for 10% -> 10%
where the time goes in v9:
time: 96.9 us; the launch traced here: 96.6 us
  waiting for transfers between devices  30.3 us (31%)
  blocking collectives  30.1 us (31%)
  Pallas kernels  24.4 us (25%)
  starting transfers between devices  8.2 us (8%)
  local copies, waits for them, and re-layouts  3.24 us (3%)
    all_to_all x1, blocking collectives, on_device(): lax.all_to_all(sent, 'tile', split_axis=0, concat_axis=0, tiled=True)  30.1 us
    all_to_all x1, waiting for transfers between devices, on_device(): lax.all_to_all(codes, ('tile', 'sub'), split_axis=0, concat_axis=0, tiled...  25.9 us
    pallas_call x1, Pallas kernels, score_windows(): pl.pallas_call(functools.partial(score_kernel, capacity), grid_spec=pltpu...  12.1 us
    pallas_call x1, Pallas kernels, prepare_windows(): pl.pallas_call(window_kernel, grid=(amount // group,), in_specs=[pl.Block...  9.96 us
    ppermute x1, waiting for transfers between devices, on_device(): lax.ppermute(jnp.where(sub == 0, first, last), ('tile', 'sub'), ups + downs)  4.35 us
    all_to_all x1, starting transfers between devices, on_device(): lax.all_to_all(codes, ('tile', 'sub'), split_axis=0, concat_axis=0, tiled...  3.51 us
    unnamed x23, local copies, waits for them, and re-layouts  3.24 us
  transfers between devices with their start and end apart: 4, of which 2 were waited for; matrix products, arithmetic and copies ran while one was open for 3% of the time, Pallas kernels for 10%

profile of v9, /device:TPU:1, one launch (start us, length us, event | category | flops | bytes accessed | tf_op | source)
XLA Modules:
  0.0 96.6 jit_solution(4405883619369680064)
XLA Ops:
  0.0 0.9 copy-done
  1.0 0.2 spread.1
  1.1 30.1 %all_to_all.10 = bf16[4,1024,128]{2,1,0:T(8,128)(2,1)S(1)} all-to-all(bf16[4,1024,128]{2,1,0:T(8,128)(2,1)S(1)} %bitcast.18), channel_id=1, replica_groups=mesh['groups'=2,'tile'=4,'pair'=2,'sub'=2] {'tile'}, dimensions={0} | all-to-all | bytes 2097152 | tf_op jit(solution)/shard_map/all_to_all | solution.py:425
  31.3 1.8 %collective-permute-start = (bf16[128,32,128]{2,1,0:T(8,128)(2,1)S(1)}, bf16[128,32,128]{2,1,0:T(8,128)(2,1)}, u32[]{:S(2)}, u32[]{:S(2)}) collective-permute-start(bf16[128,32,128]{2,1,0:T(8,128)(2,1)S(1)} %bitcast.19), channel_id=1, source_target_pairs={{0,1},{1,0},{2,3},{3,2},{4,5},{5,4},{6,7},{7,6},{8,9},{9,8},{10,11... | collective-permute-start | bytes 3145736 | tf_op jit(solution)/shard_map/ppermute | solution.py:431
  33.0 0.0 copy-start.9
  33.0 0.0 copy-start.10
  33.0 2.2 %copy.13 = bf16[8,8,128,128]{3,2,1,0:T(8,128)(2,1)S(1)} copy(bf16[8,8,128,128]{3,1,2,0:T(8,128)(2,1)} %bitcast.26) | data formatting | bytes 4194304
  35.3 0.0 copy-done.6
  35.3 0.2 convert_reduce_fusion.ranks
  35.6 0.0 copy-start.1
  35.6 0.0 copy-start.2
  35.6 0.0 copy-start.3
  35.6 0.0 copy-start.4
  35.6 10.0 %window_spectra.1 = (f32[64,128,128]{2,1,0:T(8,128)}, f32[64,32,128]{2,1,0:T(8,128)}) custom-call(bf16[64,128,128]{2,1,0:T(8,128)(2,1)S(1)} %bitcast.21, bf16[320,128]{1,0:T(8,128)(2,1)S(1)} %copy-done.8, bf16[64,256]{1,0:T(8,128)(2,1)S(1)} %copy-done.10, bf16[256,256]{1,0:T(8,128)(2,1)S(1)} %copy-done.7, bf16[256,128]{1,0:T(8,128)(2,1)S(1)} %copy-done.9), custom_call_target="tpu_custom_call" | custom-call | flops 7549747200 | bytes 7680000 | tf_op jit(solution)/shard_map/window_spectra/pallas_call | solution.py:320
  45.6 0.0 collective-permute-done.rest_1_
  45.6 12.1 %scores.1 = s16[8,520,128]{2,1,0:T(8,128)(2,1)} custom-call(s32[64]{0:T(128)S(1)} %get-tuple-element.18.choice, s32[64]{0:T(128)S(1)} %get-tuple-element.17.place, s32[64]{0:T(128)S(1)} %bitcast.25, s32[64]{0:T(128)S(1)} %convert_reduce_fusion.ranks, s32[64]{0:T(128)S(1)} %bitcast.23, s32[1]{0:T(128)} %bitcast.3.position, ...), custom_call_target="tpu_custom_call" | custom-call | tf_op jit(solution)/shard_map/scores/pallas_call | solution.py:345
  57.7 3.5 %all-to-all-start.1 = ((s16[8,520,128]{2,1,0:T(8,128)(2,1)}), s16[8,520,128]{2,1,0:T(8,128)(2,1)S(1)}, u32[]{:S(2)}, u32[]{:S(2)}) async-start(s16[8,520,128]{2,1,0:T(8,128)(2,1)} %scores.1), calls=%async_computation.1 | async-start | bytes 2129920 | tf_op jit(solution)/shard_map/all_to_all | solution.py:443
  61.2 25.9 %all-to-all-done.1.codes = s16[8,520,128]{2,1,0:T(8,128)(2,1)S(1)} async-done(((s16[8,520,128]{2,1,0:T(8,128)(2,1)}), s16[8,520,128]{2,1,0:T(8,128)(2,1)S(1)}, u32[]{:S(2)}, u32[]{:S(2)}) %all-to-all-start.1) | async-done | bytes 1064992 | tf_op jit(solution)/shard_map/all_to_all | solution.py:443
  87.2 1.3 %average.1 = (f32[32,4096]{1,0:T(8,128)S(1)}, f32[8,4096]{1,0:T(8,128)S(1)}, f32[8,4096]{1,0:T(8,128)S(1)}) custom-call(s16[8,520,128]{2,1,0:T(8,128)(2,1)S(1)} %all-to-all-done.1.codes), custom_call_target="tpu_custom_call" | custom-call | tf_op jit(solution)/shard_map/average/pallas_call | solution.py:373
  88.5 1.0 %collective-permute-start.1 = (f32[8,4096]{1,0:T(8,128)S(1)}, f32[8,4096]{1,0:T(8,128)S(1)}, u32[]{:S(2)}, u32[]{:S(2)}) collective-permute-start(f32[8,4096]{1,0:T(8,128)S(1)} %get-tuple-element.16), channel_id=1, source_target_pairs={{0,1},{1,0},{2,3},{3,2},{4,5},{5,4},{6,7},{7,6},{8,9},{9,8},{10,11... | collective-permute-start | bytes 393224 | tf_op jit(solution)/shard_map/ppermute | solution.py:446
  89.5 1.9 %collective-permute-start.2 = (f32[8,4096]{1,0:T(8,128)S(1)}, f32[8,4096]{1,0:T(8,128)S(1)}, u32[]{:S(2)}, u32[]{:S(2)}) collective-permute-start(f32[8,4096]{1,0:T(8,128)S(1)} %get-tuple-element.15), channel_id=1, source_target_pairs={{1,4},{5,8},{9,12},{4,1},{8,5},{12,9},{3,6},{7,10},{11,14},{6,3},{... | collective-permute-start | bytes 393224 | tf_op jit(solution)/shard_map/ppermute | solution.py:449
  91.5 0.0 collective-permute-done.1.inner
  91.5 4.3 %collective-permute-done.2.outer = f32[8,4096]{1,0:T(8,128)S(1)} collective-permute-done((f32[8,4096]{1,0:T(8,128)S(1)}, f32[8,4096]{1,0:T(8,128)S(1)}, u32[]{:S(2)}, u32[]{:S(2)}) %collective-permute-start.2) | collective-permute-done | bytes 131104 | tf_op jit(solution)/shard_map/ppermute | solution.py:449
  95.8 0.8 finish.1
  (16 shorter events, 0.1 us)
Async XLA Ops:
  0.0 0.9 copy-start
  31.3 14.3 %collective-permute-start = (bf16[128,32,128]{2,1,0:T(8,128)(2,1)S(1)}, bf16[128,32,128]{2,1,0:T(8,128)(2,1)}, u32[]{:S(2)}, u32[]{:S(2)}) collective-permute-start(bf16[128,32,128]{2,1,0:T(8,128)(2,1)S(1)} %bitcast.19), channel_id=1, source_target_pairs={{0,1},{1,0},{2,3},{3,2},{4,5},{5,4},{6,7},{7,6},{8,9},{9,8},{10,11... | collective-permute-start | bytes 3145736 | tf_op jit(solution)/shard_map/ppermute | solution.py:431
  33.0 2.3 %copy-start.6 = (s32[1,64,1]{1,2,0:T(1,128)S(1)}, s32[1,64,1]{1,2,0:T(1,128)}, u32[]{:S(2)}) copy-start(s32[1,64,1]{1,2,0:T(1,128)} %param.14) | copy-start | bytes 772
  33.0 2.5 %copy-start.5 = (s32[1,64]{1,0:T(1,128)S(1)}, s32[1,64]{1,0:T(1,128)}, u32[]{:S(2)}) copy-start(s32[1,64]{1,0:T(1,128)} %param.15) | copy-start | bytes 772
  33.0 2.5 %copy-start.7 = (bf16[256,256]{1,0:T(8,128)(2,1)S(1)}, bf16[256,256]{1,0:T(8,128)(2,1)}, u32[]{:S(2)}) copy-start(bf16[256,256]{1,0:T(8,128)(2,1)} %constant.61.clone.window_lanes) | copy-start | bytes 393220
  33.0 2.5 %copy-start.8 = (bf16[320,128]{1,0:T(8,128)(2,1)S(1)}, bf16[320,128]{1,0:T(8,128)(2,1)}, u32[]{:S(2)}) copy-start(bf16[320,128]{1,0:T(8,128)(2,1)} %constant.59.clone.window_rows) | copy-start | bytes 245764
  33.0 2.5 %copy-start.9 = (bf16[256,128]{1,0:T(8,128)(2,1)S(1)}, bf16[256,128]{1,0:T(8,128)(2,1)}, u32[]{:S(2)}) copy-start(bf16[256,128]{1,0:T(8,128)(2,1)} %constant.62.clone.band_lanes) | copy-start | bytes 196612
  33.0 2.5 %copy-start.10 = (bf16[64,256]{1,0:T(8,128)(2,1)S(1)}, bf16[64,256]{1,0:T(8,128)(2,1)}, u32[]{:S(2)}) copy-start(bf16[64,256]{1,0:T(8,128)(2,1)} %constant.60.clone.square_rows) | copy-start | bytes 98308
  35.6 10.0 %copy-start.1 = (bf16[256,512]{1,0:T(8,128)(2,1)S(1)}, bf16[256,512]{1,0:T(8,128)(2,1)}, u32[]{:S(2)}) copy-start(bf16[256,512]{1,0:T(8,128)(2,1)} %constant.63.clone.chip_lanes) | copy-start | bytes 786436
  35.6 10.0 %copy-start.2 = (bf16[512,256]{1,0:T(8,128)(2,1)S(1)}, bf16[512,256]{1,0:T(8,128)(2,1)}, u32[]{:S(2)}) copy-start(bf16[512,256]{1,0:T(8,128)(2,1)} %constant.66.clone.inverse_lanes) | copy-start | bytes 786436
  35.6 10.0 %copy-start.3 = (bf16[128,192]{1,0:T(8,128)(2,1)S(1)}, bf16[128,192]{1,0:T(8,128)(2,1)}, u32[]{:S(2)}) copy-start(bf16[128,192]{1,0:T(8,128)(2,1)} %constant.64.clone.chip_rows) | copy-start | bytes 147460
  35.6 10.0 %copy-start.4 = (bf16[128,256]{1,0:T(8,128)(2,1)S(1)}, bf16[128,256]{1,0:T(8,128)(2,1)}, u32[]{:S(2)}) copy-start(bf16[128,256]{1,0:T(8,128)(2,1)} %constant.65.clone.inverse_rows) | copy-start | bytes 196612
  57.7 29.5 %all-to-all-start.1 = ((s16[8,520,128]{2,1,0:T(8,128)(2,1)}), s16[8,520,128]{2,1,0:T(8,128)(2,1)S(1)}, u32[]{:S(2)}, u32[]{:S(2)}) async-start(s16[8,520,128]{2,1,0:T(8,128)(2,1)} %scores.1), calls=%async_computation.1 | async-start | bytes 2129920 | tf_op jit(solution)/shard_map/all_to_all | solution.py:443
  88.5 3.0 %collective-permute-start.1 = (f32[8,4096]{1,0:T(8,128)S(1)}, f32[8,4096]{1,0:T(8,128)S(1)}, u32[]{:S(2)}, u32[]{:S(2)}) collective-permute-start(f32[8,4096]{1,0:T(8,128)S(1)} %get-tuple-element.16), channel_id=1, source_target_pairs={{0,1},{1,0},{2,3},{3,2},{4,5},{5,4},{6,7},{7,6},{8,9},{9,8},{10,11... | collective-permute-start | bytes 393224 | tf_op jit(solution)/shard_map/ppermute | solution.py:446
  89.5 6.3 %collective-permute-start.2 = (f32[8,4096]{1,0:T(8,128)S(1)}, f32[8,4096]{1,0:T(8,128)S(1)}, u32[]{:S(2)}, u32[]{:S(2)}) collective-permute-start(f32[8,4096]{1,0:T(8,128)S(1)} %get-tuple-element.15), channel_id=1, source_target_pairs={{1,4},{5,8},{9,12},{4,1},{8,5},{12,9},{3,6},{7,10},{11,14},{6,3},{... | collective-permute-start | bytes 393224 | tf_op jit(solution)/shard_map/ppermute | solution.py:449

commit v10 on v9

--- a/solution.py
+++ b/solution.py
@@ -208,38 +208,44 @@
             packs[own, 2 * WIN:3 * WIN] = low[:ROWS]
             packs[own, 3 * WIN:] = low[ROWS:]
 
-    for part in range(group + 4):
+    def conclude(first):
+        both = dot(packs[first * ROWS:(first + piece) * ROWS, :], inverse_lanes[...])
+        scores = []
+        for part in range(piece):
+            own = slice(part * ROWS, (part + 1) * ROWS)
+            numerator = both[own, :WIN] + both[own, WIN:]
+            scores.append(numerator * (scale[first + part] * gain[first + part:first + part + 1]))
+        largest = [jnp.max(jnp.abs(score), axis=0, keepdims=True) for score in scores]
+        largest = jnp.max(jnp.concatenate(largest, axis=0), axis=1, keepdims=True)
+        power = jnp.ceil(jnp.log2(jnp.maximum(largest, 1e-30)))
+        shrink = jnp.exp2(-power).astype(bf16).astype(f32)
+        for part in range(piece):
+            window = base + first + part
+            score = scores[part]
+            size = jnp.maximum(jnp.abs(score) * shrink[part:part + 1], 1e-30)
+            root = size * lax.rsqrt(size) * CODE
+            root = jnp.minimum(root, CODE)
+            code = jnp.round(jnp.where(score < 0, -root, root)).astype(jnp.int32).astype(jnp.int16)
+            to = target[window]
+            out[to, pl.ds(pl.multiple_of(ranks[window] * ROWS, ROWS), ROWS), :] = code
+            here = lane == position[0] * capacity + ranks[window]
+            named = (slots[window] + 1).astype(f32)
+            mark = jnp.where(line == 0, named, jnp.where(line == 1, power[part:part + 1], 0.0))
+            marks[to] = marks[to] + jnp.where(here, mark, 0.0)
+
+    lag, piece = 6, min(4, group)
+    for part in range(group + 2 * lag):
         if part < group:
             chip_spectrum(part)
-        if 2 <= part < group + 2:
-            multiply(part - 2)
-            if part % 2 == 1:
-                invert((part - 2) // 2)
-        if part >= 4 and part % 2 == 1:
-            pack((part - 4) // 2)
-    both = dot(packs[...], inverse_lanes[...])
-    scores = []
-    for part in range(group):
-        own = slice(part * ROWS, (part + 1) * ROWS)
-        numerator = both[own, :WIN] + both[own, WIN:]
-        scores.append(numerator * (scale[part] * gain[part:part + 1]))
-    largest = jnp.concatenate([jnp.max(jnp.abs(score), axis=0, keepdims=True) for score in scores], axis=0)
-    largest = jnp.max(largest, axis=1, keepdims=True)
-    power = jnp.ceil(jnp.log2(jnp.maximum(largest, 1e-30)))
-    shrink = jnp.exp2(-power).astype(bf16).astype(f32)
-    for part in range(group):
-        window = base + part
-        score = scores[part]
-        size = jnp.maximum(jnp.abs(score) * shrink[part:part + 1], 1e-30)
-        root = size * lax.rsqrt(size) * CODE
-        root = jnp.minimum(root, CODE)
-        code = jnp.round(jnp.where(score < 0, -root, root)).astype(jnp.int32).astype(jnp.int16)
-        to = target[window]
-        out[to, pl.ds(pl.multiple_of(ranks[window] * ROWS, ROWS), ROWS), :] = code
-        here = lane == position[0] * capacity + ranks[window]
-        named = (slots[window] + 1).astype(f32)
-        mark = jnp.where(line == 0, named, jnp.where(line == 1, power[part:part + 1], 0.0))
-        marks[to] = marks[to] + jnp.where(here, mark, 0.0)
+        if lag <= part < group + lag:
+            multiply(part - lag)
+            if (part - lag) % 2 == 1:
+                invert((part - lag) // 2)
+        done = part - 2 * lag
+        if done >= 0 and done % 2 == 1:
+            pack(done // 2)
+            if (done + 1) % piece == 0:
+                conclude(done + 1 - piece)
 
     @pl.when(step == pl.num_programs(0) - 1)
     def _():

time: 96.9 us -> 94.8 us (0.978)
  Pallas kernels: 24.4 us -> 22.2 us
    pallas_call x1, Pallas kernels: 12.1 us -> 9.97 us  [score_windows(): pl.pallas_call(functools.partial(score_kernel, capacity), grid_spec=pltpu...]
  transfers between devices with their start and end apart: 4 -> 4, of which waited for: 2 -> 2; matrix products, arithmetic and copies ran while one was open for 3% -> 3% of each run, Pallas kernels for 10% -> 11%
where the time goes in v10:
time: 94.8 us; the launch traced here: 94.5 us
  waiting for transfers between devices  30.3 us (32%)
  blocking collectives  30.1 us (32%)
  Pallas kernels  22.2 us (23%)
  starting transfers between devices  8.2 us (9%)
  local copies, waits for them, and re-layouts  3.24 us (3%)
    all_to_all x1, blocking collectives, on_device(): lax.all_to_all(sent, 'tile', split_axis=0, concat_axis=0, tiled=True)  30.1 us
    all_to_all x1, waiting for transfers between devices, on_device(): lax.all_to_all(codes, ('tile', 'sub'), split_axis=0, concat_axis=0, tiled...  25.9 us
    pallas_call x1, Pallas kernels, score_windows(): pl.pallas_call(functools.partial(score_kernel, capacity), grid_spec=pltpu...  9.97 us
    pallas_call x1, Pallas kernels, prepare_windows(): pl.pallas_call(window_kernel, grid=(amount // group,), in_specs=[pl.Block...  9.96 us
    ppermute x1, waiting for transfers between devices, on_device(): lax.ppermute(jnp.where(sub == 0, first, last), ('tile', 'sub'), ups + downs)  4.35 us
    all_to_all x1, starting transfers between devices, on_device(): lax.all_to_all(codes, ('tile', 'sub'), split_axis=0, concat_axis=0, tiled...  3.51 us
    unnamed x23, local copies, waits for them, and re-layouts  3.24 us
    ppermute x1, starting transfers between devices, on_device(): lax.ppermute(jnp.where(sub == 0, first, last), ('tile', 'sub'), ups + downs)  1.91 us
  transfers between devices with their start and end apart: 4, of which 2 were waited for; matrix products, arithmetic and copies ran while one was open for 3% of the time, Pallas kernels for 11%

profile of v10, /device:TPU:1, one launch (start us, length us, event | category | flops | bytes accessed | tf_op | source)
XLA Modules:
  0.0 94.5 jit_solution(11844763956274371709)
XLA Ops:
  0.0 0.9 %copy-done = bf16[1,32,4096]{2,1,0:T(8,128)(2,1)S(1)} copy-done((bf16[1,32,4096]{2,1,0:T(8,128)(2,1)S(1)}, bf16[1,32,4096]{2,1,0:T(8,128)(2,1)}, u32[]{:S(2)}) %copy-start) | copy-done | bytes 262168
  1.0 0.2 spread.1
  1.1 30.1 %all_to_all.10 = bf16[4,1024,128]{2,1,0:T(8,128)(2,1)S(1)} all-to-all(bf16[4,1024,128]{2,1,0:T(8,128)(2,1)S(1)} %bitcast.18), channel_id=1, replica_groups=mesh['groups'=2,'tile'=4,'pair'=2,'sub'=2] {'tile'}, dimensions={0} | all-to-all | bytes 2097152 | tf_op jit(solution)/shard_map/all_to_all | solution.py:431
  31.3 1.8 %collective-permute-start = (bf16[128,32,128]{2,1,0:T(8,128)(2,1)S(1)}, bf16[128,32,128]{2,1,0:T(8,128)(2,1)}, u32[]{:S(2)}, u32[]{:S(2)}) collective-permute-start(bf16[128,32,128]{2,1,0:T(8,128)(2,1)S(1)} %bitcast.19), channel_id=1, source_target_pairs={{0,1},{1,0},{2,3},{3,2},{4,5},{5,4},{6,7},{7,6},{8,9},{9,8},{10,11... | collective-permute-start | bytes 3145736 | tf_op jit(solution)/shard_map/ppermute | solution.py:437
  33.0 0.0 copy-start.9
  33.0 0.0 copy-start.10
  33.0 2.2 %copy.13 = bf16[8,8,128,128]{3,2,1,0:T(8,128)(2,1)S(1)} copy(bf16[8,8,128,128]{3,1,2,0:T(8,128)(2,1)} %bitcast.26) | data formatting | bytes 4194304
  35.3 0.0 copy-done.6
  35.3 0.2 convert_reduce_fusion.ranks
  35.6 0.0 copy-start.1
  35.6 0.0 copy-start.2
  35.6 0.0 copy-start.3
  35.6 0.0 copy-start.4
  35.6 10.0 %window_spectra.1 = (f32[64,128,128]{2,1,0:T(8,128)}, f32[64,32,128]{2,1,0:T(8,128)}) custom-call(bf16[64,128,128]{2,1,0:T(8,128)(2,1)S(1)} %bitcast.21, bf16[320,128]{1,0:T(8,128)(2,1)S(1)} %copy-done.8, bf16[64,256]{1,0:T(8,128)(2,1)S(1)} %copy-done.10, bf16[256,256]{1,0:T(8,128)(2,1)S(1)} %copy-done.7, bf16[256,128]{1,0:T(8,128)(2,1)S(1)} %copy-done.9), custom_call_target="tpu_custom_call" | custom-call | flops 7549747200 | bytes 7680000 | tf_op jit(solution)/shard_map/window_spectra/pallas_call | solution.py:326
  45.6 0.0 collective-permute-done.rest_1_
  45.6 10.0 %scores.1 = s16[8,520,128]{2,1,0:T(8,128)(2,1)} custom-call(s32[64]{0:T(128)S(1)} %get-tuple-element.18.choice, s32[64]{0:T(128)S(1)} %get-tuple-element.17.place, s32[64]{0:T(128)S(1)} %bitcast.25, s32[64]{0:T(128)S(1)} %convert_reduce_fusion.ranks, s32[64]{0:T(128)S(1)} %bitcast.23, s32[1]{0:T(128)} %bitcast.3.position, ...), custom_call_target="tpu_custom_call" | custom-call | tf_op jit(solution)/shard_map/scores/pallas_call | solution.py:351
  55.6 3.5 %all-to-all-start.1 = ((s16[8,520,128]{2,1,0:T(8,128)(2,1)}), s16[8,520,128]{2,1,0:T(8,128)(2,1)S(1)}, u32[]{:S(2)}, u32[]{:S(2)}) async-start(s16[8,520,128]{2,1,0:T(8,128)(2,1)} %scores.1), calls=%async_computation.1 | async-start | bytes 2129920 | tf_op jit(solution)/shard_map/all_to_all | solution.py:449
  59.1 25.9 %all-to-all-done.1.codes = s16[8,520,128]{2,1,0:T(8,128)(2,1)S(1)} async-done(((s16[8,520,128]{2,1,0:T(8,128)(2,1)}), s16[8,520,128]{2,1,0:T(8,128)(2,1)S(1)}, u32[]{:S(2)}, u32[]{:S(2)}) %all-to-all-start.1) | async-done | bytes 1064992 | tf_op jit(solution)/shard_map/all_to_all | solution.py:449
  85.0 1.3 %average.1 = (f32[32,4096]{1,0:T(8,128)S(1)}, f32[8,4096]{1,0:T(8,128)S(1)}, f32[8,4096]{1,0:T(8,128)S(1)}) custom-call(s16[8,520,128]{2,1,0:T(8,128)(2,1)S(1)} %all-to-all-done.1.codes), custom_call_target="tpu_custom_call" | custom-call | tf_op jit(solution)/shard_map/average/pallas_call | solution.py:379
  86.4 1.0 %collective-permute-start.1 = (f32[8,4096]{1,0:T(8,128)S(1)}, f32[8,4096]{1,0:T(8,128)S(1)}, u32[]{:S(2)}, u32[]{:S(2)}) collective-permute-start(f32[8,4096]{1,0:T(8,128)S(1)} %get-tuple-element.16), channel_id=1, source_target_pairs={{0,1},{1,0},{2,3},{3,2},{4,5},{5,4},{6,7},{7,6},{8,9},{9,8},{10,11... | collective-permute-start | bytes 393224 | tf_op jit(solution)/shard_map/ppermute | solution.py:452
  87.4 1.9 %collective-permute-start.2 = (f32[8,4096]{1,0:T(8,128)S(1)}, f32[8,4096]{1,0:T(8,128)S(1)}, u32[]{:S(2)}, u32[]{:S(2)}) collective-permute-start(f32[8,4096]{1,0:T(8,128)S(1)} %get-tuple-element.15), channel_id=1, source_target_pairs={{1,4},{5,8},{9,12},{4,1},{8,5},{12,9},{3,6},{7,10},{11,14},{6,3},{... | collective-permute-start | bytes 393224 | tf_op jit(solution)/shard_map/ppermute | solution.py:455
  89.3 0.0 collective-permute-done.1.inner
  89.3 4.3 %collective-permute-done.2.outer = f32[8,4096]{1,0:T(8,128)S(1)} collective-permute-done((f32[8,4096]{1,0:T(8,128)S(1)}, f32[8,4096]{1,0:T(8,128)S(1)}, u32[]{:S(2)}, u32[]{:S(2)}) %collective-permute-start.2) | collective-permute-done | bytes 131104 | tf_op jit(solution)/shard_map/ppermute | solution.py:455
  93.7 0.8 finish.1
  (16 shorter events, 0.1 us)
Async XLA Ops:
  0.0 0.9 %copy-start = (bf16[1,32,4096]{2,1,0:T(8,128)(2,1)S(1)}, bf16[1,32,4096]{2,1,0:T(8,128)(2,1)}, u32[]{:S(2)}) copy-start(bf16[1,32,4096]{2,1,0:T(8,128)(2,1)} %param.12) | copy-start | bytes 786436
  31.3 14.3 %collective-permute-start = (bf16[128,32,128]{2,1,0:T(8,128)(2,1)S(1)}, bf16[128,32,128]{2,1,0:T(8,128)(2,1)}, u32[]{:S(2)}, u32[]{:S(2)}) collective-permute-start(bf16[128,32,128]{2,1,0:T(8,128)(2,1)S(1)} %bitcast.19), channel_id=1, source_target_pairs={{0,1},{1,0},{2,3},{3,2},{4,5},{5,4},{6,7},{7,6},{8,9},{9,8},{10,11... | collective-permute-start | bytes 3145736 | tf_op jit(solution)/shard_map/ppermute | solution.py:437
  33.0 2.3 %copy-start.6 = (s32[1,64,1]{1,2,0:T(1,128)S(1)}, s32[1,64,1]{1,2,0:T(1,128)}, u32[]{:S(2)}) copy-start(s32[1,64,1]{1,2,0:T(1,128)} %param.14) | copy-start | bytes 772
  33.0 2.5 %copy-start.5 = (s32[1,64]{1,0:T(1,128)S(1)}, s32[1,64]{1,0:T(1,128)}, u32[]{:S(2)}) copy-start(s32[1,64]{1,0:T(1,128)} %param.15) | copy-start | bytes 772
  33.0 2.5 %copy-start.7 = (bf16[256,256]{1,0:T(8,128)(2,1)S(1)}, bf16[256,256]{1,0:T(8,128)(2,1)}, u32[]{:S(2)}) copy-start(bf16[256,256]{1,0:T(8,128)(2,1)} %constant.61.clone.window_lanes) | copy-start | bytes 393220
  33.0 2.5 %copy-start.8 = (bf16[320,128]{1,0:T(8,128)(2,1)S(1)}, bf16[320,128]{1,0:T(8,128)(2,1)}, u32[]{:S(2)}) copy-start(bf16[320,128]{1,0:T(8,128)(2,1)} %constant.59.clone.window_rows) | copy-start | bytes 245764
  33.0 2.5 %copy-start.9 = (bf16[256,128]{1,0:T(8,128)(2,1)S(1)}, bf16[256,128]{1,0:T(8,128)(2,1)}, u32[]{:S(2)}) copy-start(bf16[256,128]{1,0:T(8,128)(2,1)} %constant.62.clone.band_lanes) | copy-start | bytes 196612
  33.0 2.5 %copy-start.10 = (bf16[64,256]{1,0:T(8,128)(2,1)S(1)}, bf16[64,256]{1,0:T(8,128)(2,1)}, u32[]{:S(2)}) copy-start(bf16[64,256]{1,0:T(8,128)(2,1)} %constant.60.clone.square_rows) | copy-start | bytes 98308
  35.6 10.0 %copy-start.1 = (bf16[256,512]{1,0:T(8,128)(2,1)S(1)}, bf16[256,512]{1,0:T(8,128)(2,1)}, u32[]{:S(2)}) copy-start(bf16[256,512]{1,0:T(8,128)(2,1)} %constant.63.clone.chip_lanes) | copy-start | bytes 786436
  35.6 10.0 %copy-start.2 = (bf16[512,256]{1,0:T(8,128)(2,1)S(1)}, bf16[512,256]{1,0:T(8,128)(2,1)}, u32[]{:S(2)}) copy-start(bf16[512,256]{1,0:T(8,128)(2,1)} %constant.66.clone.inverse_lanes) | copy-start | bytes 786436
  35.6 10.0 %copy-start.3 = (bf16[128,192]{1,0:T(8,128)(2,1)S(1)}, bf16[128,192]{1,0:T(8,128)(2,1)}, u32[]{:S(2)}) copy-start(bf16[128,192]{1,0:T(8,128)(2,1)} %constant.64.clone.chip_rows) | copy-start | bytes 147460
  35.6 10.0 %copy-start.4 = (bf16[128,256]{1,0:T(8,128)(2,1)S(1)}, bf16[128,256]{1,0:T(8,128)(2,1)}, u32[]{:S(2)}) copy-start(bf16[128,256]{1,0:T(8,128)(2,1)} %constant.65.clone.inverse_rows) | copy-start | bytes 196612
  55.6 29.5 %all-to-all-start.1 = ((s16[8,520,128]{2,1,0:T(8,128)(2,1)}), s16[8,520,128]{2,1,0:T(8,128)(2,1)S(1)}, u32[]{:S(2)}, u32[]{:S(2)}) async-start(s16[8,520,128]{2,1,0:T(8,128)(2,1)} %scores.1), calls=%async_computation.1 | async-start | bytes 2129920 | tf_op jit(solution)/shard_map/all_to_all | solution.py:449
  86.4 3.0 %collective-permute-start.1 = (f32[8,4096]{1,0:T(8,128)S(1)}, f32[8,4096]{1,0:T(8,128)S(1)}, u32[]{:S(2)}, u32[]{:S(2)}) collective-permute-start(f32[8,4096]{1,0:T(8,128)S(1)} %get-tuple-element.16), channel_id=1, source_target_pairs={{0,1},{1,0},{2,3},{3,2},{4,5},{5,4},{6,7},{7,6},{8,9},{9,8},{10,11... | collective-permute-start | bytes 393224 | tf_op jit(solution)/shard_map/ppermute | solution.py:452
  87.4 6.3 %collective-permute-start.2 = (f32[8,4096]{1,0:T(8,128)S(1)}, f32[8,4096]{1,0:T(8,128)S(1)}, u32[]{:S(2)}, u32[]{:S(2)}) collective-permute-start(f32[8,4096]{1,0:T(8,128)S(1)} %get-tuple-element.15), channel_id=1, source_target_pairs={{1,4},{5,8},{9,12},{4,1},{8,5},{12,9},{3,6},{7,10},{11,14},{6,3},{... | collective-permute-start | bytes 393224 | tf_op jit(solution)/shard_map/ppermute | solution.py:455
